TPU v7x, 32 devices: a whole 2x2x4 slice. The times are simulated.
32 devices in a mesh: dp: 8 (over z, x), tensor: 4 (over y, core).
Axes of the slice: x: 2, y: 2, z: 4, core: 2. Of those that a mesh axis runs over, the one named last changes fastest.
Arguments:
- token_ids: int32 [48, 512], P('dp'), may hold values from 0 to 50431
- lengths: int32 [48], P('dp'), may hold values from 128 to 512, as said below
- partners: int32 [48], replicated, may hold values from 0 to 47, as said below
- embedding: float32 [50432, 1024], P('dp', 'tensor'), may hold values from -0.18 to 0.18
- positions: float32 [514, 1024], P(None, 'tensor'), may hold values from -0.18 to 0.18
- attn_weights: float32 [4, 1024, 1024], P(None, None, 'tensor')
- ffn_weights: float32 [2, 1024, 4096], P(None, None, 'tensor')
- bias_qv: float32 [2, 1024], P(None, 'tensor'), may hold values from -1.8 to 1.8
- bias_up: float32 [4096], P('tensor'), may hold values from -1.8 to 1.8
- norms: float32 [8, 1024], replicated
- head_first: float32 [1024, 256], replicated, may hold values from -0.1875 to 0.1875
- head_second: float32 [256, 64], replicated, may hold values from -0.375 to 0.375
- head_bias: float32 [256], replicated, may hold values from -1.8 to 1.8
- mom_embedding: float32 [50432, 1024], P('dp', 'tensor'), may hold values from -5.9604645e-07 to 5.9604645e-07
- mom_positions: float32 [514, 1024], P(None, 'tensor'), may hold values from -5.9604645e-07 to 5.9604645e-07
- mom_attn: float32 [4, 1024, 1024], P(None, None, 'tensor'), may hold values from -5.9604645e-07 to 5.9604645e-07
- ffn_momentum: float32 [2, 1024, 4096], P(None, None, 'tensor'), may hold values from -5.9604645e-07 to 5.9604645e-07
- mom_bias_qv: float32 [2, 1024], P(None, 'tensor'), may hold values from -2.861023e-06 to 2.861023e-06
- mom_bias_up: float32 [4096], P('tensor'), may hold values from -2.861023e-06 to 2.861023e-06
- mom_norms: float32 [8, 1024], replicated, may hold values from -2.861023e-06 to 2.861023e-06
- mom_head_first: float32 [1024, 256], replicated, may hold values from -5.9604645e-07 to 5.9604645e-07
- mom_head_second: float32 [256, 64], replicated, may hold values from -5.9604645e-07 to 5.9604645e-07
- mom_head_bias: float32 [256], replicated, may hold values from -2.861023e-06 to 2.861023e-06
Outputs:
- new_embedding: float32 [50432, 1024], P('dp', 'tensor')
- new_positions: float32 [514, 1024], P(None, 'tensor')
- new_attn: float32 [4, 1024, 1024], P(None, None, 'tensor')
- new_ffn: float32 [2, 1024, 4096], P(None, None, 'tensor')
- new_bias_qv: float32 [2, 1024], P(None, 'tensor')
- new_bias_up: float32 [4096], P('tensor')
- new_norms: float32 [8, 1024], replicated
- new_head_first: float32 [1024, 256], replicated
- new_head_second: float32 [256, 64], replicated
- new_head_bias: float32 [256], replicated
- next_embedding: float32 [50432, 1024], P('dp', 'tensor')
- next_positions: float32 [514, 1024], P(None, 'tensor')
- next_attn: float32 [4, 1024, 1024], P(None, None, 'tensor')
- next_ffn: float32 [2, 1024, 4096], P(None, None, 'tensor')
- next_bias_qv: float32 [2, 1024], P(None, 'tensor')
- next_bias_up: float32 [4096], P('tensor')
- next_norms: float32 [8, 1024], replicated
- next_head_first: float32 [1024, 256], replicated
- next_head_second: float32 [256, 64], replicated
- next_head_bias: float32 [256], replicated
- loss: float32 [], replicated
- grad_norm: float32 [], replicated
Inputs may be any that keep to these rules, and one draw needn't show every extreme that they name: `lengths`: every length is at least 128, and some sequence has exactly 512. partners pair the sequences: partners[partners[i]] = i and partners[i] != i.
All inputs are finite; a program needn't handle non-finite values.
Results may differ from a plain program's by a relative error of at most 0.0003.
Values sent between devices are 32-bit elements; how exact they have to be, the bound alone decides.
A program may use at most 384 MiB of HBM per device.

v0:
```python
import math

import jax
import jax.numpy as jnp
from jax import lax
from jax.sharding import PartitionSpec as P

HEAD_DIM = 64
PARAMS = 65044736


EPS = 1e-05
SOFTMAX_TEMP = 0.1
DECAY = 0.9
RATE = 100000.0
CLIP_SCALE = 1e-06
HIGH = lax.Precision.HIGHEST


def precise_product(left, right):
    return jnp.matmul(left, right, precision=HIGH)


def norm_rows(values, gain, shift):
    center = values - jnp.mean(values, axis=-1, keepdims=True)
    spread = jnp.mean(center * center, axis=-1, keepdims=True)
    return center * lax.rsqrt(spread + EPS) * gain + shift


def attend(normed, lengths, attn, bias_qv):
    seqs, slots, width = normed.shape
    cols = attn.shape[2]
    heads = cols // HEAD_DIM
    queries = (precise_product(normed, attn[0]) + bias_qv[0]).reshape(seqs, slots, heads, HEAD_DIM)
    keys_all = precise_product(normed, attn[1]).reshape(seqs, slots, heads, HEAD_DIM)
    values = (precise_product(normed, attn[2]) + bias_qv[1]).reshape(seqs, slots, heads, HEAD_DIM)
    scores = jnp.einsum("sqhd,skhd->shqk", queries, keys_all, precision=HIGH) / math.sqrt(HEAD_DIM)
    valid = lax.broadcasted_iota(jnp.int32, (seqs, slots), 1) < lengths[:, None]
    scores = jnp.where(valid[:, None, None, :], scores, -1e30)
    probs = jax.nn.softmax(scores, axis=-1)
    mixed = jnp.einsum("shqk,skhd->sqhd", probs, values, precision=HIGH).reshape(seqs, slots, cols)
    return precise_product(mixed, attn[3].T)


def expand(normed, ffn, bias_up):
    hidden = jax.nn.gelu(precise_product(normed, ffn[0]) + bias_up, approximate=False)
    return precise_product(hidden, ffn[1].T)


def contrast(pooled, head_first, head_second, head_bias, partners):
    middle = jax.nn.gelu(precise_product(pooled, head_first) + head_bias, approximate=False)
    output = precise_product(middle, head_second)
    unit_vectors = output * lax.rsqrt(jnp.sum(output * output, axis=-1, keepdims=True) + 1e-06)
    similarity_scores = precise_product(unit_vectors, unit_vectors.T) / SOFTMAX_TEMP
    count = similarity_scores.shape[0]
    index = lax.broadcasted_iota(jnp.int32, (count,), 0)
    similarity_scores = jnp.where(index[:, None] == index[None, :], -1e30, similarity_scores)
    totals = jax.nn.logsumexp(similarity_scores, axis=-1)
    paired_rows = jnp.sum(
        jnp.where(index[None, :] == partners[:, None], similarity_scores, 0.0), axis=-1
    )
    return jnp.sum(totals - paired_rows)


def owner_rows(ids_part, base, vocab_rows):
    local_ids = ids_part - base
    inside = (local_ids >= 0) & (local_ids < vocab_rows)
    return jnp.where(inside, local_ids, vocab_rows)


def advance(weight, moment, grad, factor):
    clipped = factor * grad
    moment_new = DECAY * moment + (1.0 - DECAY) * clipped
    return (weight - RATE * (DECAY * moment_new + (1.0 - DECAY) * clipped), moment_new)


def squares(array):
    return jnp.sum(array * array)


def on_device(
    token_ids,
    lengths,
    partners,
    embedding,
    positions,
    attn_weights,
    ffn_weights,
    bias_qv,
    bias_up,
    norms,
    head_first,
    head_second,
    head_bias,
    mom_embedding,
    mom_positions,
    mom_attn,
    ffn_momentum,
    mom_bias_qv,
    mom_bias_up,
    mom_norms,
    mom_head_first,
    mom_head_second,
    mom_head_bias,
):
    seqs, slots = token_ids.shape
    vocab_rows, cols = embedding.shape
    dp_rank = lax.axis_index("dp")
    tp_rank = lax.axis_index("tensor")
    base = dp_rank * vocab_rows
    all_ids = lax.all_gather(token_ids, "dp", axis=0, tiled=True).reshape(-1)
    padded_table = jnp.concatenate([embedding, jnp.zeros((1, cols), jnp.float32)], axis=0)
    rows_ids = owner_rows(all_ids, base, vocab_rows)
    token_rows = lax.psum_scatter(
        jnp.take(padded_table, rows_ids, axis=0), "dp", scatter_dimension=0, tiled=True
    )
    token_cols = token_rows.reshape(seqs, slots, cols) + positions[2 : slots + 2][None]
    embedded = lax.all_gather(token_cols, "tensor", axis=2, tiled=True)
    h_zero, ln_zero_pull = jax.vjp(norm_rows, embedded, norms[0], norms[1])
    attn_part, attn_pull = jax.vjp(
        lambda normed, weights, biases: attend(normed, lengths, weights, biases),
        h_zero,
        attn_weights,
        bias_qv,
    )
    x_one = h_zero + lax.psum(attn_part, "tensor") + norms[6]
    h_one, ln_one_pull = jax.vjp(norm_rows, x_one, norms[2], norms[3])
    ffn_part, ffn_pull = jax.vjp(expand, h_one, ffn_weights, bias_up)
    x_two = h_one + lax.psum(ffn_part, "tensor") + norms[7]
    h_two, ln_two_pull = jax.vjp(norm_rows, x_two, norms[4], norms[5])
    valid = (lax.broadcasted_iota(jnp.int32, (seqs, slots), 1) < lengths[:, None]).astype(
        jnp.float32
    )
    len_float = lengths.astype(jnp.float32)
    pooled = jnp.sum(h_two * valid[:, :, None], axis=1) / len_float[:, None]
    all_pooled = lax.all_gather(pooled, "dp", axis=0, tiled=True)
    loss, head_pull = jax.vjp(
        lambda rows, first_w, second_w, bias_w: contrast(rows, first_w, second_w, bias_w, partners),
        all_pooled,
        head_first,
        head_second,
        head_bias,
    )
    back_pooled_all, grad_head_first, grad_head_second, grad_head_bias = head_pull(
        jnp.ones_like(loss)
    )
    back_pooled = lax.dynamic_slice_in_dim(back_pooled_all, dp_rank * seqs, seqs)
    back_h_two = valid[:, :, None] * (back_pooled / len_float[:, None])[:, None, :]
    back_x_two, grad_gain_two, grad_shift_two = ln_two_pull(back_h_two)
    back_h_one_part, grad_ffn, grad_bias_up = ffn_pull(back_x_two)
    back_h_one = back_x_two + lax.psum(back_h_one_part, "tensor")
    back_x_one, grad_gain_one, grad_shift_one = ln_one_pull(back_h_one)
    back_h_zero_part, grad_attn, grad_bias_qv = attn_pull(back_x_one)
    back_h_zero = back_x_one + lax.psum(back_h_zero_part, "tensor")
    back_embedded, grad_gain_zero, grad_shift_zero = ln_zero_pull(back_h_zero)
    back_cols = lax.dynamic_slice_in_dim(back_embedded, tp_rank * cols, cols, 2)
    grad_positions = jnp.pad(
        jnp.sum(back_cols, axis=0), ((2, positions.shape[0] - slots - 2), (0, 0))
    )
    grad_norms = jnp.stack(
        [
            grad_gain_zero,
            grad_shift_zero,
            grad_gain_one,
            grad_shift_one,
            grad_gain_two,
            grad_shift_two,
            jnp.sum(back_x_one, axis=(0, 1)),
            jnp.sum(back_x_two, axis=(0, 1)),
        ]
    )
    back_flat = back_cols.reshape(seqs * slots, cols)
    target = owner_rows(all_ids, base, vocab_rows)
    grad_embedding = jax.ops.segment_sum(
        lax.all_gather(back_flat, "dp", axis=0, tiled=True), target, num_segments=vocab_rows + 1
    )[:vocab_rows]
    first_dp = (dp_rank == 0).astype(jnp.float32)
    first_all = first_dp * (tp_rank == 0).astype(jnp.float32)
    grad_attn, grad_ffn, grad_positions, grad_bias_qv, grad_bias_up, grad_norms = lax.psum(
        (grad_attn, grad_ffn, grad_positions, grad_bias_qv, grad_bias_up, grad_norms), "dp"
    )
    big_squares = first_dp * (squares(grad_attn) + squares(grad_ffn))
    local_squares = (
        big_squares
        + squares(grad_embedding)
        + first_dp * (squares(grad_positions) + squares(grad_bias_qv) + squares(grad_bias_up))
        + first_all
        * (
            squares(grad_norms)
            + squares(grad_head_first)
            + squares(grad_head_second)
            + squares(grad_head_bias)
        )
    )
    total_squares = lax.psum(local_squares, ("dp", "tensor"))
    grad_norm = jnp.sqrt(total_squares)
    factor = jnp.minimum(1.0, CLIP_SCALE * math.sqrt(PARAMS) / (grad_norm + 1e-06))
    new_attn, next_attn = advance(attn_weights, mom_attn, grad_attn, factor)
    new_ffn, next_ffn = advance(ffn_weights, ffn_momentum, grad_ffn, factor)
    new_embedding, next_embedding = advance(embedding, mom_embedding, grad_embedding, factor)
    new_positions, next_positions = advance(positions, mom_positions, grad_positions, factor)
    new_bias_qv, next_bias_qv = advance(bias_qv, mom_bias_qv, grad_bias_qv, factor)
    new_bias_up, next_bias_up = advance(bias_up, mom_bias_up, grad_bias_up, factor)
    new_norms, next_norms = advance(norms, mom_norms, grad_norms, factor)
    new_head_first, next_head_first = advance(head_first, mom_head_first, grad_head_first, factor)
    new_head_second, next_head_second = advance(
        head_second, mom_head_second, grad_head_second, factor
    )
    new_head_bias, next_head_bias = advance(head_bias, mom_head_bias, grad_head_bias, factor)
    return (
        new_embedding,
        new_positions,
        new_attn,
        new_ffn,
        new_bias_qv,
        new_bias_up,
        new_norms,
        new_head_first,
        new_head_second,
        new_head_bias,
        next_embedding,
        next_positions,
        next_attn,
        next_ffn,
        next_bias_qv,
        next_bias_up,
        next_norms,
        next_head_first,
        next_head_second,
        next_head_bias,
        loss,
        grad_norm,
    )


def solution(mesh):
    in_specs = (
        P("dp", None),
        P("dp"),
        P(),
        P("dp", "tensor"),
        P(None, "tensor"),
        P(None, None, "tensor"),
        P(None, None, "tensor"),
        P(None, "tensor"),
        P("tensor"),
        P(),
        P(),
        P(),
        P(),
        P("dp", "tensor"),
        P(None, "tensor"),
        P(None, None, "tensor"),
        P(None, None, "tensor"),
        P(None, "tensor"),
        P("tensor"),
        P(),
        P(),
        P(),
        P(),
    )
    out_specs = (
        P("dp", "tensor"),
        P(None, "tensor"),
        P(None, None, "tensor"),
        P(None, None, "tensor"),
        P(None, "tensor"),
        P("tensor"),
        P(),
        P(),
        P(),
        P(),
        P("dp", "tensor"),
        P(None, "tensor"),
        P(None, None, "tensor"),
        P(None, None, "tensor"),
        P(None, "tensor"),
        P("tensor"),
        P(),
        P(),
        P(),
        P(),
        P(),
        P(),
    )
    return jax.shard_map(
        on_device, mesh=mesh, in_specs=in_specs, out_specs=out_specs, check_vma=False
    )
```

profile of v0, /device:TPU:0, one launch (start us, length us, event | category | flops | bytes accessed | tf_op | source)
XLA Modules:
  0.0 3406.0 jit_solution(14313139311768946980)
XLA Ops:
  7.2 32.5 all-gather
  46.9 95.1 %gather_fusion = f32[24576,256]{1,0:T(8,128)} fusion(f32[6305,256]{1,0:T(8,128)} %concatenate.3, s32[24576]{0:T(1024)S(1)} %broadcast_clamp_fusion), kind=kCustom, calls=%fused_computation | custom fusion | bytes 50429952 | tf_op jit(solution)/shard_map/jit(_take)/gather | solution.py:115
  160.6 403.7 %reduce-scatter.2.cloned.1.call-done = f32[3072,256]{1,0:T(8,128)} async-done(((f32[24576,256]{1,0:T(8,128)}), f32[3072,256]{1,0:T(8,128)}) %reduce-scatter.2.cloned.1.call-update) | async-done | bytes 3145744 | tf_op jit(solution)/shard_map/reduce_scatter | solution.py:114
  572.7 77.0 %all-gather.5.cloned.1.call-done = f32[6,512,1024]{2,1,0:T(8,128)} async-done(((f32[6,512,256]{2,1,0:T(8,128)}), f32[6,512,1024]{2,1,0:T(8,128)}) %all-gather.5.cloned.1.call-update) | async-done | bytes 12582928 | tf_op jit(solution)/shard_map/all_gather | solution.py:118
  692.4 25.3 fusion
  743.4 26.6 fusion.23
  769.9 23.5 fusion.73
  793.5 220.8 %all-reduce.18.cloned.1.call-done = f32[6,512,1024]{2,1,0:T(8,128)} async-done(((f32[6,512,1024]{2,1,0:T(8,128)}), f32[6,512,1024]{2,1,0:T(8,128)}) %all-reduce.18.cloned.1.call-update) | async-done | bytes 12582928 | tf_op jit(solution)/shard_map/psum | solution.py:126
  1026.9 50.6 %fusion.56 = (u8[512,1024]{1,0:T(8,128)(4,1)S(1)}, u8[512,1024]{1,0:T(8,128)(4,1)}, f32[6,512,1024]{2,1,0:T(8,128)S(1)}) fusion(f32[1024]{0:T(1024)} %param.31, f32[2,1024,1024]{2,1,0:T(8,128)} %param.29, f32[6,512,1024]{2,1,0:T(8,128)S(1)} %get-tuple-element.72, f32[1024]{0:T(1024)} %bitcast.215, f32[1024]{0:T(1024)} %bitcast.203, ...), kind=kOutput, calls=%fused_computation.117 | convolution fusion | flops 38710280192 | bytes 30445568 | tf_op jit(solution)/shard_map/jvp()/dot_general | solution.py:21
  1077.6 28.5 fusion.4
  1110.5 44.9 %fusion.41 = f32[6,512,1024]{2,1,0:T(8,128)} fusion(f32[6,512,1024]{2,1,0:T(8,128)S(1)} %fusion.4, f32[6,512,1024]{2,1,0:T(8,128)S(1)} %get-tuple-element.98, f32[1024]{0:T(1024)} %param.31, f32[2,1024,1024]{2,1,0:T(8,128)} %param.29), kind=kOutput, calls=%fused_computation.94 | convolution fusion | flops 38664142848 | bytes 41947136 | tf_op jit(solution)/shard_map/jvp()/dot_general | solution.py:21
  1156.0 220.4 %all-reduce.20.cloned.1.call-done = f32[6,512,1024]{2,1,0:T(8,128)} async-done(((f32[6,512,1024]{2,1,0:T(8,128)}), f32[6,512,1024]{2,1,0:T(8,128)}) %all-reduce.20.cloned.1.call-update) | async-done | bytes 12582928 | tf_op jit(solution)/shard_map/psum | solution.py:129
  1391.2 30.9 all-gather.1
  1437.9 52.7 %fusion.127 = (f32[1024]{0:T(1024)}, f32[6,512,1024]{2,1,0:T(8,128)}) fusion(f32[6,512,1024]{2,1,0:T(8,128)} %copy-done.11, f32[2,1024,1024]{2,1,0:T(8,128)S(1)} %bitcast.176, f32[6,512]{1,0:T(8,128)S(1)} %negate_multiply_fusion.4, f32[6,512]{1,0:T(8,128)S(1)} %multiply_multiply_fusion.29, f32[6,512,1024]{2,1,0:T(8,128)S(1)} %copy-done.1, ...), kind=kOutput, calls=%fused_computation.271 | convolution fusion | flops 38727057408 | bytes 54652928 | tf_op jit(solution)/shard_map/transpose(jvp())/dot_general | solution.py:21
  1490.6 44.8 %fusion.43 = f32[6,512,1024]{2,1,0:T(8,128)} fusion(f32[6,512,1024]{2,1,0:T(8,128)} %get-tuple-element.114, f32[2,1024,1024]{2,1,0:T(8,128)S(1)} %bitcast.176), kind=kOutput, calls=%fused_computation.96 | convolution fusion | flops 38654705664 | bytes 29360128 | tf_op jit(solution)/shard_map/transpose(jvp())/dot_general | solution.py:21
  1536.9 51.3 %fusion.58 = f32[1,1024,1024]{2,1,0:T(8,128)} fusion(f32[6,512,1024]{2,1,0:T(8,128)} %copy-done.11, f32[6,512,1024]{2,1,0:T(8,128)} %copy-done.10, f32[1024]{0:T(1024)S(1)} %copy-done.74, f32[6,512]{1,0:T(8,128)S(1)} %negate_multiply_fusion.4, f32[6,512,1024]{2,1,0:T(8,128)} %copy-done, f32[6,512]{1,0:T(8,128)S(1)} %multiply_multiply_fusion.29, ...), kind=kOutput, calls=%fused_computation.119 | convolution fusion | flops 38689308672 | bytes 42037248 | tf_op jit(solution)/shard_map/transpose(jvp())/dot_general | solution.py:21
  1588.2 167.9 %all-reduce.22.cloned.1.call-done = f32[6,512,1024]{2,1,0:T(8,128)} async-done(((f32[6,512,1024]{2,1,0:T(8,128)}), f32[6,512,1024]{2,1,0:T(8,128)}) %all-reduce.22.cloned.1.call-update) | async-done | bytes 12582928 | tf_op jit(solution)/shard_map/psum | solution.py:151
  1797.3 33.0 bitcast_reduce_fusion.1
  1830.2 31.4 multiply_reduce_fusion
  1861.6 25.6 select_multiply_fusion
  1887.2 27.5 fusion.130
  1936.6 23.4 fusion.68
  1960.0 22.5 fusion.71
  1982.5 25.9 add_add_fusion.3
  2009.1 47.5 %fusion.57 = f32[1,1024,1024]{2,1,0:T(8,128)} fusion(f32[6,512,1024]{2,1,0:T(8,128)} %get-tuple-element.114, f32[6,512,1024]{2,1,0:T(8,128)} %copy-done.4, f32[1024]{0:T(1024)S(1)} %bitcast.217, f32[1024]{0:T(1024)S(1)} %bitcast.207, f32[6,512]{1,0:T(8,128)S(1)} %copy-done.45, f32[6,512]{1,0:T(8,128)S(1)} %copy-done.40), kind=kOutput, calls=%fused_computation.118 | convolution fusion | flops 38667288576 | bytes 29392896 | tf_op jit(solution)/shard_map/transpose(jvp())/dot_general | solution.py:21
  2064.7 24.5 fusion.61
  2155.8 73.7 %all-reduce.24.cloned.1.call-done = f32[6,512,1024]{2,1,0:T(8,128)} async-done(((f32[6,512,1024]{2,1,0:T(8,128)}), f32[6,512,1024]{2,1,0:T(8,128)}) %all-reduce.24.cloned.1.call-update) | async-done | bytes 12582928 | tf_op jit(solution)/shard_map/psum | solution.py:154
  2265.1 39.9 %all-reduce.10 = (f32[2,256]{1,0:T(2,128)S(1)}, f32[1024]{0:T(1024)S(1)}, f32[8,1024]{1,0:T(8,128)S(1)}) all-reduce(f32[2,256]{1,0:T(2,128)S(1)} %pad_add_fusion.2, f32[1024]{0:T(1024)S(1)} %copy-done.81, f32[8,1024]{1,0:T(8,128)S(1)} %stack.35), channel_id=1, replica_groups=mesh['dp'=8,'tensor'=4] {'dp'}, use_global_device_ids=true, to_apply=%region_36.37 | all-reduce | flops 9728 | bytes 77824 | tf_op jit(solution)/shard_map/psum | solution.py:179
  2309.4 363.9 %all-reduce.26.cloned.1.call-done = (f32[4,1024,256]{2,1,0:T(8,128)}, f32[2,1024,1024]{2,1,0:T(8,128)}, f32[514,256]{1,0:T(8,128)}) async-done(((f32[4,1024,256]{2,1,0:T(8,128)}, f32[2,1024,1024]{2,1,0:T(8,128)}, f32[514,256]{1,0:T(8,128)}), (f32[4,1024,256]{2,1,0:T(8,128)}, f32[2,1024,1024]{2,1,0:T(8,128)}, f32[514,256]{1,0:T(8,128)})) %all-reduce.26.cloned.1.call-update) | async-done | bytes 13109264 | tf_op jit(solution)/shard_map/psum | solution.py:179
  2689.1 465.7 %all-gather.7.cloned.1.call-done = f32[24576,256]{1,0:T(8,128)} async-done(((f32[3072,256]{1,0:T(8,128)}), f32[24576,256]{1,0:T(8,128)}) %all-gather.7.cloned.1.call-update) | async-done | bytes 25165840 | tf_op jit(solution)/shard_map/all_gather | solution.py:175
  3154.8 151.0 %scatter_custom_fusion = f32[6305,256]{1,0:T(8,128)} fusion(s32[24576]{0:T(1024)} %bitcast.193, f32[24576,256]{1,0:T(8,128)} %all-gather.7.cloned.1.call-done, f32[]{:T(128)} %constant.62.clone.1), kind=kCustom, calls=%fused_computation.108 | custom fusion | flops 6291456 | bytes 6456832 | tf_op jit(solution)/shard_map/scatter-add | solution.py:174
  3311.7 45.6 %psum.87 = f32[]{:T(128)} all-reduce(f32[]{:T(128)S(6)} %add.365), channel_id=1, replica_groups=mesh['dp'=8,'tensor'=4] {'dp','tensor'}, use_global_device_ids=true, to_apply=%region_55.56 | all-reduce | flops 1 | bytes 8 | tf_op jit(solution)/shard_map/psum | solution.py:195
  (315 shorter events, 384.0 us)
Async XLA Ops:
  7.2 557.2 %reduce-scatter.2.cloned.1.call-start = ((), (), s32[]{:S(2)}) async-start(), calls=%async_computation.1 | async-start | bytes 28311552 | tf_op jit(solution)/shard_map/reduce_scatter | solution.py:114
  159.6 411.8 %copy-start.76 = (f32[2,256]{1,0:T(2,128)S(1)}, f32[2,256]{1,0:T(2,128)}, u32[]{:S(2)}) copy-start(f32[2,256]{1,0:T(2,128)} %param.30) | copy-start | bytes 6148
  159.6 411.8 %copy-start.90 = (s32[6]{0:T(128)S(1)}, s32[6]{0:T(128)}, u32[]{:S(2)}) copy-start(s32[6]{0:T(128)} %param.24) | copy-start | bytes 76
  159.6 412.5 %copy-start.52 = (f32[8,1024]{1,0:T(8,128)S(1)}, f32[8,1024]{1,0:T(8,128)}, u32[]{:S(2)}) copy-start(f32[8,1024]{1,0:T(8,128)} %param.32) | copy-start | bytes 98308
  159.6 490.1 %all-gather.5.cloned.1.call-start = ((), (), s32[]{:S(2)}) async-start(), calls=%async_computation.2 | async-start | bytes 15728640 | tf_op jit(solution)/shard_map/all_gather | solution.py:118
  568.4 445.9 %all-reduce.18.cloned.1.call-start = ((), (), s32[]{:S(2)}) async-start(), calls=%async_computation.3 | async-start | bytes 25165824 | tf_op jit(solution)/shard_map/psum | solution.py:126
  572.1 171.2 %copy-start.25 = (pred[6,512]{1,0:T(8,128)(4,1)}, pred[6,512]{1,0:T(8,128)(4,1)S(1)}, u32[]{:S(2)}) copy-start(pred[6,512]{1,0:T(8,128)(4,1)S(1)} %get-tuple-element.95) | copy-start | bytes 9220
  572.7 441.6 %copy-start.57 = (f32[1,1024]{1,0:T(1,128)}, f32[1,1024]{1,0:T(1,128)S(1)}, u32[]{:S(2)}) copy-start(f32[1,1024]{1,0:T(1,128)S(1)} %get-tuple-element.88) | copy-start | bytes 12292
  572.7 441.6 %copy-start.63 = (f32[1,1024]{1,0:T(1,128)}, f32[1,1024]{1,0:T(1,128)S(1)}, u32[]{:S(2)}) copy-start(f32[1,1024]{1,0:T(1,128)S(1)} %get-tuple-element.87) | copy-start | bytes 12292
  655.0 359.3 %copy-start.37 = (f32[6,512]{1,0:T(8,128)}, f32[6,512]{1,0:T(8,128)S(1)}, u32[]{:S(2)}) copy-start(f32[6,512]{1,0:T(8,128)S(1)} %broadcast_multiply_fusion.2) | copy-start | bytes 36868
  661.5 352.8 %copy-start.42 = (f32[6,512]{1,0:T(8,128)}, f32[6,512]{1,0:T(8,128)S(1)}, u32[]{:S(2)}) copy-start(f32[6,512]{1,0:T(8,128)S(1)} %fusion.94) | copy-start | bytes 36868
  793.5 583.0 %all-reduce.20.cloned.1.call-start = ((), (), s32[]{:S(2)}) async-start(), calls=%async_computation.4 | async-start | bytes 25165824 | tf_op jit(solution)/shard_map/psum | solution.py:129
  1024.1 748.9 %copy-start.39 = (f32[6,512]{1,0:T(8,128)}, f32[6,512]{1,0:T(8,128)S(1)}, u32[]{:S(2)}) copy-start(f32[6,512]{1,0:T(8,128)S(1)} %broadcast_multiply_fusion.1) | copy-start | bytes 36868
  1025.8 747.2 %copy-start.44 = (f32[6,512]{1,0:T(8,128)}, f32[6,512]{1,0:T(8,128)S(1)}, u32[]{:S(2)}) copy-start(f32[6,512]{1,0:T(8,128)S(1)} %fusion.95) | copy-start | bytes 36868
  1155.4 221.1 %copy-start.59 = (f32[1,1024]{1,0:T(1,128)S(1)}, f32[1,1024]{1,0:T(1,128)}, u32[]{:S(2)}) copy-start(f32[1,1024]{1,0:T(1,128)} %get-tuple-element.85) | copy-start | bytes 12292
  1155.4 221.1 %copy-start.65 = (f32[1,1024]{1,0:T(1,128)S(1)}, f32[1,1024]{1,0:T(1,128)}, u32[]{:S(2)}) copy-start(f32[1,1024]{1,0:T(1,128)} %get-tuple-element.84) | copy-start | bytes 12292
  1155.4 221.1 %copy-start.73 = (f32[1,1024]{1,0:T(1,128)S(1)}, f32[1,1024]{1,0:T(1,128)}, u32[]{:S(2)}) copy-start(f32[1,1024]{1,0:T(1,128)} %get-tuple-element.83) | copy-start | bytes 12292
  1155.4 600.7 %all-reduce.22.cloned.1.call-start = ((), (), s32[]{:S(2)}) async-start(), calls=%async_computation.5 | async-start | bytes 25165824 | tf_op jit(solution)/shard_map/psum | solution.py:151
  1535.3 694.1 %all-reduce.24.cloned.1.call-start = ((), (), s32[]{:S(2)}) async-start(), calls=%async_computation.6 | async-start | bytes 25165824 | tf_op jit(solution)/shard_map/psum | solution.py:154
  1588.2 184.7 %copy-start.51 = (f32[6,512]{1,0:T(8,128)S(1)}, f32[6,512]{1,0:T(8,128)}, u32[]{:S(2)}) copy-start(f32[6,512]{1,0:T(8,128)} %copy-done.50) | copy-start | bytes 36868
  2008.4 664.8 %all-reduce.26.cloned.1.call-start = ((), (), s32[]{:S(2)}) async-start(), calls=%async_computation.8 | async-start | bytes 26230784 | tf_op jit(solution)/shard_map/psum | solution.py:179
  2155.7 88.3 %copy-start.49 = (f32[6,512]{1,0:T(8,128)S(1)}, f32[6,512]{1,0:T(8,128)}, u32[]{:S(2)}) copy-start(f32[6,512]{1,0:T(8,128)} %copy-done.48) | copy-start | bytes 36868
  2260.8 894.0 %all-gather.7.cloned.1.call-start = ((), (), s32[]{:S(2)}) async-start(), calls=%async_computation.7 | async-start | bytes 28311552 | tf_op jit(solution)/shard_map/all_gather | solution.py:175
  2677.0 681.1 %copy-start.79 = (f32[256]{0:T(256)S(1)}, f32[256]{0:T(256)}, u32[]{:S(2)}) copy-start(f32[256]{0:T(256)} %param.35) | copy-start | bytes 3076
  2677.0 681.1 %copy-start.89 = (f32[256]{0:T(256)S(1)}, f32[256]{0:T(256)}, u32[]{:S(2)}) copy-start(f32[256]{0:T(256)} %param.45) | copy-start | bytes 3076
  2677.0 681.6 %copy-start.77 = (f32[2,256]{1,0:T(2,128)S(1)}, f32[2,256]{1,0:T(2,128)}, u32[]{:S(2)}) copy-start(f32[2,256]{1,0:T(2,128)} %param.30) | copy-start | bytes 6148
  2677.0 681.6 %copy-start.88 = (f32[2,256]{1,0:T(2,128)S(1)}, f32[2,256]{1,0:T(2,128)}, u32[]{:S(2)}) copy-start(f32[2,256]{1,0:T(2,128)} %param.40) | copy-start | bytes 6148
  2677.0 682.2 %copy-start.75 = (f32[1024]{0:T(1024)S(1)}, f32[1024]{0:T(1024)}, u32[]{:S(2)}) copy-start(f32[1024]{0:T(1024)} %param.31) | copy-start | bytes 12292
  2677.1 682.2 %copy-start.82 = (f32[1024]{0:T(1024)S(1)}, f32[1024]{0:T(1024)}, u32[]{:S(2)}) copy-start(f32[1024]{0:T(1024)} %param.41) | copy-start | bytes 12292
  2677.1 682.8 %copy-start.53 = (f32[8,1024]{1,0:T(8,128)S(1)}, f32[8,1024]{1,0:T(8,128)}, u32[]{:S(2)}) copy-start(f32[8,1024]{1,0:T(8,128)} %param.32) | copy-start | bytes 98308
  2677.1 682.8 %copy-start.62 = (f32[8,1024]{1,0:T(8,128)S(1)}, f32[8,1024]{1,0:T(8,128)}, u32[]{:S(2)}) copy-start(f32[8,1024]{1,0:T(8,128)} %param.42) | copy-start | bytes 98308
  3310.9 61.4 %slice-start.3 = ((s8[6463488]{0:T(1024)(128)(4,1)}), s8[2269184]{0:T(1024)(128)(4,1)S(1)}, s32[]{:S(2)}) async-start(s8[6463488]{0:T(1024)(128)(4,1)} %bitcast.166), calls=%async_computation.12 | async-start | bytes 4538368
  (76 other events, 1032.1 us)
Sparse Core Ops, SparseCore 0:
  159.7 404.6 reduce-scatter.1
  568.5 81.2 all-gather.4
  793.6 220.6 all-reduce.17
  1155.5 220.8 all-reduce.19
  1535.5 220.6 all-reduce.21
  2008.6 220.8 all-reduce.23
  2260.9 412.2 all-reduce.25
  2675.4 479.3 all-gather.6
where the time goes:
time: 3420 us; the launch traced here: 3410 us
  waiting for transfers between devices  1990 us (58%)
  matrix products  707 us (21%)
  other arithmetic  407 us (12%)
  blocking collectives  149 us (4%)
  local copies, waits for them, and re-layouts  125 us (4%)
    dot_general x27, matrix products, precise_product(): return jnp.matmul(left, right, precision=HIGH)  541 us
    all_gather x1, waiting for transfers between devices, on_device(): lax.all_gather(back_flat, 'dp', axis=0, tiled=True)  466 us
    reduce_scatter x1, waiting for transfers between devices, on_device(): lax.psum_scatter(jnp.take(padded_table, rows_ids, axis=0), 'dp', scatter_...  404 us
    psum x1, waiting for transfers between devices, on_device(): lax.psum((grad_attn, grad_ffn, grad_positions, grad_bias_qv, grad_bias_up...  364 us
    psum x1, waiting for transfers between devices, on_device(): x_one = h_zero + lax.psum(attn_part, 'tensor') + norms[6]  221 us
    psum x1, waiting for transfers between devices, on_device(): x_two = h_one + lax.psum(ffn_part, 'tensor') + norms[7]  220 us
    psum x1, waiting for transfers between devices, on_device(): back_h_one = back_x_two + lax.psum(back_h_one_part, 'tensor')  168 us
    scatter-add x1, other arithmetic, on_device(): jax.ops.segment_sum(lax.all_gather(back_flat, 'dp', axis=0, tiled=True),...  151 us
  transfers between devices with their start and end apart: 8, of which 8 were waited for; matrix products, arithmetic and copies ran while one was open for 6% of the time, Pallas kernels for 0%

commit v1 on v0

--- a/solution.py
+++ b/solution.py
@@ -1,3 +1,4 @@
+import functools
 import math
 
 import jax
@@ -15,6 +16,8 @@
 RATE = 100000.0
 CLIP_SCALE = 1e-06
 HIGH = lax.Precision.HIGHEST
+PRODUCT = lax.Precision.HIGH
+CAPACITY = 96
 
 
 def precise_product(left, right):
@@ -233,6 +236,335 @@
     )
 
 
+def normalise(values):
+    center = values - jnp.mean(values, axis=-1, keepdims=True)
+    scale = lax.rsqrt(jnp.mean(center * center, axis=-1, keepdims=True) + EPS)
+    return center * scale, scale
+
+
+def normalise_back(back, gain, unit, scale):
+    inner = back * gain
+    grad = scale * (
+        inner
+        - jnp.mean(inner, axis=-1, keepdims=True)
+        - unit * jnp.mean(inner * unit, axis=-1, keepdims=True)
+    )
+    return grad, jnp.sum(back * unit, axis=0), jnp.sum(back, axis=0)
+
+
+def gelu_both(values):
+    cdf = 0.5 * (1.0 + lax.erf(values * math.sqrt(0.5)))
+    pdf = jnp.exp(-0.5 * values * values) * (1.0 / math.sqrt(2.0 * math.pi))
+    return values * cdf, cdf + values * pdf
+
+
+def product(subscripts, left, right):
+    return jnp.einsum(subscripts, left, right, precision=PRODUCT)
+
+
+def request_lists(ids, vocab_rows, owners):
+    count = ids.shape[0]
+    index = lax.broadcasted_iota(jnp.int32, (count,), 0)
+    earlier = index[None, :] < index[:, None]
+    same = (ids[None, :] == ids[:, None]) & earlier
+    first = jnp.logical_not(jnp.any(same, axis=1))
+    owner = ids // vocab_rows
+    ahead = (owner[None, :] == owner[:, None]) & earlier & first[None, :]
+    rank = jnp.sum(ahead.astype(jnp.int32), axis=1)
+    return owner, jnp.where(first, rank, -1)
+
+
+def round_list(ids, owner, rank, round_index, owners):
+    place = rank - round_index * CAPACITY
+    inside = (rank >= 0) & (place >= 0) & (place < CAPACITY)
+    place = jnp.where(inside, owner * CAPACITY + place, -1)
+    wanted = lax.broadcasted_iota(jnp.int32, (owners * CAPACITY, 1), 0)
+    return jnp.sum(jnp.where(place[None, :] == wanted, ids[None, :] + 1, 0), axis=1) - 1
+
+
+def trade(block):
+    return lax.all_to_all(block, ("dp", "tensor"), 0, 0, tiled=True)
+
+
+def fast_on_device(
+    token_ids, lengths, partners, embedding, positions, attn_weights, ffn_weights, bias_qv, bias_up, norms,
+    head_first, head_second, head_bias, mom_embedding, mom_positions, mom_attn, ffn_momentum, mom_bias_qv,
+    mom_bias_up, mom_norms, mom_head_first, mom_head_second, mom_head_bias, *, groups, shards
+):
+    seqs, slots = token_ids.shape
+    half = slots // 2
+    vocab_rows, cols = embedding.shape
+    width = cols * shards
+    devices = groups * shards
+    hidden = bias_up.shape[0]
+    heads = width // HEAD_DIM
+    dp_rank = lax.axis_index("dp")
+    tp_rank = lax.axis_index("tensor")
+    pair = tp_rank // 2
+    side = tp_rank % 2
+    base = dp_rank * vocab_rows
+
+    whole_seq = 3 * pair + 2 * side
+    split_seq = 3 * pair + 1
+    whole_ids = lax.dynamic_index_in_dim(token_ids, whole_seq, 0, keepdims=False)
+    split_ids = lax.dynamic_index_in_dim(token_ids, split_seq, 0, keepdims=False)
+    ids = jnp.concatenate([whole_ids, lax.dynamic_slice_in_dim(split_ids, side * half, half)])
+    count = ids.shape[0]
+    whole_length = lax.dynamic_index_in_dim(lengths, whole_seq, 0, keepdims=False)
+    split_length = lax.dynamic_index_in_dim(lengths, split_seq, 0, keepdims=False)
+
+    all_attn = lax.all_gather(attn_weights, "tensor")
+    all_ffn_up = lax.all_gather(ffn_weights[0], "tensor")
+    all_ffn_down = lax.all_gather(ffn_weights[1], "tensor")
+    small = jnp.concatenate([positions[2 : slots + 2], bias_qv, bias_up.reshape(-1, cols)], axis=0)
+    all_small = lax.all_gather(small, "tensor")
+    all_positions = all_small[:, :slots].transpose(1, 0, 2).reshape(slots, width)
+    all_bias_qv = all_small[:, slots : slots + 2].transpose(1, 0, 2).reshape(2, width)
+    all_bias_up = all_small[:, slots + 2 :].reshape(-1)
+
+    owner, rank = request_lists(ids, vocab_rows, groups)
+    rounds_here = jnp.max(rank) // CAPACITY + 1
+
+    def serve(round_index):
+        wanted = round_list(ids, owner, rank, round_index, groups)
+        lists = jnp.broadcast_to(wanted.reshape(groups, 1, CAPACITY), (groups, shards, CAPACITY))
+        lists = lists.reshape(devices, CAPACITY)
+        tail = jnp.broadcast_to(rounds_here, (devices, 1)).astype(jnp.int32)
+        lists = jnp.concatenate([lists, tail, jnp.zeros((devices, 127 - CAPACITY % 128), jnp.int32)], axis=1)
+        asked = trade(lists)
+        rows = asked[:, :CAPACITY].reshape(-1) - base
+        rounds = jnp.max(asked[:, CAPACITY])
+        return wanted, rows, rounds
+
+    def fetch(wanted, rows):
+        found = jnp.take(embedding, rows, axis=0, mode="clip")
+        landed = trade(found).reshape(groups, shards, CAPACITY, cols)
+        landed = landed.transpose(0, 2, 1, 3).reshape(groups * CAPACITY, width)
+        chosen = (ids[:, None] == wanted[None, :]).astype(jnp.float32)
+        return jnp.matmul(chosen, landed, precision=HIGH)
+
+    wanted_first, rows_first, rounds = serve(0)
+    tokens = fetch(wanted_first, rows_first)
+
+    def more(state):
+        return state[0] < rounds
+
+    def fetch_more(state):
+        round_index, total = state
+        wanted, rows, _ = serve(round_index)
+        return round_index + 1, total + fetch(wanted, rows)
+
+    _, tokens = lax.while_loop(more, fetch_more, (jnp.int32(1), tokens))
+    own_positions = jnp.concatenate(
+        [all_positions, lax.dynamic_slice_in_dim(all_positions, side * half, half)], axis=0
+    )
+    embedded = tokens + own_positions
+    unit_zero, scale_zero = normalise(embedded)
+    h_zero = unit_zero * norms[0] + norms[1]
+
+    swap = [(i, i ^ 1) for i in range(shards)]
+    h_other = lax.ppermute(h_zero[slots:], "tensor", swap)
+    h_keys = jnp.concatenate([h_zero, h_other], axis=0)
+    queries = product("td,jdc->tjc", h_zero, all_attn[:, 0]).reshape(count, width) + all_bias_qv[0]
+    keys_all = product("td,jdc->tjc", h_keys, all_attn[:, 1]).reshape(count + half, width)
+    values = product("td,jdc->tjc", h_keys, all_attn[:, 2]).reshape(count + half, width) + all_bias_qv[1]
+    key_index = lax.broadcasted_iota(jnp.int32, (slots,), 0)
+    own_first = jnp.where(
+        key_index < half, side * half + key_index, (1 - side) * half + key_index - half
+    )
+    root = 1.0 / math.sqrt(HEAD_DIM)
+
+    def split_heads(array):
+        return array.reshape(-1, heads, HEAD_DIM)
+
+    def attend_block(q, k, v, valid):
+        scores = product("qhd,khd->hqk", q, k) * root
+        scores = jnp.where(valid[None, None, :], scores, -1e30)
+        probs = jnp.exp(scores - jnp.max(scores, axis=-1, keepdims=True))
+        probs = probs / jnp.sum(probs, axis=-1, keepdims=True)
+        return probs, product("hqk,khd->qhd", probs, v)
+
+    q_whole, q_split = split_heads(queries[:slots]), split_heads(queries[slots:])
+    k_whole, k_split = split_heads(keys_all[:slots]), split_heads(keys_all[slots:])
+    v_whole, v_split = split_heads(values[:slots]), split_heads(values[slots:])
+    p_whole, a_whole = attend_block(q_whole, k_whole, v_whole, key_index < whole_length)
+    p_split, a_split = attend_block(q_split, k_split, v_split, own_first < split_length)
+    mixed = jnp.concatenate([a_whole.reshape(slots, width), a_split.reshape(half, width)], axis=0)
+    mixed_parts = mixed.reshape(count, shards, cols)
+    x_one = h_zero + product("tjc,jdc->td", mixed_parts, all_attn[:, 3]) + norms[6]
+    unit_one, scale_one = normalise(x_one)
+    h_one = unit_one * norms[2] + norms[3]
+
+    up = product("td,jdc->tjc", h_one, all_ffn_up) + all_bias_up.reshape(shards, hidden)
+    act, act_slope = gelu_both(up)
+    x_two = h_one + product("tjc,jdc->td", act, all_ffn_down) + norms[7]
+    unit_two, scale_two = normalise(x_two)
+    h_two = unit_two * norms[4] + norms[5]
+
+    slot = lax.broadcasted_iota(jnp.int32, (count,), 0)
+    in_whole = slot < slots
+    place = jnp.where(in_whole, slot, slot - slots + side * half)
+    keep = place < jnp.where(in_whole, whole_length, split_length)
+    weight_whole = jnp.where(keep & in_whole, 1.0 / whole_length.astype(jnp.float32), 0.0)
+    weight_split = jnp.where(keep & ~in_whole, 1.0 / split_length.astype(jnp.float32), 0.0)
+    sums = jnp.stack(
+        [jnp.sum(h_two * weight_whole[:, None], axis=0), jnp.sum(h_two * weight_split[:, None], axis=0)]
+    )
+    all_sums = lax.all_gather(sums, ("dp", "tensor")).reshape(groups * shards // 2, 2, 2, width)
+    all_pooled = jnp.stack(
+        [all_sums[:, 0, 0], all_sums[:, 0, 1] + all_sums[:, 1, 1], all_sums[:, 1, 0]], axis=1
+    ).reshape(groups * seqs, width)
+    loss, head_pull = jax.vjp(
+        lambda rows, first_w, second_w, bias_w: contrast(rows, first_w, second_w, bias_w, partners),
+        all_pooled,
+        head_first,
+        head_second,
+        head_bias,
+    )
+    back_pooled, grad_head_first, grad_head_second, grad_head_bias = head_pull(jnp.ones_like(loss))
+    first_row = dp_rank * seqs
+    back_whole = lax.dynamic_index_in_dim(back_pooled, first_row + whole_seq, 0, keepdims=False)
+    back_split = lax.dynamic_index_in_dim(back_pooled, first_row + split_seq, 0, keepdims=False)
+    back_h_two = weight_whole[:, None] * back_whole[None, :] + weight_split[:, None] * back_split[None, :]
+
+    back_x_two, grad_gain_two, grad_shift_two = normalise_back(back_h_two, norms[4], unit_two, scale_two)
+    grad_down = product("td,tjc->jdc", back_x_two, act)
+    sum_down = lax.psum_scatter(grad_down, "tensor", scatter_dimension=0, tiled=False)
+    back_up = product("td,jdc->tjc", back_x_two, all_ffn_down) * act_slope
+    grad_up = product("td,tjc->jdc", h_one, back_up)
+    sum_up = lax.psum_scatter(grad_up, "tensor", scatter_dimension=0, tiled=False)
+    grad_bias_up = jnp.sum(back_up, axis=0)
+    back_h_one = back_x_two + product("tjc,jdc->td", back_up, all_ffn_up)
+    back_x_one, grad_gain_one, grad_shift_one = normalise_back(back_h_one, norms[2], unit_one, scale_one)
+
+    back_mixed_parts = product("td,jdc->tjc", back_x_one, all_attn[:, 3])
+    grad_out = product("td,tjc->jdc", back_x_one, mixed_parts)
+    back_mixed = back_mixed_parts.reshape(count, width)
+
+    def attend_back(q, k, v, probs, mixed_block, back):
+        back_v = product("hqk,qhd->khd", probs, back)
+        back_p = product("qhd,khd->hqk", back, v)
+        inner = jnp.sum(back * mixed_block, axis=-1).T
+        back_s = probs * (back_p - inner[:, :, None]) * root
+        return product("hqk,khd->qhd", back_s, k), product("hqk,qhd->khd", back_s, q), back_v
+
+    dq_whole, dk_whole, dv_whole = attend_back(
+        q_whole, k_whole, v_whole, p_whole, a_whole, split_heads(back_mixed[:slots])
+    )
+    dq_split, dk_split, dv_split = attend_back(
+        q_split, k_split, v_split, p_split, a_split, split_heads(back_mixed[slots:])
+    )
+    back_q = jnp.concatenate([dq_whole, dq_split], axis=0).reshape(count, shards, cols)
+    back_k = jnp.concatenate([dk_whole, dk_split], axis=0).reshape(count + half, shards, cols)
+    back_v = jnp.concatenate([dv_whole, dv_split], axis=0).reshape(count + half, shards, cols)
+    back_keys = product("tjc,jdc->td", back_k, all_attn[:, 1]) + product("tjc,jdc->td", back_v, all_attn[:, 2])
+    back_other = lax.ppermute(back_keys[count:], "tensor", swap)
+    grad_q = product("td,tjc->jdc", h_zero, back_q)
+    grad_k = product("td,tjc->jdc", h_keys, back_k)
+    grad_v = product("td,tjc->jdc", h_keys, back_v)
+    back_h_zero = back_x_one + product("tjc,jdc->td", back_q, all_attn[:, 0]) + back_keys[:count]
+    back_h_zero = back_h_zero + jnp.pad(back_other, ((slots, 0), (0, 0)))
+    back_embedded, grad_gain_zero, grad_shift_zero = normalise_back(back_h_zero, norms[0], unit_zero, scale_zero)
+
+    def give_back(wanted, rows, listed, total):
+        chosen = (wanted[:, None] == ids[None, :]).astype(jnp.float32)
+        summed = jnp.matmul(chosen, back_embedded, precision=HIGH)
+        parts = summed.reshape(groups, CAPACITY, shards, cols).transpose(0, 2, 1, 3)
+        landed = trade(parts.reshape(devices * CAPACITY, cols))
+        target = jnp.where(rows >= 0, rows, vocab_rows)
+        return total.at[target].add(landed, mode="drop")
+
+    zero_table = jnp.zeros((vocab_rows, cols), jnp.float32)
+    grad_embedding = give_back(wanted_first, rows_first, None, zero_table)
+
+    def give_more(state):
+        round_index, total = state
+        wanted, rows, _ = serve(round_index)
+        return round_index + 1, give_back(wanted, rows, None, total)
+
+    _, grad_embedding = lax.while_loop(more, give_more, (jnp.int32(1), grad_embedding))
+
+    half_rows = jnp.where(side == 0, 1.0, 0.0) * back_embedded[slots:]
+    other_rows = back_embedded[slots:] - half_rows
+    grad_pos_full = back_embedded[:slots] + jnp.concatenate([half_rows, other_rows], axis=0)
+    grad_pos_parts = grad_pos_full.reshape(slots, shards, cols).transpose(1, 0, 2)
+    grad_attn_parts = jnp.concatenate([grad_q, grad_k, grad_v, grad_out, grad_pos_parts], axis=1)
+    sum_attn = lax.psum_scatter(grad_attn_parts, "tensor", scatter_dimension=0, tiled=False)
+    with jax.named_scope("sum_ffn_down"):
+        sum_down = lax.psum(sum_down, "dp")
+    sum_down, sum_up = lax.optimization_barrier((sum_down, sum_up))
+    sum_up = lax.psum(sum_up, "dp")
+    sum_up, sum_attn = lax.optimization_barrier((sum_up, sum_attn))
+    sum_attn = lax.psum(sum_attn, "dp")
+    grad_small = jnp.concatenate(
+        [
+            jnp.stack(
+                [
+                    grad_gain_zero,
+                    grad_shift_zero,
+                    grad_gain_one,
+                    grad_shift_one,
+                    grad_gain_two,
+                    grad_shift_two,
+                    jnp.sum(back_x_one, axis=0),
+                    jnp.sum(back_x_two, axis=0),
+                    jnp.sum(back_q, axis=0).reshape(-1),
+                    jnp.sum(back_v, axis=0).reshape(-1),
+                ]
+            ),
+            grad_bias_up.reshape(-1, width),
+        ],
+        axis=0,
+    )
+    sum_small = lax.psum(grad_small, ("dp", "tensor"))
+    grad_norms = sum_small[:8]
+    grad_bias_qv = lax.dynamic_slice_in_dim(sum_small[8:10], tp_rank * cols, cols, 1)
+    grad_bias_up = lax.dynamic_slice_in_dim(sum_small[10:].reshape(-1), tp_rank * hidden, hidden)
+    grad_attn = sum_attn[: 4 * width].reshape(4, width, cols)
+    grad_ffn_up, grad_ffn_down = sum_up, sum_down
+    grad_pos = sum_attn[4 * width :]
+
+    first_dp = (dp_rank == 0).astype(jnp.float32)
+    first_all = first_dp * (tp_rank == 0).astype(jnp.float32)
+    local_squares = (
+        squares(grad_embedding)
+        + first_dp
+        * (
+            squares(sum_attn)
+            + squares(grad_ffn_up)
+            + squares(grad_ffn_down)
+            + squares(grad_bias_qv)
+            + squares(grad_bias_up)
+        )
+        + first_all
+        * (
+            squares(grad_norms)
+            + squares(grad_head_first)
+            + squares(grad_head_second)
+            + squares(grad_head_bias)
+        )
+    )
+    grad_norm = jnp.sqrt(lax.psum(local_squares, ("dp", "tensor")))
+    factor = jnp.minimum(1.0, CLIP_SCALE * math.sqrt(PARAMS) / (grad_norm + 1e-06))
+    grad_positions = jnp.pad(grad_pos, ((2, positions.shape[0] - slots - 2), (0, 0)))
+    grad_ffn = jnp.stack([grad_ffn_up, grad_ffn_down])
+    new_embedding, next_embedding = advance(embedding, mom_embedding, grad_embedding, factor)
+    new_positions, next_positions = advance(positions, mom_positions, grad_positions, factor)
+    new_attn, next_attn = advance(attn_weights, mom_attn, grad_attn, factor)
+    new_ffn, next_ffn = advance(ffn_weights, ffn_momentum, grad_ffn, factor)
+    new_bias_qv, next_bias_qv = advance(bias_qv, mom_bias_qv, grad_bias_qv, factor)
+    new_bias_up, next_bias_up = advance(bias_up, mom_bias_up, grad_bias_up, factor)
+    new_norms, next_norms = advance(norms, mom_norms, grad_norms, factor)
+    new_head_first, next_head_first = advance(head_first, mom_head_first, grad_head_first, factor)
+    new_head_second, next_head_second = advance(head_second, mom_head_second, grad_head_second, factor)
+    new_head_bias, next_head_bias = advance(head_bias, mom_head_bias, grad_head_bias, factor)
+    return (
+        new_embedding, new_positions, new_attn, new_ffn, new_bias_qv, new_bias_up, new_norms, new_head_first,
+        new_head_second, new_head_bias, next_embedding, next_positions, next_attn, next_ffn, next_bias_qv,
+        next_bias_up, next_norms, next_head_first, next_head_second, next_head_bias, loss, grad_norm,
+    )
+
+
 def solution(mesh):
     in_specs = (
         P("dp", None),
@@ -283,6 +615,14 @@
         P(),
         P(),
     )
-    return jax.shard_map(
-        on_device, mesh=mesh, in_specs=in_specs, out_specs=out_specs, check_vma=False
-    )
+    groups, shards = mesh.shape["dp"], mesh.shape["tensor"]
+
+    def run(*arrays):
+        body = on_device
+        if 2 * (arrays[0].shape[0] // groups) == 3 * shards:
+            body = functools.partial(fast_on_device, groups=groups, shards=shards)
+        return jax.shard_map(
+            body, mesh=mesh, in_specs=in_specs, out_specs=out_specs, check_vma=False
+        )(*arrays)
+
+    return run

time: 3420 us -> 1570 us (0.46)
  waiting for transfers between devices: 1990 us -> 670 us
  other arithmetic: 407 us -> 120 us
  matrix products: 707 us -> 440 us
    psum x5 -> x3, waiting for transfers between devices: 1050 us -> 463 us  [the longest x1 162 us: fast_on_device(): sum_attn = lax.psum(sum_attn, 'dp')]
    dot_general x27 -> x9, matrix products: 541 us -> 11.2 us  [precise_product(): return jnp.matmul(left, right, precision=HIGH)]
    all_gather x2 -> x4, waiting for transfers between devices: 543 us -> 96.8 us  [the longest x1 72.8 us: fast_on_device(): all_ffn_down = lax.all_gather(ffn_weights[1], 'tensor')]
    reduce_scatter x1 -> x3, waiting for transfers between devices: 404 us -> 43.1 us  [the longest x1 43.1 us: fast_on_device(): lax.psum_scatter(grad_attn_parts, 'tensor', scatter_dimension=0, tiled=Fa...]
    dot_general x6 -> x32, matrix products: 166 us -> 429 us  [the longest x30 416 us: product(): return jnp.einsum(subscripts, left, right, precision=PRODUCT)]
    scatter-add x1, other arithmetic: 151 us -> 20.6 us  [give_back(): return total.at[target].add(landed, mode='drop')]
    reduce_sum x15 -> x16, other arithmetic: 108 us -> 20.5 us  [the longest x2 6.04 us: attend_block(): probs = probs / jnp.sum(probs, axis=-1, keepdims=True)]
    gather x1, local copies, waits for them, and re-layouts: 95.1 us -> 15.2 us  [fetch(): found = jnp.take(embedding, rows, axis=0, mode='clip')]
  transfers between devices with their start and end apart: 8 -> 15, of which waited for: 8 -> 8; matrix products, arithmetic and copies ran while one was open for 6% -> 35% of each run, Pallas kernels for 0% -> 0%
where the time goes in v1:
time: 1570 us; the launch traced here: 1560 us
  waiting for transfers between devices  670 us (43%)
  matrix products  440 us (28%)
  local copies, waits for them, and re-layouts  157 us (10%)
  other arithmetic  120 us (8%)
  blocking collectives  119 us (8%)
  between operations  28.1 us (2%)
    dot_general x30, matrix products, product(): return jnp.einsum(subscripts, left, right, precision=PRODUCT)  416 us
    psum x1, waiting for transfers between devices, fast_on_device(): sum_attn = lax.psum(sum_attn, 'dp')  162 us
    psum x1, waiting for transfers between devices, fast_on_device(): sum_up = lax.psum(sum_up, 'dp')  160 us
    psum x1, waiting for transfers between devices, fast_on_device(): sum_down = lax.psum(sum_down, 'dp')  140 us
    all_gather x1, waiting for transfers between devices, fast_on_device(): all_ffn_down = lax.all_gather(ffn_weights[1], 'tensor')  72.8 us
    all_to_all x3, waiting for transfers between devices, trade(): return lax.all_to_all(block, ('dp', 'tensor'), 0, 0, tiled=True)  66 us
    unnamed x286, local copies, waits for them, and re-layouts  65.2 us
    reduce_scatter x1, waiting for transfers between devices, fast_on_device(): lax.psum_scatter(grad_attn_parts, 'tensor', scatter_dimension=0, tiled=Fa...  43.1 us
  transfers between devices with their start and end apart: 15, of which 8 were waited for; matrix products, arithmetic and copies ran while one was open for 35% of the time, Pallas kernels for 0%

profile of v1, /device:TPU:0, one launch (start us, length us, event | category | flops | bytes accessed | tf_op | source)
XLA Modules:
  0.0 1558.1 jit_solution(14142041608199921427)
XLA Ops:
  40.6 15.2 gather_fusion.1
  71.5 58.9 %all-to-all-done.5 = f32[32,96,256]{2,1,0:T(8,128)S(1)} async-done(((f32[32,96,256]{2,1,0:T(8,128)}), f32[32,96,256]{2,1,0:T(8,128)S(1)}, u32[]{:S(2)}, u32[]{:S(2)}) %all-to-all-start.5) | async-done | bytes 3145760 | tf_op jit(solution)/shard_map/all_to_all | solution.py:286
  153.4 24.0 %all-gather.14.cloned.1.call-done = f32[16,1024,256]{2,1,0:T(8,128)} async-done(((f32[4,1024,256]{2,1,0:T(8,128)}), f32[16,1024,256]{2,1,0:T(8,128)}) %all-gather.14.cloned.1.call-update) | async-done | bytes 16777232 | tf_op jit(solution)/shard_map/all_gather | solution.py:316
  232.7 9.4 fusion.11
  293.7 26.9 %fusion.52 = f32[768,4,1024]{2,0,1:T(8,128)} fusion(f32[4,1024,1024]{2,1,0:T(8,128)} %all-gather.10.cloned.1.call-done, f32[1024]{0:T(1024)S(1)} %bitcast.452, f32[1024]{0:T(1024)S(1)} %bitcast.430, f32[768,1024]{1,0:T(8,128)} %copy-done.15, f32[768]{0:T(1024)S(1)} %add_rsqrt_fusion.1, f32[768]{0:T(1024)S(1)} %broadcast_multiply_fusion.7), kind=kOutput, calls=%fused_computation.114 | convolution fusion | flops 19330498560 | bytes 32520192 | tf_op jit(solution)/shard_map/td,jdc->tjc/dot_general | solution.py:262
  320.6 72.8 %all-gather.12.cloned.1.call-done = f32[4,1024,1024]{2,1,0:T(8,128)} async-done(((f32[1,1024,1024]{2,1,0:T(8,128)}), f32[4,1024,1024]{2,1,0:T(8,128)}) %all-gather.12.cloned.1.call-update) | async-done | bytes 16777232 | tf_op jit(solution)/shard_map/all_gather | solution.py:318
  393.5 29.8 %fusion.146 = (f32[768]{0:T(1024)S(1)}, f32[768,1024]{1,0:T(8,128)S(1)}) fusion(f32[1024]{0:T(1024)S(1)} %bitcast.457, f32[4,1024,1024]{2,1,0:T(8,128)} %all-gather.12.cloned.1.call-done, f32[768,4,1024]{2,0,1:T(8,128)} %fusion.52, f32[4,1024]{1,0:T(4,128)S(1)} %bitcast.446, f32[1024]{0:T(1024)S(1)} %bitcast.453, f32[1024]{0:T(1024)S(1)} %bitcast.431, ...), kind=kOutput, calls=%fused_computation.338 | convolution fusion | flops 19348586496 | bytes 35689472 | tf_op jit(solution)/shard_map/tjc,jdc->td/dot_general | solution.py:262
  425.1 41.2 %all-gather.4 = f32[32,2,1024]{2,1,0:T(2,128)S(1)} all-gather(f32[1,2,1024]{2,1,0:T(2,128)S(1)} %maximum_bitcast_fusion.1), channel_id=4, replica_groups=mesh['dp'=8,'tensor'=4] {'dp','tensor'}, dimensions={0}, use_global_device_ids=true | all-gather | bytes 270336 | tf_op jit(solution)/shard_map/all_gather | solution.py:413
  477.9 28.9 %convolution_bitcast_fusion.1 = f32[4,1024,1024]{1,2,0:T(8,128)} fusion(f32[768,4,1024]{2,0,1:T(8,128)} %fusion.52, f32[4,1024]{1,0:T(4,128)S(1)} %bitcast.447, f32[768,1024]{1,0:T(8,128)S(1)} %get-tuple-element.496, f32[768]{0:T(1024)S(1)} %broadcast_multiply_fusion.4, f32[768]{0:T(1024)S(1)} %broadcast_multiply_fusion.5, f32[1024]{0:T(1024)S(1)} %bitcast.420, ...), kind=kOutput, calls=%fused_computation.45 | convolution fusion | flops 19350945792 | bytes 32552960 | tf_op jit(solution)/shard_map/td,tjc->jdc/dot_general | solution.py:262
  506.9 36.2 %fusion.152 = (f32[4,1024]{1,0:T(4,128)}, f32[768,4,1024]{2,0,1:T(8,128)}) fusion(f32[768,4,1024]{2,0,1:T(8,128)} %fusion.52, f32[4,1024]{1,0:T(4,128)S(1)} %bitcast.448, f32[4,1024,1024]{2,1,0:T(8,128)} %all-gather.12.cloned.1.call-done, f32[768]{0:T(1024)S(1)} %broadcast_multiply_fusion.4, f32[768,1024]{1,0:T(8,128)S(1)} %get-tuple-element.496, ...), kind=kOutput, calls=%fused_computation.344 | convolution fusion | flops 19369816064 | bytes 45152256 | tf_op jit(solution)/shard_map/td,jdc->tjc/dot_general | solution.py:262
  543.1 26.9 %convolution_bitcast_fusion = f32[4,1024,1024]{1,2,0:T(8,128)} fusion(f32[768,4,1024]{2,0,1:T(8,128)} %get-tuple-element.516, f32[1024]{0:T(1024)S(1)} %bitcast.454, f32[1024]{0:T(1024)S(1)} %bitcast.432, f32[768,1024]{1,0:T(8,128)} %copy-done.15, f32[768]{0:T(1024)S(1)} %add_rsqrt_fusion.1, f32[768]{0:T(1024)S(1)} %broadcast_multiply_fusion.7), kind=kOutput, calls=%fused_computation.44 | convolution fusion | flops 19330498560 | bytes 32520192 | tf_op jit(solution)/shard_map/td,tjc->jdc/dot_general | solution.py:262
  570.1 31.7 %multiply_reduce_fusion.5 = (f32[1024]{0:T(1024)}, f32[768]{0:T(1024)S(1)}, f32[768]{0:T(1024)S(1)}, f32[1024]{0:T(1024)}, f32[768,1024]{1,0:T(8,128)S(1)}) fusion(f32[768]{0:T(1024)S(1)} %add_rsqrt_fusion.1, f32[768,1024]{1,0:T(8,128)} %copy-done.15, f32[768]{0:T(1024)S(1)} %broadcast_multiply_fusion.7, f32[1024]{0:T(1024)S(1)} %bitcast.433, ...), kind=kOutput, calls=%fused_computation.119 | convolution fusion | flops 19343077376 | bytes 38852608 | tf_op jit(solution)/shard_map/tjc,jdc->td/dot_general | solution.py:262
  603.6 9.2 fusion.36
  625.8 20.6 %multiply_multiply_fusion.1 = f32[16,512,512]{1,2,0:T(8,128)} fusion(f32[512,16,64]{0,2,1:T(8,128)S(1)} %bitcast.373, f32[512,16,64]{0,2,1:T(8,128)S(1)} %bitcast.391, f32[16,512]{1,0:T(8,128)S(1)} %bitcast.426, f32[16,512]{1,0:T(8,128)S(1)} %copy-done.95, f32[16,512]{1,0:T(8,128)S(1)} %copy-done.71, f32[16,512,512]{1,2,0:T(8,128)} %copy-done.4, ...), kind=kOutput, calls=%fused_computation.31 | convolution fusion | flops 1639972864 | bytes 37847552 | tf_op jit(solution)/shard_map/qhd,khd->hqk/dot_general | solution.py:262
  646.4 13.5 convolution_bitcast_fusion.5
  671.1 12.3 fusion.150
  687.5 16.1 %fusion.25 = f32[1024,1024,1]{1,0,2:T(8,128)S(1)} fusion(f32[1024,4,256]{0,2,1:T(8,128)S(1)} %bitcast.381, f32[4,4,1024,256]{3,2,1,0:T(8,128)} %bitcast.359), kind=kOutput, calls=%fused_computation.69 | convolution fusion | flops 6442450944 | bytes 12582912 | tf_op jit(solution)/shard_map/tjc,jdc->td/dot_general | solution.py:262
  703.6 16.2 %bitcast_add_fusion = f32[1024,1024]{1,0:T(8,128)S(1)} fusion(f32[1024,1024,1]{1,0,2:T(8,128)S(1)} %fusion.25, f32[1024,4,256]{0,2,1:T(8,128)S(1)} %bitcast.380, f32[4,4,1024,256]{3,2,1,0:T(8,128)} %bitcast.360), kind=kOutput, calls=%fused_computation.77 | convolution fusion | flops 6443499520 | bytes 16777216 | tf_op jit(solution)/shard_map/tjc,jdc->td/dot_general | solution.py:262
  727.7 10.0 fusion.148
  747.6 10.7 bitcast_dynamic-update-slice_fusion.2
  758.3 9.5 bitcast_dynamic-update-slice_fusion.1
  774.8 14.9 multiply_reduce_fusion.6
  818.2 140.1 %all-reduce.6.cloned.1.call-done = f32[1024,1024]{0,1:T(8,128)} async-done(((f32[1024,1024]{0,1:T(8,128)}), f32[1024,1024]{0,1:T(8,128)}) %all-reduce.6.cloned.1.call-update) | async-done | bytes 4194320 | tf_op jit(solution)/shard_map/sum_ffn_down/psum | solution.py:494
  968.4 11.8 copy.249
  994.3 38.2 %psum.38 = f32[14,1024]{1,0:T(8,128)S(1)} all-reduce(f32[14,1024]{1,0:T(8,128)S(1)} %concatenate.97), channel_id=1, replica_groups=mesh['dp'=8,'tensor'=4] {'dp','tensor'}, use_global_device_ids=true, to_apply=%region_60.61 | all-reduce | flops 14336 | bytes 114688 | tf_op jit(solution)/shard_map/psum | solution.py:519
  1036.9 20.6 %scatter_custom_fusion.1 = f32[6304,256]{1,0:T(8,128)} fusion(s32[3072]{0:T(1024)} %bitcast.449, f32[3072,256]{1,0:T(8,128)} %bitcast.90, f32[]{:T(128)} %constant.123.clone.1), kind=kCustom, calls=%fused_computation.95 | custom fusion | flops 786432 | bytes 6455808 | tf_op jit(solution)/shard_map/scatter-add | solution.py:475
  1057.5 43.1 %reduce-scatter.8.cloned.1.call-done = f32[1,4608,256]{1,2,0:T(8,128)} async-done(((f32[4,4608,256]{1,2,0:T(8,128)}), f32[1,4608,256]{1,2,0:T(8,128)}) %reduce-scatter.8.cloned.1.call-update) | async-done | bytes 4718608 | tf_op jit(solution)/shard_map/reduce_scatter | solution.py:492
  1100.6 160.3 %all-reduce.8.cloned.1.call-done = f32[1024,1024]{0,1:T(8,128)} async-done(((f32[1024,1024]{0,1:T(8,128)}), f32[1024,1024]{0,1:T(8,128)}) %all-reduce.8.cloned.1.call-update) | async-done | bytes 4194320 | tf_op jit(solution)/shard_map/psum | solution.py:496
  1271.1 162.4 %all-reduce.10.cloned.1.call-done = f32[4608,256]{0,1:T(8,128)} async-done(((f32[4608,256]{0,1:T(8,128)}), f32[4608,256]{0,1:T(8,128)}) %all-reduce.10.cloned.1.call-update) | async-done | bytes 4718608 | tf_op jit(solution)/shard_map/psum | solution.py:498
  1441.8 39.3 %psum.39 = f32[]{:T(128)} all-reduce(f32[]{:T(128)S(6)} %add.624), channel_id=1, replica_groups=mesh['dp'=8,'tensor'=4] {'dp','tensor'}, use_global_device_ids=true, to_apply=%region_68.69 | all-reduce | flops 1 | bytes 8 | tf_op jit(solution)/shard_map/psum | solution.py:547
  1484.2 14.2 multiply_add_fusion
  1528.6 13.1 multiply_subtract_fusion.1
  (470 shorter events, 351.9 us)
Async XLA Ops:
  7.2 59.1 %all-gather.16.cloned.1.call-start = ((), (), s32[]{:S(2)}) async-start(), calls=%async_computation.19 | async-start | bytes 2662400 | tf_op jit(solution)/shard_map/all_gather | solution.py:320
  10.6 166.9 %all-gather.14.cloned.1.call-start = ((), (), s32[]{:S(2)}) async-start(), calls=%async_computation.18 | async-start | bytes 20971520 | tf_op jit(solution)/shard_map/all_gather | solution.py:316
  11.3 282.3 %all-gather.10.cloned.1.call-start = ((), (), s32[]{:S(2)}) async-start(), calls=%async_computation.10 | async-start | bytes 20971520 | tf_op jit(solution)/shard_map/all_gather | solution.py:317
  26.1 14.4 all-to-all-start.4
  55.8 74.7 %all-to-all-start.5 = ((f32[32,96,256]{2,1,0:T(8,128)}), f32[32,96,256]{2,1,0:T(8,128)S(1)}, u32[]{:S(2)}, u32[]{:S(2)}) async-start(f32[32,96,256]{2,1,0:T(8,128)} %bitcast.368), calls=%async_computation.5 | async-start | bytes 6291456 | tf_op jit(solution)/shard_map/all_to_all | solution.py:286
  58.6 334.9 %all-gather.12.cloned.1.call-start = ((), (), s32[]{:S(2)}) async-start(), calls=%async_computation.11 | async-start | bytes 20971520 | tf_op jit(solution)/shard_map/all_gather | solution.py:318
  59.2 688.3 %reduce-scatter.4.cloned.1.call-start = ((), (), s32[]{:S(2)}) async-start(), calls=%async_computation.12 | async-start | bytes 20971520 | tf_op jit(solution)/shard_map/reduce_scatter | solution.py:432
  61.9 184.1 %copy-start.122 = (pred[512]{0:T(512)(128)(4,1)}, pred[512]{0:T(512)(128)(4,1)S(1)}, u32[]{:S(2)}) copy-start(pred[512]{0:T(512)(128)(4,1)S(1)} %iota_compare_fusion.8) | copy-start | bytes 1540
  152.3 130.0 %copy-start.7 = (f32[768,1024]{1,0:T(8,128)}, f32[768,1024]{1,0:T(8,128)S(1)}, u32[]{:S(2)}) copy-start(f32[768,1024]{1,0:T(8,128)S(1)} %multiply_add_fusion.6) | copy-start | bytes 9437188
  153.4 55.9 %collective-permute-start = (f32[256,1024]{1,0:T(8,128)}, f32[256,1024]{1,0:T(8,128)}, u32[]{:S(2)}, u32[]{:S(2)}) collective-permute-start(f32[256,1024]{1,0:T(8,128)} %slice.211), channel_id=1, source_target_pairs={{0,1},{1,0},{2,3},{3,2},{4,5},{5,4},{6,7},{7,6},{8,9},{9,8},{10,11... | collective-permute-start | bytes 3145736 | tf_op jit(solution)/shard_map/ppermute | solution.py:366
  423.3 146.8 %copy-start.5 = (f32[768,1024]{1,0:T(8,128)}, f32[768,1024]{1,0:T(8,128)S(1)}, u32[]{:S(2)}) copy-start(f32[768,1024]{1,0:T(8,128)S(1)} %get-tuple-element.496) | copy-start | bytes 9437188
  423.4 146.7 %copy-start.74 = (f32[768]{0:T(1024)}, f32[768]{0:T(1024)S(1)}, u32[]{:S(2)}) copy-start(f32[768]{0:T(1024)S(1)} %broadcast_multiply_fusion.6) | copy-start | bytes 9220
  423.9 146.2 %copy-start.87 = (f32[768]{0:T(1024)}, f32[768]{0:T(1024)S(1)}, u32[]{:S(2)}) copy-start(f32[768]{0:T(1024)S(1)} %add_rsqrt_fusion) | copy-start | bytes 9220
  506.8 311.4 %reduce-scatter.6.cloned.1.call-start = ((), (), s32[]{:S(2)}) async-start(), calls=%async_computation.14 | async-start | bytes 20971520 | tf_op jit(solution)/shard_map/reduce_scatter | solution.py:435
  570.0 388.3 %all-reduce.6.cloned.1.call-start = ((), (), s32[]{:S(2)}) async-start(), calls=%async_computation.13 | async-start | bytes 8388608 | tf_op jit(solution)/shard_map/sum_ffn_down/psum | solution.py:494
  720.8 53.9 %collective-permute-start.1 = (f32[256,1024]{1,0:T(8,128)}, f32[256,1024]{1,0:T(8,128)}, u32[]{:S(2)}, u32[]{:S(2)}) collective-permute-start(f32[256,1024]{1,0:T(8,128)} %slice.233), channel_id=1, source_target_pairs={{0,1},{1,0},{2,3},{3,2},{4,5},{5,4},{6,7},{7,6},{8,9},{9,8},{10,11... | collective-permute-start | bytes 3145736 | tf_op jit(solution)/shard_map/ppermute | solution.py:461
  747.5 353.1 %reduce-scatter.8.cloned.1.call-start = ((), (), s32[]{:S(2)}) async-start(), calls=%async_computation.16 | async-start | bytes 23592960 | tf_op jit(solution)/shard_map/reduce_scatter | solution.py:492
  814.6 222.3 %all-to-all-start.6 = ((f32[32,96,256]{2,1,0:T(8,128)}), f32[32,96,256]{2,1,0:T(8,128)}, u32[]{:S(2)}, u32[]{:S(2)}) async-start(f32[32,96,256]{2,1,0:T(8,128)} %bitcast.89), calls=%async_computation.6 | async-start | bytes 6291456 | tf_op jit(solution)/shard_map/all_to_all | solution.py:286
  818.1 442.7 %all-reduce.8.cloned.1.call-start = ((), (), s32[]{:S(2)}) async-start(), calls=%async_computation.15 | async-start | bytes 8388608 | tf_op jit(solution)/shard_map/psum | solution.py:496
  958.3 475.2 %all-reduce.10.cloned.1.call-start = ((), (), s32[]{:S(2)}) async-start(), calls=%async_computation.17 | async-start | bytes 9437184 | tf_op jit(solution)/shard_map/psum | solution.py:498
  1057.5 203.4 %copy-start.57 = (s32[768]{0:T(1024)S(1)}, s32[768]{0:T(1024)}, u32[]{:S(2)}) copy-start(s32[768]{0:T(1024)} %copy-done.56) | copy-start | bytes 9220
  1057.5 203.4 %copy-start.61 = (s32[768]{0:T(1024)S(1)}, s32[768]{0:T(1024)}, u32[]{:S(2)}) copy-start(s32[768]{0:T(1024)} %copy-done.60) | copy-start | bytes 9220
  1271.0 170.5 %copy-start.62 = (f32[514,256]{1,0:T(8,128)S(1)}, f32[514,256]{1,0:T(8,128)}, u32[]{:S(2)}) copy-start(f32[514,256]{1,0:T(8,128)} %param.41) | copy-start | bytes 1579012
  1271.0 210.7 %copy-start.115 = (f32[256]{0:T(256)S(1)}, f32[256]{0:T(256)}, u32[]{:S(2)}) copy-start(f32[256]{0:T(256)} %param.39) | copy-start | bytes 3076
  1271.0 210.8 %copy-start.116 = (f32[256]{0:T(256)S(1)}, f32[256]{0:T(256)}, u32[]{:S(2)}) copy-start(f32[256]{0:T(256)} %get-tuple-element.521) | copy-start | bytes 3076
  1271.0 210.8 %copy-start.128 = (f32[256]{0:T(256)S(1)}, f32[256]{0:T(256)}, u32[]{:S(2)}) copy-start(f32[256]{0:T(256)} %param.49) | copy-start | bytes 3076
  1271.0 211.3 %copy-start.73 = (f32[8,1024]{1,0:T(8,128)S(1)}, f32[8,1024]{1,0:T(8,128)}, u32[]{:S(2)}) copy-start(f32[8,1024]{1,0:T(8,128)} %param.36) | copy-start | bytes 98308
  1271.0 211.3 %copy-start.96 = (f32[8,1024]{1,0:T(8,128)S(1)}, f32[8,1024]{1,0:T(8,128)}, u32[]{:S(2)}) copy-start(f32[8,1024]{1,0:T(8,128)} %param.46) | copy-start | bytes 98308
  1271.0 212.0 %copy-start.111 = (f32[1024]{0:T(1024)S(1)}, f32[1024]{0:T(1024)}, u32[]{:S(2)}) copy-start(f32[1024]{0:T(1024)} %param.35) | copy-start | bytes 12292
  1271.1 212.0 %copy-start.121 = (f32[1024]{0:T(1024)S(1)}, f32[1024]{0:T(1024)}, u32[]{:S(2)}) copy-start(f32[1024]{0:T(1024)} %param.45) | copy-start | bytes 12292
  1271.1 212.6 %copy-start.112 = (f32[2,256]{1,0:T(2,128)S(1)}, f32[2,256]{1,0:T(2,128)}, u32[]{:S(2)}) copy-start(f32[2,256]{1,0:T(2,128)} %param.34) | copy-start | bytes 6148
  1271.1 212.5 %copy-start.127 = (f32[2,256]{1,0:T(2,128)S(1)}, f32[2,256]{1,0:T(2,128)}, u32[]{:S(2)}) copy-start(f32[2,256]{1,0:T(2,128)} %param.44) | copy-start | bytes 6148
  (120 other events, 1863.6 us)
Sparse Core Ops, SparseCore 0:
  10.7 25.4 all-gather.15
  37.7 139.6 all-gather.13
  179.6 105.9 all-gather.9
  287.5 105.9 all-gather.11
  506.9 122.2 reduce-scatter.3
  631.8 126.1 reduce-scatter.5
  761.7 196.4 all-reduce.5
  960.9 139.6 reduce-scatter.7
  1104.7 156.0 all-reduce.7
  1264.8 168.6 all-reduce.9

commit v2 on v1

--- a/solution.py
+++ b/solution.py
@@ -4,6 +4,8 @@
 import jax
 import jax.numpy as jnp
 from jax import lax
+from jax.experimental import pallas as pl
+from jax.experimental.pallas import tpu as pltpu
 from jax.sharding import PartitionSpec as P
 
 HEAD_DIM = 64
@@ -17,7 +19,7 @@
 CLIP_SCALE = 1e-06
 HIGH = lax.Precision.HIGHEST
 PRODUCT = lax.Precision.HIGH
-CAPACITY = 96
+CAPACITY = 88
 
 
 def precise_product(left, right):
@@ -236,6 +238,392 @@
     )
 
 
+MESH = pl.DeviceIdType.MESH
+VMEM = pl.BlockSpec(memory_space=pltpu.VMEM)
+
+
+def cube_partners(groups, shards):
+    dp, tp = lax.axis_index("dp"), lax.axis_index("tensor")
+    partners = []
+    for size, at in ((shards, 1), (groups, 0)):
+        bit = 1
+        while bit < size:
+            here = (dp, tp)[at]
+            there = here + bit * (1 - 2 * ((here // bit) % 2))
+            partners.append((dp, there) if at else (there, tp))
+            bit *= 2
+    return partners
+
+
+def greet(partners):
+    barrier = pltpu.get_barrier_semaphore()
+    for partner in partners:
+        pl.semaphore_signal(barrier, inc=1, device_id=partner, device_id_type=MESH)
+    pl.semaphore_wait(barrier, len(partners))
+
+
+def cube_sum_kernel(groups, shards, x_ref, o_ref, sent, landed, send_sem, recv_sem):
+    partners = cube_partners(groups, shards)
+    greet(partners)
+    sent[0] = x_ref[...]
+    for stage, partner in enumerate(partners):
+        copy = pltpu.make_async_remote_copy(
+            src_ref=sent.at[stage],
+            dst_ref=landed.at[stage],
+            send_sem=send_sem.at[stage],
+            recv_sem=recv_sem.at[stage],
+            device_id=partner,
+            device_id_type=MESH,
+        )
+        copy.start()
+        copy.wait()
+        sent[stage + 1] = sent[stage] + landed[stage]
+    o_ref[...] = sent[len(partners)]
+
+
+def cube_stages(groups, shards):
+    return (groups * shards).bit_length() - 1
+
+
+def cube_sum(block, groups, shards, collective_id):
+    stages = cube_stages(groups, shards)
+    return pl.pallas_call(
+        functools.partial(cube_sum_kernel, groups, shards),
+        out_shape=jax.ShapeDtypeStruct(block.shape, block.dtype),
+        in_specs=[VMEM],
+        out_specs=VMEM,
+        scratch_shapes=[
+            pltpu.VMEM((stages + 1, *block.shape), block.dtype),
+            pltpu.VMEM((stages, *block.shape), block.dtype),
+            pltpu.SemaphoreType.DMA((stages,)),
+            pltpu.SemaphoreType.DMA((stages,)),
+        ],
+        compiler_params=pltpu.CompilerParams(collective_id=collective_id, has_side_effects=True),
+    )(block)
+
+
+def cube_gather_kernel(groups, shards, x_ref, o_ref, held, send_sem, recv_sem):
+    partners = cube_partners(groups, shards)
+    greet(partners)
+    me = lax.axis_index("dp") * shards + lax.axis_index("tensor")
+    held[pl.ds(me, 1)] = x_ref[...][None]
+    for stage, partner in enumerate(partners):
+        size = 1 << stage
+        mine = pl.ds((me // size) * size, size)
+        copy = pltpu.make_async_remote_copy(
+            src_ref=held.at[mine],
+            dst_ref=held.at[mine],
+            send_sem=send_sem.at[stage],
+            recv_sem=recv_sem.at[stage],
+            device_id=partner,
+            device_id_type=MESH,
+        )
+        copy.start()
+        copy.wait()
+    o_ref[...] = held[...]
+
+
+def cube_gather(block, groups, shards, collective_id):
+    stages = cube_stages(groups, shards)
+    shape = (groups * shards, *block.shape)
+    return pl.pallas_call(
+        functools.partial(cube_gather_kernel, groups, shards),
+        out_shape=jax.ShapeDtypeStruct(shape, block.dtype),
+        in_specs=[VMEM],
+        out_specs=VMEM,
+        scratch_shapes=[
+            pltpu.VMEM(shape, block.dtype),
+            pltpu.SemaphoreType.DMA((stages,)),
+            pltpu.SemaphoreType.DMA((stages,)),
+        ],
+        compiler_params=pltpu.CompilerParams(collective_id=collective_id, has_side_effects=True),
+    )(block)
+
+
+def ring_kernel(groups, parts, arrays, *refs):
+    inputs, outputs, slots = refs[:arrays], refs[arrays : 2 * arrays], refs[2 * arrays : 3 * arrays]
+    send_sem, recv_sem = refs[3 * arrays :]
+    depth = groups // 2
+    dp, tp = lax.axis_index("dp"), lax.axis_index("tensor")
+    side, level = dp % 2, dp // 2
+    place = level * (1 - side) + (groups - 1 - level) * side
+
+    def device_at(spot):
+        spot = (spot + groups) % groups
+        far = spot // depth
+        return (2 * (spot * (1 - far) + (groups - 1 - spot) * far) + far, tp)
+
+    greet([device_at(place + 1), device_at(place - 1)])
+    streams = []
+    for array in range(arrays):
+        rows = inputs[array].shape[1] // (2 * parts)
+        for part in range(2 * parts):
+            streams.append((array, 1 - 2 * (part % 2), pl.ds(part * rows, rows)))
+
+    def chunk(step, way):
+        return (place + groups * 2 - way * step) % groups
+
+    copies = []
+
+    def send(index, step, source, target):
+        copy = pltpu.make_async_remote_copy(
+            src_ref=source,
+            dst_ref=target,
+            send_sem=send_sem.at[index, step],
+            recv_sem=recv_sem.at[index, step],
+            device_id=device_at(place + streams[index][1]),
+            device_id_type=MESH,
+        )
+        copy.start()
+        copies.append(copy)
+        return copy
+
+    flying = [None] * len(streams)
+    for step in range(groups - 1):
+        for index, (array, way, rows) in enumerate(streams):
+            if step == 0:
+                source = inputs[array].at[chunk(0, way), rows]
+            else:
+                flying[index].wait_recv()
+                source = slots[array].at[step - 1, rows]
+                source[...] = source[...] + inputs[array][chunk(step, way), rows]
+            flying[index] = send(index, step, source, slots[array].at[step, rows])
+    for step in range(groups - 1):
+        for index, (array, way, rows) in enumerate(streams):
+            flying[index].wait_recv()
+            now = chunk(groups - 1 + step, way)
+            if step == 0:
+                outputs[array][now, rows] = slots[array][groups - 2, rows] + inputs[array][now, rows]
+            place_out = outputs[array].at[now, rows]
+            flying[index] = send(index, groups - 1 + step, place_out, place_out)
+    for copy in flying:
+        copy.wait_recv()
+    for copy in copies:
+        copy.wait_send()
+
+
+def ring_sum(arrays, groups, parts, collective_id):
+    blocks = [array.reshape(groups, array.shape[0] // groups, array.shape[1]) for array in arrays]
+    streams = 2 * parts * len(blocks)
+    steps = 2 * (groups - 1)
+    moved = sum(2 * block.size * 4 for block in blocks)
+    sums = pl.pallas_call(
+        functools.partial(ring_kernel, groups, parts, len(blocks)),
+        out_shape=[jax.ShapeDtypeStruct(block.shape, block.dtype) for block in blocks],
+        in_specs=[VMEM] * len(blocks),
+        out_specs=[VMEM] * len(blocks),
+        scratch_shapes=[
+            *[pltpu.VMEM((groups - 1, *block.shape[1:]), block.dtype) for block in blocks],
+            pltpu.SemaphoreType.DMA((streams, steps)),
+            pltpu.SemaphoreType.DMA((streams, steps)),
+        ],
+        compiler_params=pltpu.CompilerParams(
+            collective_id=collective_id, has_side_effects=True, vmem_limit_bytes=48 << 20
+        ),
+        cost_estimate=pl.CostEstimate(flops=moved, bytes_accessed=60 * moved, transcendentals=0),
+    )(*blocks)
+    return [total.reshape(array.shape) for total, array in zip(sums, arrays)]
+
+
+def spread_kernel(groups, w_ref, o_ref, local_sem, pair_send, pair_recv, ring_send, ring_recv, core_send, core_recv):
+    depth = groups // 2
+    dp, tp = lax.axis_index("dp"), lax.axis_index("tensor")
+    far = tp + 2 - 4 * (tp // 2)
+    core = (dp, tp + 1 - 2 * (tp % 2))
+    side, level = dp % 2, dp // 2
+    place = level * (1 - side) + (groups - 1 - level) * side
+
+    def index_at(spot):
+        spot = (spot + groups) % groups
+        back = spot // depth
+        return 2 * (spot * (1 - back) + (groups - 1 - spot) * back) + back
+
+    def send(source, target, send_sem, recv_sem, device):
+        copy = pltpu.make_async_remote_copy(
+            src_ref=source,
+            dst_ref=target,
+            send_sem=send_sem,
+            recv_sem=recv_sem,
+            device_id=device,
+            device_id_type=MESH,
+        )
+        copy.start()
+        return copy
+
+    greet([(index_at(place + 1), tp), (index_at(place - 1), tp), core, (dp, far)])
+    cross = send(w_ref.at[dp], o_ref.at[tp, dp], pair_send.at[0], pair_recv.at[0], (dp, far))
+    near = send(w_ref, o_ref.at[tp], pair_send.at[1], pair_recv.at[1], core)
+    local = pltpu.make_async_copy(w_ref, o_ref.at[tp], local_sem)
+    local.start()
+    cross.wait_recv()
+    lanes = ring_send.shape[0]
+    size = w_ref.shape[1] // lanes
+    flying = [None] * lanes
+    started = [cross]
+    handed = [near]
+    for step in range(groups):
+        for lane in range(lanes):
+            way = 1 - 2 * (lane % 2)
+            block = o_ref.at[far, index_at(place + groups - way * step), pl.ds(lane * size, size)]
+            if step > 0:
+                flying[lane].wait_recv()
+            if step < groups - 1:
+                flying[lane] = send(
+                    block, block, ring_send.at[lane, step], ring_recv.at[lane, step], (index_at(place + way), tp)
+                )
+                started.append(flying[lane])
+            handed.append(send(block, block, core_send.at[lane, step], core_recv.at[lane, step], core))
+    for copy in handed:
+        copy.wait_recv()
+        copy.wait_send()
+    for copy in started:
+        copy.wait_send()
+    local.wait()
+
+
+def spread(weight, groups, collective_id):
+    rows = weight.shape[0] // groups
+    lanes = 4
+    moved = 4 * weight.size
+    gathered = pl.pallas_call(
+        functools.partial(spread_kernel, groups),
+        out_shape=jax.ShapeDtypeStruct((4, groups, rows, weight.shape[1]), weight.dtype),
+        in_specs=[pl.BlockSpec(memory_space=pl.ANY)],
+        out_specs=VMEM,
+        scratch_shapes=[
+            pltpu.SemaphoreType.DMA,
+            pltpu.SemaphoreType.DMA((2,)),
+            pltpu.SemaphoreType.DMA((2,)),
+            pltpu.SemaphoreType.DMA((lanes, groups - 1)),
+            pltpu.SemaphoreType.DMA((lanes, groups - 1)),
+            pltpu.SemaphoreType.DMA((lanes, groups)),
+            pltpu.SemaphoreType.DMA((lanes, groups)),
+        ],
+        compiler_params=pltpu.CompilerParams(
+            collective_id=collective_id, has_side_effects=True, vmem_limit_bytes=32 << 20
+        ),
+        cost_estimate=pl.CostEstimate(flops=moved, bytes_accessed=30 * moved, transcendentals=0),
+    )(weight.reshape(groups, rows, weight.shape[1]))
+    return gathered.reshape(4, *weight.shape)
+
+
+def halves(array):
+    high = array.astype(jnp.bfloat16)
+    return high, (array - high.astype(jnp.float32)).astype(jnp.bfloat16)
+
+
+def dot_rows(left, right):
+    return lax.dot_general(left, right, (((1,), (1,)), ((), ())), preferred_element_type=jnp.float32)
+
+
+def dot_plain(left, right):
+    return lax.dot_general(left, right, (((1,), (0,)), ((), ())), preferred_element_type=jnp.float32)
+
+
+def one_head(array, head):
+    lane = lax.broadcasted_iota(jnp.int32, array.shape, 1)
+    return jnp.where(lane // HEAD_DIM == head, array, 0.0)
+
+
+def score_tile(twice_k, low_k, high_q, low_q, bias):
+    wide = dot_rows(twice_k, jnp.concatenate([high_q, low_q], axis=1))
+    return wide + dot_rows(low_k, high_q) + bias
+
+
+def attend_kernel(slots, tile, q_ref, k_ref, v_ref, bias_ref, o_ref, lse_ref):
+    scale = 1.0 / math.sqrt(HEAD_DIM)
+    high_k, low_k = halves(k_ref[0])
+    twice_k = jnp.concatenate([high_k, high_k], axis=1)
+    high_v, low_v = halves(v_ref[0].T)
+    for start in range(0, q_ref.shape[1], tile):
+        rows = pl.ds(start, tile)
+        first = 0 if start < slots else slots
+        keys = slice(first, first + slots)
+        found = []
+        for head in range(2):
+            high_q, low_q = halves(one_head(q_ref[0, rows] * scale, head))
+            scores = score_tile(twice_k[keys], low_k[keys], high_q, low_q, bias_ref[pl.ds(first, slots)])
+            peak = jnp.max(scores, axis=0, keepdims=True)
+            probs = jnp.exp(scores - peak)
+            total = jnp.sum(probs, axis=0, keepdims=True)
+            lse_ref[0, pl.ds(head, 1), rows] = peak + jnp.log(total)
+            high_p, low_p = halves(probs)
+            lanes = slice(head * HEAD_DIM, (head + 1) * HEAD_DIM)
+            both = jnp.concatenate([high_v[lanes, keys], low_v[lanes, keys]], axis=0)
+            wide = dot_plain(both, high_p)
+            mixed = wide[:HEAD_DIM] + wide[HEAD_DIM:] + dot_plain(high_v[lanes, keys], low_p)
+            found.append(mixed / total)
+        o_ref[0, rows] = jnp.concatenate(found, axis=0).T
+
+
+def attend_back_kernel(slots, tile, q_ref, k_ref, v_ref, bias_ref, o_ref, lse_ref, d_ref, dq_ref, dk_ref, dv_ref):
+    scale = 1.0 / math.sqrt(HEAD_DIM)
+    high_k, low_k = halves(k_ref[0])
+    twice_k = jnp.concatenate([high_k, high_k], axis=1)
+    high_v, low_v = halves(v_ref[0])
+    twice_v = jnp.concatenate([high_v, high_v], axis=1)
+    high_kt, low_kt = halves(k_ref[0].T)
+    ones = jnp.ones((8, 2 * HEAD_DIM), jnp.bfloat16)
+    lanes = 2 * HEAD_DIM
+    for first in (0, slots):
+        keys = slice(first, first + slots)
+        key_rows = pl.ds(first, slots)
+        for start in range(first, min(first + slots, q_ref.shape[1]), tile):
+            rows = pl.ds(start, tile)
+            back_qt = []
+            for head in range(2):
+                high_q, low_q = halves(one_head(q_ref[0, rows] * scale, head))
+                back = one_head(d_ref[0, rows], head)
+                high_d, low_d = halves(back)
+                scores = score_tile(twice_k[keys], low_k[keys], high_q, low_q, bias_ref[key_rows])
+                probs = jnp.exp(scores - lse_ref[0, pl.ds(head, 1), rows])
+                high_x, low_x = halves(back * o_ref[0, rows])
+                inner = (dot_rows(ones, high_x) + dot_rows(ones, low_x))[:1]
+                back_s = probs * (score_tile(twice_v[keys], low_v[keys], high_d, low_d, 0.0) - inner)
+                high_p, low_p = halves(probs)
+                high_s, low_s = halves(back_s)
+                wide = dot_plain(high_p, jnp.concatenate([high_d, low_d], axis=1))
+                back_v = wide[:, :lanes] + wide[:, lanes:] + dot_plain(low_p, high_d)
+                wide = dot_plain(high_s, jnp.concatenate([high_q, low_q], axis=1))
+                back_k = wide[:, :lanes] + wide[:, lanes:] + dot_plain(low_s, high_q)
+                if start == first and head == 0:
+                    dv_ref[0, key_rows] = back_v
+                    dk_ref[0, key_rows] = back_k
+                else:
+                    dv_ref[0, key_rows] += back_v
+                    dk_ref[0, key_rows] += back_k
+                mine = slice(head * HEAD_DIM, (head + 1) * HEAD_DIM)
+                both = jnp.concatenate([high_kt[mine, keys], low_kt[mine, keys]], axis=0)
+                wide = dot_plain(both, high_s)
+                back_qt.append(wide[:HEAD_DIM] + wide[HEAD_DIM:] + dot_plain(high_kt[mine, keys], low_s))
+            dq_ref[0, rows] = jnp.concatenate(back_qt, axis=0).T * scale
+
+
+def attend_call(kernel, slots, inputs, outputs):
+    lanes = 2 * HEAD_DIM
+    queries = inputs[0]
+    per_shard = queries.shape[2] // lanes
+    pairs = queries.shape[0] * per_shard
+
+    def spec(shape):
+        if shape[1] == 1:
+            return pl.BlockSpec(shape, lambda i: (0, 0))
+        if shape[1] == 2:
+            return pl.BlockSpec((1, *shape[1:]), lambda i: (i, 0, 0))
+        return pl.BlockSpec((1, shape[1], lanes), lambda i: (i // per_shard, 0, i % per_shard))
+
+    work = 7 * 2 * pairs * 2 * queries.shape[1] * slots * HEAD_DIM * 3
+    return pl.pallas_call(
+        functools.partial(kernel, slots, slots // 2),
+        grid=(pairs,),
+        in_specs=[spec(x.shape) for x in inputs],
+        out_specs=[spec(shape) for shape in outputs],
+        out_shape=[jax.ShapeDtypeStruct(shape, jnp.float32) for shape in outputs],
+        compiler_params=pltpu.CompilerParams(vmem_limit_bytes=48 << 20),
+        cost_estimate=pl.CostEstimate(flops=4 * work, bytes_accessed=20 << 20, transcendentals=0),
+    )(*inputs)
+
+
 def normalise(values):
     center = values - jnp.mean(values, axis=-1, keepdims=True)
     scale = lax.rsqrt(jnp.mean(center * center, axis=-1, keepdims=True) + EPS)
@@ -314,12 +702,19 @@
     split_length = lax.dynamic_index_in_dim(lengths, split_seq, 0, keepdims=False)
 
     all_attn = lax.all_gather(attn_weights, "tensor")
-    all_ffn_up = lax.all_gather(ffn_weights[0], "tensor")
     all_ffn_down = lax.all_gather(ffn_weights[1], "tensor")
     small = jnp.concatenate([positions[2 : slots + 2], bias_qv, bias_up.reshape(-1, cols)], axis=0)
-    all_small = lax.all_gather(small, "tensor")
+    swap = [(i, i ^ 1) for i in range(shards)]
+    swap_pair = [(i, i ^ 2) for i in range(shards)]
+    far_small = lax.ppermute(small, "tensor", swap_pair)
+    rows_small = jnp.stack([small, lax.ppermute(small, "tensor", swap), far_small, lax.ppermute(far_small, "tensor", swap)])
+    all_small = jnp.concatenate(
+        [
+            lax.dynamic_index_in_dim(rows_small, 2 * ((j // 2 + pair) % 2) + (j + side) % 2, 0)
+            for j in range(shards)
+        ]
+    )
     all_positions = all_small[:, :slots].transpose(1, 0, 2).reshape(slots, width)
-    all_bias_qv = all_small[:, slots : slots + 2].transpose(1, 0, 2).reshape(2, width)
     all_bias_up = all_small[:, slots + 2 :].reshape(-1)
 
     owner, rank = request_lists(ids, vocab_rows, groups)
@@ -330,21 +725,25 @@
         lists = jnp.broadcast_to(wanted.reshape(groups, 1, CAPACITY), (groups, shards, CAPACITY))
         lists = lists.reshape(devices, CAPACITY)
         tail = jnp.broadcast_to(rounds_here, (devices, 1)).astype(jnp.int32)
-        lists = jnp.concatenate([lists, tail, jnp.zeros((devices, 127 - CAPACITY % 128), jnp.int32)], axis=1)
+        lists = jnp.concatenate([lists, tail, jnp.zeros((devices, 127 - CAPACITY), jnp.int32)], axis=1)
         asked = trade(lists)
         rows = asked[:, :CAPACITY].reshape(-1) - base
         rounds = jnp.max(asked[:, CAPACITY])
         return wanted, rows, rounds
 
-    def fetch(wanted, rows):
-        found = jnp.take(embedding, rows, axis=0, mode="clip")
-        landed = trade(found).reshape(groups, shards, CAPACITY, cols)
+    def ask(rows):
+        return trade(jnp.take(embedding, rows, axis=0, mode="clip"))
+
+    def expand(wanted, landed):
+        landed = landed.reshape(groups, shards, CAPACITY, cols)
         landed = landed.transpose(0, 2, 1, 3).reshape(groups * CAPACITY, width)
         chosen = (ids[:, None] == wanted[None, :]).astype(jnp.float32)
         return jnp.matmul(chosen, landed, precision=HIGH)
 
     wanted_first, rows_first, rounds = serve(0)
-    tokens = fetch(wanted_first, rows_first)
+    landed, up_weights = lax.optimization_barrier((ask(rows_first), ffn_weights[0]))
+    all_ffn_up = spread(up_weights, groups, 6)
+    tokens = expand(wanted_first, landed)
 
     def more(state):
         return state[0] < rounds
@@ -352,7 +751,7 @@
     def fetch_more(state):
         round_index, total = state
         wanted, rows, _ = serve(round_index)
-        return round_index + 1, total + fetch(wanted, rows)
+        return round_index + 1, total + expand(wanted, ask(rows))
 
     _, tokens = lax.while_loop(more, fetch_more, (jnp.int32(1), tokens))
     own_positions = jnp.concatenate(
@@ -362,41 +761,30 @@
     unit_zero, scale_zero = normalise(embedded)
     h_zero = unit_zero * norms[0] + norms[1]
 
-    swap = [(i, i ^ 1) for i in range(shards)]
     h_other = lax.ppermute(h_zero[slots:], "tensor", swap)
     h_keys = jnp.concatenate([h_zero, h_other], axis=0)
-    queries = product("td,jdc->tjc", h_zero, all_attn[:, 0]).reshape(count, width) + all_bias_qv[0]
-    keys_all = product("td,jdc->tjc", h_keys, all_attn[:, 1]).reshape(count + half, width)
-    values = product("td,jdc->tjc", h_keys, all_attn[:, 2]).reshape(count + half, width) + all_bias_qv[1]
+    bias_q, bias_v = all_small[:, slots], all_small[:, slots + 1]
+    queries = product("td,jdc->jtc", h_zero, all_attn[:, 0]) + bias_q[:, None, :]
+    keys_all = product("td,jdc->jtc", h_keys, all_attn[:, 1])
+    values = product("td,jdc->jtc", h_keys, all_attn[:, 2]) + bias_v[:, None, :]
     key_index = lax.broadcasted_iota(jnp.int32, (slots,), 0)
     own_first = jnp.where(
         key_index < half, side * half + key_index, (1 - side) * half + key_index - half
     )
-    root = 1.0 / math.sqrt(HEAD_DIM)
-
-    def split_heads(array):
-        return array.reshape(-1, heads, HEAD_DIM)
-
-    def attend_block(q, k, v, valid):
-        scores = product("qhd,khd->hqk", q, k) * root
-        scores = jnp.where(valid[None, None, :], scores, -1e30)
-        probs = jnp.exp(scores - jnp.max(scores, axis=-1, keepdims=True))
-        probs = probs / jnp.sum(probs, axis=-1, keepdims=True)
-        return probs, product("hqk,khd->qhd", probs, v)
-
-    q_whole, q_split = split_heads(queries[:slots]), split_heads(queries[slots:])
-    k_whole, k_split = split_heads(keys_all[:slots]), split_heads(keys_all[slots:])
-    v_whole, v_split = split_heads(values[:slots]), split_heads(values[slots:])
-    p_whole, a_whole = attend_block(q_whole, k_whole, v_whole, key_index < whole_length)
-    p_split, a_split = attend_block(q_split, k_split, v_split, own_first < split_length)
-    mixed = jnp.concatenate([a_whole.reshape(slots, width), a_split.reshape(half, width)], axis=0)
-    mixed_parts = mixed.reshape(count, shards, cols)
-    x_one = h_zero + product("tjc,jdc->td", mixed_parts, all_attn[:, 3]) + norms[6]
+    counted = jnp.concatenate([key_index < whole_length, own_first < split_length])
+    key_bias = jnp.where(counted, 0.0, -1e30).astype(jnp.float32)[:, None]
+    mixed, lse = attend_call(
+        attend_kernel,
+        slots,
+        (queries, keys_all, values, key_bias),
+        (queries.shape, (heads // 2, 2, count)),
+    )
+    x_one = h_zero + product("jtc,jdc->td", mixed, all_attn[:, 3]) + norms[6]
     unit_one, scale_one = normalise(x_one)
     h_one = unit_one * norms[2] + norms[3]
 
     up = product("td,jdc->tjc", h_one, all_ffn_up) + all_bias_up.reshape(shards, hidden)
-    act, act_slope = gelu_both(up)
+    act, act_slope = lax.optimization_barrier(gelu_both(up))
     x_two = h_one + product("tjc,jdc->td", act, all_ffn_down) + norms[7]
     unit_two, scale_two = normalise(x_two)
     h_two = unit_two * norms[4] + norms[5]
@@ -410,7 +798,7 @@
     sums = jnp.stack(
         [jnp.sum(h_two * weight_whole[:, None], axis=0), jnp.sum(h_two * weight_split[:, None], axis=0)]
     )
-    all_sums = lax.all_gather(sums, ("dp", "tensor")).reshape(groups * shards // 2, 2, 2, width)
+    all_sums = cube_gather(sums.reshape(-1, 128), groups, shards, 5).reshape(groups * shards // 2, 2, 2, width)
     all_pooled = jnp.stack(
         [all_sums[:, 0, 0], all_sums[:, 0, 1] + all_sums[:, 1, 1], all_sums[:, 1, 0]], axis=1
     ).reshape(groups * seqs, width)
@@ -430,72 +818,43 @@
     back_x_two, grad_gain_two, grad_shift_two = normalise_back(back_h_two, norms[4], unit_two, scale_two)
     grad_down = product("td,tjc->jdc", back_x_two, act)
     sum_down = lax.psum_scatter(grad_down, "tensor", scatter_dimension=0, tiled=False)
-    back_up = product("td,jdc->tjc", back_x_two, all_ffn_down) * act_slope
-    grad_up = product("td,tjc->jdc", h_one, back_up)
+    back_up = product("td,jdc->jtc", back_x_two, all_ffn_down) * act_slope.transpose(1, 0, 2)
+    grad_up = product("td,jtc->jdc", h_one, back_up)
+    back_up, grad_up = lax.optimization_barrier((back_up, grad_up))
     sum_up = lax.psum_scatter(grad_up, "tensor", scatter_dimension=0, tiled=False)
-    grad_bias_up = jnp.sum(back_up, axis=0)
-    back_h_one = back_x_two + product("tjc,jdc->td", back_up, all_ffn_up)
+    grad_bias_up = jnp.sum(back_up, axis=1)
+    back_h_one = back_x_two + product("jtc,jdc->td", back_up, all_ffn_up)
     back_x_one, grad_gain_one, grad_shift_one = normalise_back(back_h_one, norms[2], unit_one, scale_one)
 
-    back_mixed_parts = product("td,jdc->tjc", back_x_one, all_attn[:, 3])
-    grad_out = product("td,tjc->jdc", back_x_one, mixed_parts)
-    back_mixed = back_mixed_parts.reshape(count, width)
-
-    def attend_back(q, k, v, probs, mixed_block, back):
-        back_v = product("hqk,qhd->khd", probs, back)
-        back_p = product("qhd,khd->hqk", back, v)
-        inner = jnp.sum(back * mixed_block, axis=-1).T
-        back_s = probs * (back_p - inner[:, :, None]) * root
-        return product("hqk,khd->qhd", back_s, k), product("hqk,qhd->khd", back_s, q), back_v
-
-    dq_whole, dk_whole, dv_whole = attend_back(
-        q_whole, k_whole, v_whole, p_whole, a_whole, split_heads(back_mixed[:slots])
-    )
-    dq_split, dk_split, dv_split = attend_back(
-        q_split, k_split, v_split, p_split, a_split, split_heads(back_mixed[slots:])
-    )
-    back_q = jnp.concatenate([dq_whole, dq_split], axis=0).reshape(count, shards, cols)
-    back_k = jnp.concatenate([dk_whole, dk_split], axis=0).reshape(count + half, shards, cols)
-    back_v = jnp.concatenate([dv_whole, dv_split], axis=0).reshape(count + half, shards, cols)
-    back_keys = product("tjc,jdc->td", back_k, all_attn[:, 1]) + product("tjc,jdc->td", back_v, all_attn[:, 2])
+    back_mixed = product("td,jdc->jtc", back_x_one, all_attn[:, 3])
+    grad_out = product("td,jtc->jdc", back_x_one, mixed)
+    back_q, back_k, back_v = attend_call(
+        attend_back_kernel,
+        slots,
+        (queries, keys_all, values, key_bias, mixed, lse, back_mixed),
+        (queries.shape, keys_all.shape, values.shape),
+    )
+    back_keys = product("jtc,jdc->td", back_k, all_attn[:, 1]) + product("jtc,jdc->td", back_v, all_attn[:, 2])
     back_other = lax.ppermute(back_keys[count:], "tensor", swap)
-    grad_q = product("td,tjc->jdc", h_zero, back_q)
-    grad_k = product("td,tjc->jdc", h_keys, back_k)
-    grad_v = product("td,tjc->jdc", h_keys, back_v)
-    back_h_zero = back_x_one + product("tjc,jdc->td", back_q, all_attn[:, 0]) + back_keys[:count]
+    grad_q = product("td,jtc->jdc", h_zero, back_q)
+    grad_k = product("td,jtc->jdc", h_keys, back_k)
+    grad_v = product("td,jtc->jdc", h_keys, back_v)
+    back_h_zero = back_x_one + product("jtc,jdc->td", back_q, all_attn[:, 0]) + back_keys[:count]
     back_h_zero = back_h_zero + jnp.pad(back_other, ((slots, 0), (0, 0)))
     back_embedded, grad_gain_zero, grad_shift_zero = normalise_back(back_h_zero, norms[0], unit_zero, scale_zero)
 
-    def give_back(wanted, rows, listed, total):
+    def send_back(wanted):
         chosen = (wanted[:, None] == ids[None, :]).astype(jnp.float32)
         summed = jnp.matmul(chosen, back_embedded, precision=HIGH)
         parts = summed.reshape(groups, CAPACITY, shards, cols).transpose(0, 2, 1, 3)
-        landed = trade(parts.reshape(devices * CAPACITY, cols))
+        return trade(parts.reshape(devices * CAPACITY, cols))
+
+    def add_rows(landed, rows, total):
         target = jnp.where(rows >= 0, rows, vocab_rows)
         return total.at[target].add(landed, mode="drop")
 
-    zero_table = jnp.zeros((vocab_rows, cols), jnp.float32)
-    grad_embedding = give_back(wanted_first, rows_first, None, zero_table)
-
-    def give_more(state):
-        round_index, total = state
-        wanted, rows, _ = serve(round_index)
-        return round_index + 1, give_back(wanted, rows, None, total)
-
-    _, grad_embedding = lax.while_loop(more, give_more, (jnp.int32(1), grad_embedding))
-
-    half_rows = jnp.where(side == 0, 1.0, 0.0) * back_embedded[slots:]
-    other_rows = back_embedded[slots:] - half_rows
-    grad_pos_full = back_embedded[:slots] + jnp.concatenate([half_rows, other_rows], axis=0)
-    grad_pos_parts = grad_pos_full.reshape(slots, shards, cols).transpose(1, 0, 2)
-    grad_attn_parts = jnp.concatenate([grad_q, grad_k, grad_v, grad_out, grad_pos_parts], axis=1)
-    sum_attn = lax.psum_scatter(grad_attn_parts, "tensor", scatter_dimension=0, tiled=False)
-    with jax.named_scope("sum_ffn_down"):
-        sum_down = lax.psum(sum_down, "dp")
-    sum_down, sum_up = lax.optimization_barrier((sum_down, sum_up))
-    sum_up = lax.psum(sum_up, "dp")
-    sum_up, sum_attn = lax.optimization_barrier((sum_up, sum_attn))
-    sum_attn = lax.psum(sum_attn, "dp")
+    landed_first = send_back(wanted_first)
+
     grad_small = jnp.concatenate(
         [
             jnp.stack(
@@ -508,21 +867,45 @@
                     grad_shift_two,
                     jnp.sum(back_x_one, axis=0),
                     jnp.sum(back_x_two, axis=0),
-                    jnp.sum(back_q, axis=0).reshape(-1),
-                    jnp.sum(back_v, axis=0).reshape(-1),
+                    jnp.sum(back_q, axis=1).reshape(-1),
+                    jnp.sum(back_v, axis=1).reshape(-1),
                 ]
             ),
             grad_bias_up.reshape(-1, width),
         ],
         axis=0,
     )
-    sum_small = lax.psum(grad_small, ("dp", "tensor"))
+    half_rows = jnp.where(side == 0, 1.0, 0.0) * back_embedded[slots:]
+    other_rows = back_embedded[slots:] - half_rows
+    grad_pos_full = back_embedded[:slots] + jnp.concatenate([half_rows, other_rows], axis=0)
+    grad_pos_parts = grad_pos_full.reshape(slots, shards, cols)
+    grad_pos_parts = grad_pos_parts.transpose(1, 0, 2)
+    small_size = grad_small.size
+    small_rows = jnp.pad(grad_small.reshape(-1), (0, 256 * cols - small_size)).reshape(1, 256, cols)
+    small_rows = jnp.broadcast_to(small_rows, (shards, 256, cols))
+    parts_attn = jnp.concatenate([grad_q, grad_k, grad_v, grad_out, grad_pos_parts, small_rows], axis=1)
+    sum_attn = lax.psum_scatter(parts_attn, "tensor", scatter_dimension=0, tiled=False)
+    sum_down, sum_up = ring_sum([sum_down, sum_up], groups, 2, 1)
+    landed_first, sum_up = lax.optimization_barrier((landed_first, sum_up))
+    zero_table = jnp.zeros((vocab_rows, cols), jnp.float32)
+    grad_embedding = add_rows(landed_first, rows_first, zero_table)
+
+    def give_more(state):
+        round_index, total = state
+        wanted, rows, _ = serve(round_index)
+        return round_index + 1, add_rows(send_back(wanted), rows, total)
+
+    _, grad_embedding = lax.while_loop(more, give_more, (jnp.int32(1), grad_embedding))
+
+    sum_attn, grad_embedding = lax.optimization_barrier((sum_attn, grad_embedding))
+    (sum_attn,) = ring_sum([sum_attn], groups, 2, 2)
+    sum_small = sum_attn[-256:].reshape(-1)[:small_size].reshape(grad_small.shape)
     grad_norms = sum_small[:8]
     grad_bias_qv = lax.dynamic_slice_in_dim(sum_small[8:10], tp_rank * cols, cols, 1)
     grad_bias_up = lax.dynamic_slice_in_dim(sum_small[10:].reshape(-1), tp_rank * hidden, hidden)
     grad_attn = sum_attn[: 4 * width].reshape(4, width, cols)
     grad_ffn_up, grad_ffn_down = sum_up, sum_down
-    grad_pos = sum_attn[4 * width :]
+    grad_pos = sum_attn[4 * width : -256]
 
     first_dp = (dp_rank == 0).astype(jnp.float32)
     first_all = first_dp * (tp_rank == 0).astype(jnp.float32)
@@ -530,7 +913,7 @@
         squares(grad_embedding)
         + first_dp
         * (
-            squares(sum_attn)
+            squares(sum_attn[:-256])
             + squares(grad_ffn_up)
             + squares(grad_ffn_down)
             + squares(grad_bias_qv)
@@ -544,7 +927,8 @@
             + squares(grad_head_bias)
         )
     )
-    grad_norm = jnp.sqrt(lax.psum(local_squares, ("dp", "tensor")))
+    total_squares = cube_sum(jnp.broadcast_to(local_squares, (8, 128)), groups, shards, 4)[0, 0]
+    grad_norm = jnp.sqrt(total_squares)
     factor = jnp.minimum(1.0, CLIP_SCALE * math.sqrt(PARAMS) / (grad_norm + 1e-06))
     grad_positions = jnp.pad(grad_pos, ((2, positions.shape[0] - slots - 2), (0, 0)))
     grad_ffn = jnp.stack([grad_ffn_up, grad_ffn_down])

time: 1570 us -> 1110 us (0.71)
  waiting for transfers between devices: 670 us -> 56.7 us
  Pallas kernels: 0 us -> 486 us
  matrix products: 440 us -> 312 us
  blocking collectives: 119 us -> 0 us
  local copies, waits for them, and re-layouts: 157 us -> 84 us
    pallas_call x0 -> x7, Pallas kernels: none -> 486 us  [the longest x2 311 us: ring_sum(): pl.pallas_call(functools.partial(ring_kernel, groups, parts, len(blocks))...]
    psum x3 -> x0, waiting for transfers between devices: 463 us -> none  [the longest x1 162 us: fast_on_device(): sum_attn = lax.psum(sum_attn, 'dp')]
    dot_general x30 -> x18, matrix products: 416 us -> 288 us  [product(): return jnp.einsum(subscripts, left, right, precision=PRODUCT)]
    psum x2 -> x0, blocking collectives: 77.4 us -> none  [the longest x1 39.3 us: fast_on_device(): grad_norm = jnp.sqrt(lax.psum(local_squares, ('dp', 'tensor')))]
    all_gather x1, waiting for transfers between devices: 72.8 us -> 0.01 us  [fast_on_device(): all_ffn_down = lax.all_gather(ffn_weights[1], 'tensor')]
    all_to_all x3, waiting for transfers between devices: 66 us -> 7.08 us  [trade(): return lax.all_to_all(block, ('dp', 'tensor'), 0, 0, tiled=True)]
    ppermute x0 -> x3, waiting for transfers between devices: none -> 48.9 us  [the longest x1 48.5 us: fast_on_device(): far_small = lax.ppermute(small, 'tensor', swap_pair)]
    reduce_scatter x1, waiting for transfers between devices: 43.1 us -> 0.02 us  [fast_on_device(): lax.psum_scatter(parts_attn, 'tensor', scatter_dimension=0, tiled=False)]
  transfers between devices with their start and end apart: 15 -> 13, of which waited for: 8 -> 3; matrix products, arithmetic and copies ran while one was open for 35% -> 33% of each run, Pallas kernels for 0% -> 31%
where the time goes in v2:
time: 1110 us; the launch traced here: 1100 us
  Pallas kernels  486 us (44%)
  matrix products  312 us (28%)
  other arithmetic  115 us (10%)
  local copies, waits for them, and re-layouts  84 us (8%)
  waiting for transfers between devices  56.7 us (5%)
  between operations  27.6 us (2%)
  starting transfers between devices  16.7 us (2%)
    pallas_call x2, Pallas kernels, ring_sum(): pl.pallas_call(functools.partial(ring_kernel, groups, parts, len(blocks))...  311 us
    dot_general x18, matrix products, product(): return jnp.einsum(subscripts, left, right, precision=PRODUCT)  288 us
    pallas_call x2, Pallas kernels, attend_call(): pl.pallas_call(functools.partial(kernel, slots, slots // 2), grid=(pairs,...  70.3 us
    pallas_call x1, Pallas kernels, spread(): pl.pallas_call(functools.partial(spread_kernel, groups), out_shape=jax.Sh...  69.4 us
    ppermute x1, waiting for transfers between devices, fast_on_device(): far_small = lax.ppermute(small, 'tensor', swap_pair)  48.5 us
    sub x10, other arithmetic, advance(): weight - RATE * (DECAY * moment_new + (1.0 - DECAY) * clipped)  38.8 us
    unnamed x207, local copies, waits for them, and re-layouts  25.7 us
  transfers between devices with their start and end apart: 13, of which 3 were waited for; matrix products, arithmetic and copies ran while one was open for 33% of the time, Pallas kernels for 31%

profile of v2, /device:TPU:0, one launch (start us, length us, event | category | flops | bytes accessed | tf_op | source)
XLA Modules:
  0.0 1099.4 jit_solution(4827208206611726913)
XLA Ops:
  14.1 7.3 all-to-all-start.4
  28.6 11.0 %gather_fusion.1 = f32[2816,256]{1,0:T(8,128)} fusion(f32[6304,256]{1,0:T(8,128)} %param.30, s32[3072]{0:T(1024)S(1)} %pad_clamp_fusion.1), kind=kCustom, calls=%fused_computation.1 | custom fusion | bytes 5778432 | tf_op jit(solution)/shard_map/jit(_take)/gather | solution.py:735
  42.4 8.5 fusion.118
  54.6 48.5 %collective-permute-done.1 = f32[518,256]{1,0:T(8,128)} collective-permute-done((f32[518,256]{1,0:T(8,128)}, f32[518,256]{1,0:T(8,128)}, u32[]{:S(2)}, u32[]{:S(2)}) %collective-permute-start.1) | collective-permute-done | bytes 530464 | tf_op jit(solution)/shard_map/ppermute | solution.py:709
  131.7 69.4 %shard_map.391 = f32[4,8,128,1024]{3,2,1,0:T(8,128)S(1)} custom-call(f32[8,128,1024]{2,1,0:T(8,128)S(1)} %bitcast.309), custom_call_target="tpu_custom_call" | custom-call | flops 4194304 | bytes 125829120 | tf_op jit(solution)/shard_map/pallas_call | solution.py:488
  207.0 11.2 %fusion.58.k_ref = f32[4,1024,256]{2,1,0:T(8,128)} fusion(f32[4,4,1024,256]{3,2,1,0:T(8,128)} %bitcast.329, f32[256,1024]{1,0:T(8,128)} %collective-permute-done.3, f32[768,1024]{1,0:T(8,128)} %copy-done.15), kind=kOutput, calls=%fused_computation.138 | convolution fusion | flops 6443499520 | bytes 12582912 | tf_op jit(solution)/shard_map/td,jdc->jtc/dot_general | solution.py:650
  225.2 9.0 add_bitcast_fusion.v_ref
  234.2 33.3 %shard_map.390 = (f32[4,768,256]{2,1,0:T(8,128)S(1)}, f32[8,2,768]{2,1,0:T(2,128)S(1)}) custom-call(f32[4,768,256]{2,1,0:T(8,128)} %add_bitcast_fusion.1.q_ref, f32[4,1024,256]{2,1,0:T(8,128)} %fusion.58.k_ref, f32[4,1024,256]{2,1,0:T(8,128)} %add_bitcast_fusion.v_ref, f32[1024,1]{1,0:T(8,128)S(1)} %broadcast_select_fusion.bias_ref), custom_call_target="tpu_custom_call" | custom-call | flops 67645734912 | bytes 20971520 | tf_op jit(solution)/shard_map/pallas_call | solution.py:616
  267.5 9.3 fusion.121
  277.6 28.9 %fusion.15 = (f32[768,4,1024]{2,0,1:T(8,128)}, f32[768,4,1024]{2,0,1:T(8,128)}) fusion(f32[4,1024]{1,0:T(4,128)S(1)} %bitcast.392, f32[4,1024,1024]{2,1,0:T(8,128)} %bitcast.307, f32[1024]{0:T(1024)S(1)} %bitcast.395, f32[1024]{0:T(1024)S(1)} %bitcast.372, f32[768]{0:T(1024)S(1)} %add_rsqrt_fusion.1, f32[768,1024]{1,0:T(8,128)S(1)} %get-tuple-element.408, ...), kind=kOutput, calls=%fused_computation.35 | convolution fusion | flops 19361955840 | bytes 45119488 | tf_op jit(solution)/shard_map/td,jdc->tjc/dot_general | solution.py:650
  306.5 29.7 %fusion.122 = (f32[768]{0:T(1024)S(1)}, f32[768,1024]{1,0:T(8,128)S(1)}) fusion(f32[1024]{0:T(1024)S(1)} %bitcast.398, f32[768,4,1024]{2,0,1:T(8,128)} %get-tuple-element.276, f32[4,1024,1024]{2,1,0:T(8,128)} %all-gather.4.cloned.1.call-done, f32[1024]{0:T(1024)S(1)} %bitcast.396, f32[1024]{0:T(1024)S(1)} %bitcast.373, f32[768]{0:T(1024)S(1)} %add_rsqrt_fusion.1, ...), kind=kOutput, calls=%fused_computation.316 | convolution fusion | flops 19332857856 | bytes 35673088 | tf_op jit(solution)/shard_map/tjc,jdc->td/dot_general | solution.py:650
  338.6 20.1 %shard_map.392 = f32[32,16,128]{2,1,0:T(8,128)} custom-call(f32[16,128]{1,0:T(8,128)} %reshape.652.x_ref), custom_call_target="tpu_custom_call" | custom-call | tf_op jit(solution)/shard_map/pallas_call | solution.py:329
  372.7 27.9 %convolution_bitcast_fusion = f32[4,1024,1024]{1,2,0:T(8,128)} fusion(f32[768,4,1024]{2,0,1:T(8,128)} %get-tuple-element.276, f32[768,1024]{1,0:T(8,128)S(1)} %get-tuple-element.410, f32[768]{0:T(1024)S(1)} %broadcast_multiply_fusion.4, f32[768]{0:T(1024)S(1)} %broadcast_multiply_fusion.5, f32[1024]{0:T(1024)S(1)} %bitcast.364, f32[1024]{0:T(1024)S(1)} %bitcast.359, ...), kind=kOutput, calls=%fused_computation.39 | convolution fusion | flops 19335217152 | bytes 32536576 | tf_op jit(solution)/shard_map/td,tjc->jdc/dot_general | solution.py:650
  400.7 31.4 %multiply_bitcast_fusion = f32[4,768,1024]{2,1,0:T(8,128)S(1)} fusion(f32[768,4,1024]{2,0,1:T(8,128)} %get-tuple-element.277, f32[4,1024,1024]{2,1,0:T(8,128)} %all-gather.4.cloned.1.call-done, f32[768,1024]{1,0:T(8,128)S(1)} %get-tuple-element.410, f32[768]{0:T(1024)S(1)} %broadcast_multiply_fusion.4, f32[768]{0:T(1024)S(1)} %broadcast_multiply_fusion.5, ...), kind=kOutput, calls=%fused_computation.36 | convolution fusion | flops 19338362880 | bytes 45119488 | tf_op jit(solution)/shard_map/td,jdc->jtc/dot_general | solution.py:650
  436.7 24.6 %convolution_bitcast_fusion.1 = f32[4,1024,1024]{1,2,0:T(8,128)} fusion(f32[4,768,1024]{2,1,0:T(8,128)S(1)} %multiply_bitcast_fusion, f32[1024]{0:T(1024)S(1)} %bitcast.397, f32[1024]{0:T(1024)S(1)} %bitcast.374, f32[768,1024]{1,0:T(8,128)S(1)} %copy-done.21, f32[768]{0:T(1024)S(1)} %add_rsqrt_fusion.1, f32[768]{0:T(1024)S(1)} %broadcast_multiply_fusion.7), kind=kOutput, calls=%fused_computation.40 | convolution fusion | flops 19330498560 | bytes 32520192 | tf_op jit(solution)/shard_map/td,jtc->jdc/dot_general | solution.py:650
  467.3 30.7 %multiply_reduce_fusion.4 = (f32[1024]{0:T(1024)S(1)}, f32[768]{0:T(1024)S(1)}, f32[768]{0:T(1024)S(1)}, f32[1024]{0:T(1024)S(1)}, f32[768,1024]{1,0:T(8,128)S(1)}) fusion(f32[768]{0:T(1024)S(1)} %add_rsqrt_fusion.1, f32[768,1024]{1,0:T(8,128)} %copy-done.20, f32[768]{0:T(1024)S(1)} %broadcast_multiply_fusion.7, f32[1024]{0:T(1024)S(1)} %bitcast.375, ...), kind=kOutput, calls=%fused_computation.100 | convolution fusion | flops 19343077376 | bytes 38852608 | tf_op jit(solution)/shard_map/jtc,jdc->td/dot_general | solution.py:650
  499.1 9.3 fusion.59.d_ref
  508.4 37.0 %shard_map.393 = (f32[4,768,256]{2,1,0:T(8,128)S(1)}, f32[4,1024,256]{2,1,0:T(8,128)}, f32[4,1024,256]{2,1,0:T(8,128)}) custom-call(f32[4,768,256]{2,1,0:T(8,128)} %add_bitcast_fusion.1.q_ref, f32[4,1024,256]{2,1,0:T(8,128)} %fusion.58.k_ref, f32[4,1024,256]{2,1,0:T(8,128)} %add_bitcast_fusion.v_ref, f32[1024,1]{1,0:T(8,128)S(1)} %copy-done.8, ...), custom_call_target="tpu_custom_call" | custom-call | flops 67645734912 | bytes 20971520 | tf_op jit(solution)/shard_map/pallas_call | solution.py:616
  549.0 11.6 %fusion.21 = f32[1024,1024,1]{1,0,2:T(8,128)S(1)} fusion(f32[4,1024,256]{2,1,0:T(8,128)} %get-tuple-element.280, f32[4,4,1024,256]{3,2,1,0:T(8,128)} %bitcast.332), kind=kOutput, calls=%fused_computation.71 | convolution fusion | flops 6442450944 | bytes 12582912 | tf_op jit(solution)/shard_map/jtc,jdc->td/dot_general | solution.py:650
  560.6 9.8 bitcast_add_fusion
  580.6 8.8 bitcast_dynamic-update-slice_fusion.2
  589.5 9.4 bitcast_dynamic-update-slice_fusion.1
  598.9 7.4 bitcast_dynamic-update-slice_fusion
  606.4 16.7 %multiply_reduce_fusion.5 = (f32[1024]{0:T(1024)S(1)}, f32[768]{0:T(1024)S(1)}, f32[768]{0:T(1024)S(1)}, f32[1024]{0:T(1024)S(1)}, f32[768,1024]{1,0:T(8,128)}) fusion(f32[768,1024]{1,0:T(8,128)S(1)} %copy-done.12, f32[768]{0:T(1024)S(1)} %copy-done.71, f32[768]{0:T(1024)S(1)} %copy-done.64, f32[1024]{0:T(1024)S(1)} %bitcast.349, ...), kind=kOutput, calls=%fused_computation.101 | convolution fusion | flops 4841271808 | bytes 20996096 | tf_op jit(solution)/shard_map/jtc,jdc->td/dot_general | solution.py:650
  638.4 7.2 fusion.52
  671.1 204.4 %shard_map.394 = (f32[8,128,1024]{2,1,0:T(8,128)S(1)}, f32[8,128,1024]{2,1,0:T(8,128)}) custom-call(f32[8,128,1024]{2,1,0:T(8,128)} %bitcast.321, f32[8,128,1024]{2,1,0:T(8,128)} %bitcast.322), custom_call_target="tpu_custom_call" | custom-call | flops 16777216 | bytes 1006632960 | tf_op jit(solution)/shard_map/pallas_call | solution.py:410
  877.5 18.7 %scatter_custom_fusion.1 = f32[6304,256]{1,0:T(8,128)} fusion(s32[2816]{0:T(1024)S(1)} %fusion.91, f32[2816,256]{1,0:T(8,128)S(1)} %bitcast.339, f32[]{:T(128)} %constant.315.clone.1), kind=kCustom, calls=%fused_computation.77 | custom fusion | flops 720896 | bytes 6455300 | tf_op jit(solution)/shard_map/scatter-add | solution.py:854
  908.6 106.4 %shard_map.395 = f32[8,608,256]{2,1,0:T(8,128)S(1)} custom-call(f32[8,608,256]{2,1,0:T(8,128)} %bitcast.319), custom_call_target="tpu_custom_call" | custom-call | flops 9961472 | bytes 597688320 | tf_op jit(solution)/shard_map/pallas_call | solution.py:410
  1028.2 15.5 %shard_map.396 = f32[8,128]{1,0:T(8,128)} custom-call(f32[8,128]{1,0:T(8,128)} %broadcast_in_dim.244.x_ref), custom_call_target="tpu_custom_call" | custom-call | tf_op jit(solution)/shard_map/pallas_call | solution.py:290
  1052.9 12.5 %multiply_subtract_fusion.1 = (f32[6304,256]{1,0:T(8,128)}, f32[6304,256]{1,0:T(8,128)}) fusion(f32[6304,256]{1,0:T(8,128)} %get-tuple-element.628, f32[6304,256]{1,0:T(8,128)} %get-tuple-element.286, f32[]{:T(128)S(6)} %min.3, f32[6304,256]{1,0:T(8,128)} %param.40), kind=kLoop, calls=%fused_computation.45 | loop fusion | flops 12910592 | bytes 32276484 | tf_op jit(solution)/shard_map/sub | solution.py:79
  1069.5 9.9 multiply_subtract_fusion.2
  1080.8 10.6 multiply_subtract_fusion
  (372 shorter events, 175.7 us)
Async XLA Ops:
  7.2 199.8 %all-gather.6.cloned.1.call-start = ((), (), s32[]{:S(2)}) async-start(), calls=%async_computation.14 | async-start | bytes 20971520 | tf_op jit(solution)/shard_map/all_gather | solution.py:704
  13.4 99.3 %copy-start.77 = (s32[704]{0:T(1024)}, s32[704]{0:T(1024)S(1)}, u32[]{:S(2)}) copy-start(s32[704]{0:T(1024)S(1)} %broadcast_add_fusion.4) | copy-start | bytes 8452
  14.1 14.4 %all-to-all-start.4 = ((s32[32,1,128]{2,1,0:T(1,128)}), s32[32,1,128]{2,1,0:T(1,128)S(1)}, u32[]{:S(2)}, u32[]{:S(2)}) async-start(s32[32,1,128]{2,1,0:T(1,128)} %bitcast.15), calls=%async_computation.4 | async-start | bytes 32768 | tf_op jit(solution)/shard_map/all_to_all | solution.py:674
  39.6 71.3 %all-to-all-start.5 = ((f32[32,88,256]{2,1,0:T(8,128)}), f32[32,88,256]{2,1,0:T(8,128)S(1)}, u32[]{:S(2)}, u32[]{:S(2)}) async-start(f32[32,88,256]{2,1,0:T(8,128)} %bitcast.17), calls=%async_computation.5 | async-start | bytes 5767168 | tf_op jit(solution)/shard_map/all_to_all | solution.py:674
  42.4 264.1 %all-gather.4.cloned.1.call-start = ((), (), s32[]{:S(2)}) async-start(), calls=%async_computation.10 | async-start | bytes 20971520 | tf_op jit(solution)/shard_map/all_gather | solution.py:705
  51.0 52.2 %copy-start.93 = (s32[6]{0:T(128)S(1)}, s32[6]{0:T(128)}, u32[]{:S(2)}) copy-start(s32[6]{0:T(128)} %param.28) | copy-start | bytes 76
  51.0 52.8 %copy-start.61 = (f32[8,1024]{1,0:T(8,128)S(1)}, f32[8,1024]{1,0:T(8,128)}, u32[]{:S(2)}) copy-start(f32[8,1024]{1,0:T(8,128)} %param.36) | copy-start | bytes 98308
  51.0 608.6 %reduce-scatter.6.cloned.1.call-start = ((), (), s32[]{:S(2)}) async-start(), calls=%async_computation.12 | async-start | bytes 20971520 | tf_op jit(solution)/shard_map/reduce_scatter | solution.py:820
  53.0 50.2 %collective-permute-start.1 = (f32[518,256]{1,0:T(8,128)}, f32[518,256]{1,0:T(8,128)}, u32[]{:S(2)}, u32[]{:S(2)}) collective-permute-start(f32[518,256]{1,0:T(8,128)} %get-tuple-element.386), channel_id=1, source_target_pairs={{0,2},{1,3},{2,0},{3,1},{4,6},{5,7},{6,4},{7,5},{8,10},{9,11},{10,... | collective-permute-start | bytes 1591304 | tf_op jit(solution)/shard_map/ppermute | solution.py:709
  54.6 50.5 %collective-permute-start = (f32[518,256]{1,0:T(8,128)}, f32[518,256]{1,0:T(8,128)}, u32[]{:S(2)}, u32[]{:S(2)}) collective-permute-start(f32[518,256]{1,0:T(8,128)} %get-tuple-element.386), channel_id=1, source_target_pairs={{0,1},{1,0},{2,3},{3,2},{4,5},{5,4},{6,7},{7,6},{8,9},{9,8},{10,11... | collective-permute-start | bytes 1591304 | tf_op jit(solution)/shard_map/ppermute | solution.py:710
  103.2 2.3 collective-permute-start.2
  104.4 18.7 %copy-start.67 = (f32[1,1024]{1,0:T(1,128)}, f32[1,1024]{1,0:T(1,128)S(1)}, u32[]{:S(2)}) copy-start(f32[1,1024]{1,0:T(1,128)S(1)} %get-tuple-element.397) | copy-start | bytes 12292
  126.3 80.7 %collective-permute-start.3 = (f32[256,1024]{1,0:T(8,128)}, f32[256,1024]{1,0:T(8,128)}, u32[]{:S(2)}, u32[]{:S(2)}) collective-permute-start(f32[256,1024]{1,0:T(8,128)} %slice.191), channel_id=1, source_target_pairs={{0,1},{1,0},{2,3},{3,2},{4,5},{5,4},{6,7},{7,6},{8,9},{9,8},{10,11... | collective-permute-start | bytes 3145736 | tf_op jit(solution)/shard_map/ppermute | solution.py:764
  131.2 103.0 %copy-start.7 = (f32[1024,1]{1,0:T(8,128)}, f32[1024,1]{1,0:T(8,128)S(1)}, u32[]{:S(2)}) copy-start(f32[1024,1]{1,0:T(8,128)S(1)} %broadcast_select_fusion.bias_ref) | copy-start | bytes 12292
  234.2 33.3 %copy-start.76 = (f32[1,1024]{1,0:T(1,128)S(1)}, f32[1,1024]{1,0:T(1,128)}, u32[]{:S(2)}) copy-start(f32[1,1024]{1,0:T(1,128)} %get-tuple-element.395) | copy-start | bytes 12292
  276.8 29.7 %copy-start.20 = (f32[768,1024]{1,0:T(8,128)}, f32[768,1024]{1,0:T(8,128)S(1)}, u32[]{:S(2)}) copy-start(f32[768,1024]{1,0:T(8,128)S(1)} %get-tuple-element.408) | copy-start | bytes 9437188
  277.6 28.9 %copy-start.87 = (f32[1,1024]{1,0:T(1,128)S(1)}, f32[1,1024]{1,0:T(1,128)}, u32[]{:S(2)}) copy-start(f32[1,1024]{1,0:T(1,128)} %get-tuple-element.392) | copy-start | bytes 12292
  336.2 131.0 %copy-start.13 = (f32[768,1024]{1,0:T(8,128)}, f32[768,1024]{1,0:T(8,128)S(1)}, u32[]{:S(2)}) copy-start(f32[768,1024]{1,0:T(8,128)S(1)} %get-tuple-element.410) | copy-start | bytes 9437188
  337.0 27.1 %copy-start.50 = (f32[256,64]{0,1:T(8,128)S(1)}, f32[256,64]{0,1:T(8,128)}, u32[]{:S(2)}) copy-start(f32[256,64]{0,1:T(8,128)} %param.38) | copy-start | bytes 196612
  368.8 31.9 %copy-start.55 = (f32[48,256]{1,0:T(8,128)}, f32[48,256]{1,0:T(8,128)S(1)}, u32[]{:S(2)}) copy-start(f32[48,256]{1,0:T(8,128)S(1)} %get-tuple-element.426) | copy-start | bytes 147460
  400.6 36.0 %copy-start.86 = (f32[1,1024]{1,0:T(1,128)S(1)}, f32[1,1024]{1,0:T(1,128)}, u32[]{:S(2)}) copy-start(f32[1,1024]{1,0:T(1,128)} %get-tuple-element.393) | copy-start | bytes 12292
  400.7 264.4 %reduce-scatter.8.cloned.1.call-start = ((), (), s32[]{:S(2)}) async-start(), calls=%async_computation.13 | async-start | bytes 20971520 | tf_op jit(solution)/shard_map/reduce_scatter | solution.py:824
  400.7 36.0 %copy-start.21 = (f32[768,1024]{1,0:T(8,128)S(1)}, f32[768,1024]{1,0:T(8,128)}, u32[]{:S(2)}) copy-start(f32[768,1024]{1,0:T(8,128)} %copy-done.20) | copy-start | bytes 9437188
  461.3 441.5 %reduce-scatter.4.cloned.1.call-start = ((), (), s32[]{:S(2)}) async-start(), calls=%async_computation.11 | async-start | bytes 24903680 | tf_op jit(solution)/shard_map/reduce_scatter | solution.py:887
  467.2 30.7 %copy-start.22 = (f32[768,1024]{1,0:T(8,128)S(1)}, f32[768,1024]{1,0:T(8,128)}, u32[]{:S(2)}) copy-start(f32[768,1024]{1,0:T(8,128)} %copy-done.20) | copy-start | bytes 9437188
  571.5 34.8 %collective-permute-start.4 = (f32[256,1024]{1,0:T(8,128)}, f32[256,1024]{1,0:T(8,128)}, u32[]{:S(2)}, u32[]{:S(2)}) collective-permute-start(f32[256,1024]{1,0:T(8,128)} %slice.200), channel_id=1, source_target_pairs={{0,1},{1,0},{2,3},{3,2},{4,5},{5,4},{6,7},{7,6},{8,9},{9,8},{10,11... | collective-permute-start | bytes 3145736 | tf_op jit(solution)/shard_map/ppermute | solution.py:838
  606.4 16.7 %copy-start.18 = (f32[4,4864,256]{1,2,0:T(8,128)}, f32[4,4864,256]{1,2,0:T(8,128)S(1)}, u32[]{:S(2)}) copy-start(f32[4,4864,256]{1,2,0:T(8,128)S(1)} %bitcast_dynamic-update-slice_fusion) | copy-start | bytes 59768836
  650.9 226.6 %all-to-all-start.6 = ((f32[32,88,256]{2,1,0:T(8,128)}), f32[32,88,256]{2,1,0:T(8,128)S(1)}, u32[]{:S(2)}, u32[]{:S(2)}) async-start(f32[32,88,256]{2,1,0:T(8,128)} %bitcast.84), calls=%async_computation.7 | async-start | bytes 5767168 | tf_op jit(solution)/shard_map/all_to_all | solution.py:674
  908.6 109.0 %slice-start = ((s8[6455296]{0:T(1024)(128)(4,1)}), s8[4194304]{0:T(1024)(128)(4,1)S(1)}, s32[]{:S(2)}) async-start(s8[6455296]{0:T(1024)(128)(4,1)} %bitcast.311), calls=%async_computation.15 | async-start | bytes 8388608
  908.6 109.0 %slice-start.1 = ((s8[6455296]{0:T(1024)(128)(4,1)}), s8[2260992]{0:T(1024)(128)(4,1)S(1)}, s32[]{:S(2)}) async-start(s8[6455296]{0:T(1024)(128)(4,1)} %bitcast.311), calls=%async_computation.16 | async-start | bytes 4521984
  1052.9 13.9 %copy-start.38 = (f32[514,256]{1,0:T(8,128)S(1)}, f32[514,256]{1,0:T(8,128)}, u32[]{:S(2)}) copy-start(f32[514,256]{1,0:T(8,128)} %param.31) | copy-start | bytes 1579012
  1052.9 13.9 %copy-start.54 = (f32[514,256]{1,0:T(8,128)S(1)}, f32[514,256]{1,0:T(8,128)}, u32[]{:S(2)}) copy-start(f32[514,256]{1,0:T(8,128)} %param.41) | copy-start | bytes 1579012
  (80 other events, 418.1 us)
Sparse Core Ops, SparseCore 0:
  9.6 162.2 all-gather.5
  174.0 105.8 all-gather.3
  400.8 124.2 reduce-scatter.5
  527.7 126.0 reduce-scatter.7
  656.2 151.6 reduce-scatter.3

commit v3 on v2

--- a/solution.py
+++ b/solution.py
@@ -262,44 +262,8 @@
     pl.semaphore_wait(barrier, len(partners))
 
 
-def cube_sum_kernel(groups, shards, x_ref, o_ref, sent, landed, send_sem, recv_sem):
-    partners = cube_partners(groups, shards)
-    greet(partners)
-    sent[0] = x_ref[...]
-    for stage, partner in enumerate(partners):
-        copy = pltpu.make_async_remote_copy(
-            src_ref=sent.at[stage],
-            dst_ref=landed.at[stage],
-            send_sem=send_sem.at[stage],
-            recv_sem=recv_sem.at[stage],
-            device_id=partner,
-            device_id_type=MESH,
-        )
-        copy.start()
-        copy.wait()
-        sent[stage + 1] = sent[stage] + landed[stage]
-    o_ref[...] = sent[len(partners)]
-
-
 def cube_stages(groups, shards):
     return (groups * shards).bit_length() - 1
-
-
-def cube_sum(block, groups, shards, collective_id):
-    stages = cube_stages(groups, shards)
-    return pl.pallas_call(
-        functools.partial(cube_sum_kernel, groups, shards),
-        out_shape=jax.ShapeDtypeStruct(block.shape, block.dtype),
-        in_specs=[VMEM],
-        out_specs=VMEM,
-        scratch_shapes=[
-            pltpu.VMEM((stages + 1, *block.shape), block.dtype),
-            pltpu.VMEM((stages, *block.shape), block.dtype),
-            pltpu.SemaphoreType.DMA((stages,)),
-            pltpu.SemaphoreType.DMA((stages,)),
-        ],
-        compiler_params=pltpu.CompilerParams(collective_id=collective_id, has_side_effects=True),
-    )(block)
 
 
 def cube_gather_kernel(groups, shards, x_ref, o_ref, held, send_sem, recv_sem):
@@ -340,9 +304,23 @@
     )(block)
 
 
-def ring_kernel(groups, parts, arrays, *refs):
-    inputs, outputs, slots = refs[:arrays], refs[arrays : 2 * arrays], refs[2 * arrays : 3 * arrays]
-    send_sem, recv_sem = refs[3 * arrays :]
+def fold_squares(block):
+    block = block * block
+    folded = jnp.sum(block.reshape(block.shape[0] // 8, 8, block.shape[1]), axis=0)
+    total = folded[:, :128]
+    for start in range(128, block.shape[1], 128):
+        total = total + folded[:, start : start + 128]
+    return total
+
+
+def ring_kernel(groups, shards, parts, arrays, shared_rows, *refs):
+    refs = list(refs)
+    inputs = [refs.pop(0) for _ in range(arrays)]
+    base = refs.pop(0)
+    outputs = [refs.pop(0) for _ in range(arrays)]
+    squares_ref = refs.pop(0)
+    slots = [refs.pop(0) for _ in range(arrays)]
+    send_sem, recv_sem, sent, landed, cube_send, cube_recv = refs
     depth = groups // 2
     dp, tp = lax.axis_index("dp"), lax.axis_index("tensor")
     side, level = dp % 2, dp // 2
@@ -353,79 +331,112 @@
         far = spot // depth
         return (2 * (spot * (1 - far) + (groups - 1 - spot) * far) + far, tp)
 
-    greet([device_at(place + 1), device_at(place - 1)])
+    partners = cube_partners(groups, shards) if shared_rows else []
+    greet([device_at(place + 1), device_at(place - 1), *partners])
     streams = []
     for array in range(arrays):
         rows = inputs[array].shape[1] // (2 * parts)
         for part in range(2 * parts):
-            streams.append((array, 1 - 2 * (part % 2), pl.ds(part * rows, rows)))
+            streams.append((array, 1 - 2 * (part % 2), part * rows, rows))
 
     def chunk(step, way):
         return (place + groups * 2 - way * step) % groups
 
     copies = []
 
-    def send(index, step, source, target):
+    def send(source, target, send_at, recv_at, device):
         copy = pltpu.make_async_remote_copy(
             src_ref=source,
             dst_ref=target,
-            send_sem=send_sem.at[index, step],
-            recv_sem=recv_sem.at[index, step],
-            device_id=device_at(place + streams[index][1]),
+            send_sem=send_at,
+            recv_sem=recv_at,
+            device_id=device,
             device_id_type=MESH,
         )
         copy.start()
         copies.append(copy)
         return copy
 
+    def pass_on(index, step, source, target):
+        device = device_at(place + streams[index][1])
+        return send(source, target, send_sem.at[index, step], recv_sem.at[index, step], device)
+
     flying = [None] * len(streams)
     for step in range(groups - 1):
-        for index, (array, way, rows) in enumerate(streams):
+        for index, (array, way, start, size) in enumerate(streams):
+            rows = pl.ds(start, size)
             if step == 0:
                 source = inputs[array].at[chunk(0, way), rows]
             else:
                 flying[index].wait_recv()
                 source = slots[array].at[step - 1, rows]
                 source[...] = source[...] + inputs[array][chunk(step, way), rows]
-            flying[index] = send(index, step, source, slots[array].at[step, rows])
+            flying[index] = pass_on(index, step, source, slots[array].at[step, rows])
+    total = base[...]
+    crossing = None
     for step in range(groups - 1):
-        for index, (array, way, rows) in enumerate(streams):
+        for index, (array, way, start, size) in enumerate(streams):
+            rows = pl.ds(start, size)
             flying[index].wait_recv()
             now = chunk(groups - 1 + step, way)
             if step == 0:
-                outputs[array][now, rows] = slots[array][groups - 2, rows] + inputs[array][now, rows]
-            place_out = outputs[array].at[now, rows]
-            flying[index] = send(index, groups - 1 + step, place_out, place_out)
+                block = slots[array][groups - 2, rows] + inputs[array][now, rows]
+                outputs[array][now, rows] = block
+                if shared_rows:
+                    depth_rows = inputs[array].shape[1]
+                    limit = groups * depth_rows - shared_rows * (1 - (shards - tp) // shards)
+                    at = now * depth_rows + start + lax.broadcasted_iota(jnp.int32, block.shape, 0)
+                    block = jnp.where(at < limit, block, 0.0)
+                total = total + fold_squares(block)
+            out = outputs[array].at[now, rows]
+            flying[index] = pass_on(index, groups - 1 + step, out, out)
+        if step <= len(partners) and partners:
+            if step == 0:
+                sent[0] = total
+            else:
+                crossing.wait_recv()
+                sent[step] = sent[step - 1] + landed[step - 1]
+            if step < len(partners):
+                crossing = send(
+                    sent.at[step], landed.at[step], cube_send.at[step], cube_recv.at[step], partners[step]
+                )
+    squares_ref[...] = sent[len(partners)] if partners else total
     for copy in flying:
         copy.wait_recv()
     for copy in copies:
         copy.wait_send()
 
 
-def ring_sum(arrays, groups, parts, collective_id):
+def ring_sum(arrays, base, groups, shards, parts, shared_rows, collective_id):
     blocks = [array.reshape(groups, array.shape[0] // groups, array.shape[1]) for array in arrays]
     streams = 2 * parts * len(blocks)
     steps = 2 * (groups - 1)
-    moved = sum(2 * block.size * 4 for block in blocks)
-    sums = pl.pallas_call(
-        functools.partial(ring_kernel, groups, parts, len(blocks)),
-        out_shape=[jax.ShapeDtypeStruct(block.shape, block.dtype) for block in blocks],
-        in_specs=[VMEM] * len(blocks),
-        out_specs=[VMEM] * len(blocks),
+    stages = cube_stages(groups, shards)
+    *sums, squared = pl.pallas_call(
+        functools.partial(ring_kernel, groups, shards, parts, len(blocks), shared_rows),
+        out_shape=[jax.ShapeDtypeStruct(block.shape, block.dtype) for block in [*blocks, base]],
+        in_specs=[VMEM] * (len(blocks) + 1),
+        out_specs=[VMEM] * (len(blocks) + 1),
         scratch_shapes=[
             *[pltpu.VMEM((groups - 1, *block.shape[1:]), block.dtype) for block in blocks],
             pltpu.SemaphoreType.DMA((streams, steps)),
             pltpu.SemaphoreType.DMA((streams, steps)),
+            pltpu.VMEM((stages + 1, *base.shape), base.dtype),
+            pltpu.VMEM((stages, *base.shape), base.dtype),
+            pltpu.SemaphoreType.DMA((stages,)),
+            pltpu.SemaphoreType.DMA((stages,)),
         ],
         compiler_params=pltpu.CompilerParams(
             collective_id=collective_id, has_side_effects=True, vmem_limit_bytes=48 << 20
         ),
-        cost_estimate=pl.CostEstimate(flops=moved, bytes_accessed=60 * moved, transcendentals=0),
-    )(*blocks)
-    return [total.reshape(array.shape) for total, array in zip(sums, arrays)]
-
-
-def spread_kernel(groups, w_ref, o_ref, local_sem, pair_send, pair_recv, ring_send, ring_recv, core_send, core_recv):
+        cost_estimate=pl.CostEstimate(flops=1, bytes_accessed=1024, transcendentals=0),
+    )(*blocks, base)
+    return [total.reshape(array.shape) for total, array in zip(sums, arrays)], squared
+
+
+def spread_kernel(
+    groups, w_ref, small_ref, o_ref, rows_ref, local_sem, pair_send, pair_recv, ring_send, ring_recv, core_send, core_recv
+):
     depth = groups // 2
     dp, tp = lax.axis_index("dp"), lax.axis_index("tensor")
     far = tp + 2 - 4 * (tp // 2)
@@ -453,14 +464,17 @@
     greet([(index_at(place + 1), tp), (index_at(place - 1), tp), core, (dp, far)])
     cross = send(w_ref.at[dp], o_ref.at[tp, dp], pair_send.at[0], pair_recv.at[0], (dp, far))
     near = send(w_ref, o_ref.at[tp], pair_send.at[1], pair_recv.at[1], core)
+    cross_rows = send(small_ref, rows_ref.at[tp], pair_send.at[2], pair_recv.at[2], (dp, far))
+    near_rows = send(small_ref, rows_ref.at[tp], pair_send.at[3], pair_recv.at[3], core)
     local = pltpu.make_async_copy(w_ref, o_ref.at[tp], local_sem)
     local.start()
+    rows_ref[tp] = small_ref[...]
     cross.wait_recv()
     lanes = ring_send.shape[0]
     size = w_ref.shape[1] // lanes
     flying = [None] * lanes
-    started = [cross]
-    handed = [near]
+    started = [cross, cross_rows]
+    handed = [near, near_rows]
     for step in range(groups):
         for lane in range(lanes):
             way = 1 - 2 * (lane % 2)
@@ -473,6 +487,8 @@
                 )
                 started.append(flying[lane])
             handed.append(send(block, block, core_send.at[lane, step], core_recv.at[lane, step], core))
+    cross_rows.wait_recv()
+    handed.append(send(rows_ref.at[far], rows_ref.at[far], pair_send.at[4], pair_recv.at[4], core))
     for copy in handed:
         copy.wait_recv()
         copy.wait_send()
@@ -481,19 +497,21 @@
     local.wait()
 
 
-def spread(weight, groups, collective_id):
+def spread(weight, small, groups, collective_id):
     rows = weight.shape[0] // groups
     lanes = 4
-    moved = 4 * weight.size
-    gathered = pl.pallas_call(
+    gathered, gathered_rows = pl.pallas_call(
         functools.partial(spread_kernel, groups),
-        out_shape=jax.ShapeDtypeStruct((4, groups, rows, weight.shape[1]), weight.dtype),
-        in_specs=[pl.BlockSpec(memory_space=pl.ANY)],
-        out_specs=VMEM,
+        out_shape=[
+            jax.ShapeDtypeStruct((4, groups, rows, weight.shape[1]), weight.dtype),
+            jax.ShapeDtypeStruct((4, *small.shape), small.dtype),
+        ],
+        in_specs=[pl.BlockSpec(memory_space=pl.ANY), VMEM],
+        out_specs=[VMEM, VMEM],
         scratch_shapes=[
             pltpu.SemaphoreType.DMA,
-            pltpu.SemaphoreType.DMA((2,)),
-            pltpu.SemaphoreType.DMA((2,)),
+            pltpu.SemaphoreType.DMA((5,)),
+            pltpu.SemaphoreType.DMA((5,)),
             pltpu.SemaphoreType.DMA((lanes, groups - 1)),
             pltpu.SemaphoreType.DMA((lanes, groups - 1)),
             pltpu.SemaphoreType.DMA((lanes, groups)),
@@ -502,9 +520,9 @@
         compiler_params=pltpu.CompilerParams(
             collective_id=collective_id, has_side_effects=True, vmem_limit_bytes=32 << 20
         ),
-        cost_estimate=pl.CostEstimate(flops=moved, bytes_accessed=30 * moved, transcendentals=0),
-    )(weight.reshape(groups, rows, weight.shape[1]))
-    return gathered.reshape(4, *weight.shape)
+        cost_estimate=pl.CostEstimate(flops=1, bytes_accessed=1024, transcendentals=0),
+    )(weight.reshape(groups, rows, weight.shape[1]), small)
+    return gathered.reshape(4, *weight.shape), gathered_rows
 
 
 def halves(array):
@@ -624,6 +642,143 @@
     )(*inputs)
 
 
+WIDE = 512
+
+
+def dot_three(high_left, low_left, right, dot):
+    high, low = halves(right)
+    return dot(high_left, high) + dot(high_left, low) + dot(low_left, high)
+
+
+def times_kernel(finish, extras, x_ref, w_ref, *refs):
+    more, outs, (high, low) = refs[:extras], refs[extras:-2], refs[-2:]
+
+    @pl.when((pl.program_id(0) == 0) & (pl.program_id(1) == 0))
+    def _():
+        high[...], low[...] = halves(x_ref[...])
+
+    weight = w_ref[...].reshape(w_ref.shape[-2], w_ref.shape[-1])
+    finish(dot_three(high[...], low[...], weight, dot_plain), more, outs)
+
+
+def times(x, w, which, finish, extras, outs):
+    shards, depth, columns = w.shape[0], w.shape[-2], w.shape[-1]
+    rows, wide = x.shape[0], min(WIDE, columns)
+    if w.ndim == 4:
+        w_spec = pl.BlockSpec((1, 1, depth, wide), lambda j, c: (j, which, 0, c))
+    else:
+        w_spec = pl.BlockSpec((1, depth, wide), lambda j, c: (j, 0, c))
+
+    def spec(shape):
+        return pl.BlockSpec((1, shape[1], wide), lambda j, c: (j, 0, c))
+
+    results = pl.pallas_call(
+        functools.partial(times_kernel, finish, len(extras)),
+        grid=(shards, columns // wide),
+        in_specs=[pl.BlockSpec((rows, depth), lambda j, c: (0, 0)), w_spec, *[spec(e.shape) for e in extras]],
+        out_specs=[spec(shape) for shape in outs],
+        out_shape=[jax.ShapeDtypeStruct(shape, jnp.float32) for shape in outs],
+        scratch_shapes=[pltpu.VMEM((rows, depth), jnp.bfloat16)] * 2,
+        compiler_params=pltpu.CompilerParams(vmem_limit_bytes=48 << 20),
+        cost_estimate=pl.CostEstimate(
+            flops=6 * rows * depth * shards * columns, bytes_accessed=4 * w.size, transcendentals=0
+        ),
+    )(x, w, *extras)
+    return results
+
+
+def keep_tile(tile, more, outs):
+    outs[0][0] = tile
+
+
+def add_row(tile, more, outs):
+    outs[0][0] = tile + more[0][0]
+
+
+def gelu_tile(tile, more, outs):
+    outs[0][0], outs[1][0] = gelu_both(tile + more[0][0])
+
+
+def scale_tile(tile, more, outs):
+    tile = tile * more[0][0]
+    outs[0][0] = tile
+    outs[1][0] = jnp.sum(tile, axis=0, keepdims=True)
+
+
+def gather_back_kernel(count, base_ref, *refs):
+    out = refs[-1]
+
+    @pl.when((pl.program_id(0) == 0) & (pl.program_id(1) == 0))
+    def _():
+        out[...] = base_ref[...]
+
+    for a_ref, w_ref in zip(refs[:count], refs[count : 2 * count]):
+        high, low = halves(a_ref[0])
+        weight = w_ref[...].reshape(w_ref.shape[-2], w_ref.shape[-1])
+        rows = pl.ds(0, a_ref.shape[1])
+        out[rows] += dot_three(high, low, weight, dot_rows)
+
+
+def gather_back(base, terms):
+    arrays = [array for array, _, _ in terms]
+    shards, _, columns = arrays[0].shape
+    wide = min(WIDE, columns)
+
+    def w_spec(w, which):
+        if w.ndim == 4:
+            return pl.BlockSpec((1, 1, w.shape[-2], wide), lambda j, c: (j, which, 0, c))
+        return pl.BlockSpec((1, w.shape[-2], wide), lambda j, c: (j, 0, c))
+
+    work = sum(6 * array.size * w.shape[-2] for array, w, _ in terms)
+    return pl.pallas_call(
+        functools.partial(gather_back_kernel, len(terms)),
+        grid=(shards, columns // wide),
+        in_specs=[
+            pl.BlockSpec(base.shape, lambda j, c: (0, 0)),
+            *[pl.BlockSpec((1, a.shape[1], wide), lambda j, c: (j, 0, c)) for a in arrays],
+            *[w_spec(w, which) for _, w, which in terms],
+        ],
+        out_specs=pl.BlockSpec(base.shape, lambda j, c: (0, 0)),
+        out_shape=jax.ShapeDtypeStruct(base.shape, jnp.float32),
+        compiler_params=pltpu.CompilerParams(vmem_limit_bytes=48 << 20),
+        cost_estimate=pl.CostEstimate(flops=work, bytes_accessed=16 << 20, transcendentals=0),
+    )(base, *arrays, *[w for _, w, _ in terms])
+
+
+def outer_kernel(x_ref, d_ref, *refs):
+    out, high, low = refs[-3:]
+
+    @pl.when((pl.program_id(0) == 0) & (pl.program_id(1) == 0))
+    def _():
+        high[...], low[...] = halves(x_ref[...].T)
+
+    out[0] = dot_three(high[...], low[...], d_ref[0], dot_plain)
+
+
+def outer(x, d, rows, at, into=None):
+    tokens, depth = x.shape
+    shards, _, columns = d.shape
+    wide = min(WIDE, columns)
+    held = [] if into is None else [into]
+    return pl.pallas_call(
+        outer_kernel,
+        grid=(shards, columns // wide),
+        in_specs=[
+            pl.BlockSpec((tokens, depth), lambda j, c: (0, 0)),
+            pl.BlockSpec((1, tokens, wide), lambda j, c: (j, 0, c)),
+            *[pl.BlockSpec(memory_space=pl.ANY) for _ in held],
+        ],
+        out_specs=pl.BlockSpec((1, depth, wide), lambda j, c: (j, at, c)),
+        out_shape=jax.ShapeDtypeStruct((shards, rows, columns), jnp.float32),
+        scratch_shapes=[pltpu.VMEM((depth, tokens), jnp.bfloat16)] * 2,
+        input_output_aliases={2: 0} if held else {},
+        compiler_params=pltpu.CompilerParams(vmem_limit_bytes=48 << 20),
+        cost_estimate=pl.CostEstimate(
+            flops=6 * tokens * depth * shards * columns, bytes_accessed=4 * shards * depth * columns, transcendentals=0
+        ),
+    )(x, d, *held)
+
+
 def normalise(values):
     center = values - jnp.mean(values, axis=-1, keepdims=True)
     scale = lax.rsqrt(jnp.mean(center * center, axis=-1, keepdims=True) + EPS)
@@ -702,21 +857,11 @@
     split_length = lax.dynamic_index_in_dim(lengths, split_seq, 0, keepdims=False)
 
     all_attn = lax.all_gather(attn_weights, "tensor")
+    parts_shape = (shards, count, hidden)
     all_ffn_down = lax.all_gather(ffn_weights[1], "tensor")
     small = jnp.concatenate([positions[2 : slots + 2], bias_qv, bias_up.reshape(-1, cols)], axis=0)
+    small = jnp.pad(small, ((0, -small.shape[0] % 8), (0, 0)))
     swap = [(i, i ^ 1) for i in range(shards)]
-    swap_pair = [(i, i ^ 2) for i in range(shards)]
-    far_small = lax.ppermute(small, "tensor", swap_pair)
-    rows_small = jnp.stack([small, lax.ppermute(small, "tensor", swap), far_small, lax.ppermute(far_small, "tensor", swap)])
-    all_small = jnp.concatenate(
-        [
-            lax.dynamic_index_in_dim(rows_small, 2 * ((j // 2 + pair) % 2) + (j + side) % 2, 0)
-            for j in range(shards)
-        ]
-    )
-    all_positions = all_small[:, :slots].transpose(1, 0, 2).reshape(slots, width)
-    all_bias_up = all_small[:, slots + 2 :].reshape(-1)
-
     owner, rank = request_lists(ids, vocab_rows, groups)
     rounds_here = jnp.max(rank) // CAPACITY + 1
 
@@ -731,8 +876,8 @@
         rounds = jnp.max(asked[:, CAPACITY])
         return wanted, rows, rounds
 
-    def ask(rows):
-        return trade(jnp.take(embedding, rows, axis=0, mode="clip"))
+    def find(rows):
+        return jnp.take(embedding, rows, axis=0, mode="clip")
 
     def expand(wanted, landed):
         landed = landed.reshape(groups, shards, CAPACITY, cols)
@@ -741,8 +886,11 @@
         return jnp.matmul(chosen, landed, precision=HIGH)
 
     wanted_first, rows_first, rounds = serve(0)
-    landed, up_weights = lax.optimization_barrier((ask(rows_first), ffn_weights[0]))
-    all_ffn_up = spread(up_weights, groups, 6)
+    found, up_weights = lax.optimization_barrier((find(rows_first), ffn_weights[0]))
+    all_ffn_up, all_small = spread(up_weights, small, groups, 6)
+    landed, all_small = lax.optimization_barrier((trade(found), all_small))
+    all_positions = all_small[:, :slots].transpose(1, 0, 2).reshape(slots, width)
+    all_bias_up = all_small[:, slots + 2 : slots + 2 + hidden // cols].reshape(-1)
     tokens = expand(wanted_first, landed)
 
     def more(state):
@@ -751,7 +899,7 @@
     def fetch_more(state):
         round_index, total = state
         wanted, rows, _ = serve(round_index)
-        return round_index + 1, total + expand(wanted, ask(rows))
+        return round_index + 1, total + expand(wanted, trade(find(rows)))
 
     _, tokens = lax.while_loop(more, fetch_more, (jnp.int32(1), tokens))
     own_positions = jnp.concatenate(
@@ -764,9 +912,10 @@
     h_other = lax.ppermute(h_zero[slots:], "tensor", swap)
     h_keys = jnp.concatenate([h_zero, h_other], axis=0)
     bias_q, bias_v = all_small[:, slots], all_small[:, slots + 1]
-    queries = product("td,jdc->jtc", h_zero, all_attn[:, 0]) + bias_q[:, None, :]
-    keys_all = product("td,jdc->jtc", h_keys, all_attn[:, 1])
-    values = product("td,jdc->jtc", h_keys, all_attn[:, 2]) + bias_v[:, None, :]
+    keys_shape = (shards, count + half, cols)
+    (queries,) = times(h_zero, all_attn, 0, add_row, [bias_q[:, None, :]], [(shards, count, cols)])
+    (keys_all,) = times(h_keys, all_attn, 1, keep_tile, [], [keys_shape])
+    (values,) = times(h_keys, all_attn, 2, add_row, [bias_v[:, None, :]], [keys_shape])
     key_index = lax.broadcasted_iota(jnp.int32, (slots,), 0)
     own_first = jnp.where(
         key_index < half, side * half + key_index, (1 - side) * half + key_index - half
@@ -779,13 +928,13 @@
         (queries, keys_all, values, key_bias),
         (queries.shape, (heads // 2, 2, count)),
     )
-    x_one = h_zero + product("jtc,jdc->td", mixed, all_attn[:, 3]) + norms[6]
+    x_one = gather_back(h_zero + norms[6], [(mixed, all_attn, 3)])
     unit_one, scale_one = normalise(x_one)
     h_one = unit_one * norms[2] + norms[3]
 
-    up = product("td,jdc->tjc", h_one, all_ffn_up) + all_bias_up.reshape(shards, hidden)
-    act, act_slope = lax.optimization_barrier(gelu_both(up))
-    x_two = h_one + product("tjc,jdc->td", act, all_ffn_down) + norms[7]
+    bias_tiles = all_bias_up.reshape(shards, 1, hidden)
+    act, act_slope = times(h_one, all_ffn_up, 0, gelu_tile, [bias_tiles], [parts_shape, parts_shape])
+    x_two = gather_back(h_one + norms[7], [(act, all_ffn_down, 0)])
     unit_two, scale_two = normalise(x_two)
     h_two = unit_two * norms[4] + norms[5]
 
@@ -816,30 +965,30 @@
     back_h_two = weight_whole[:, None] * back_whole[None, :] + weight_split[:, None] * back_split[None, :]
 
     back_x_two, grad_gain_two, grad_shift_two = normalise_back(back_h_two, norms[4], unit_two, scale_two)
-    grad_down = product("td,tjc->jdc", back_x_two, act)
+    grad_down = outer(back_x_two, act, width, 0)
     sum_down = lax.psum_scatter(grad_down, "tensor", scatter_dimension=0, tiled=False)
-    back_up = product("td,jdc->jtc", back_x_two, all_ffn_down) * act_slope.transpose(1, 0, 2)
-    grad_up = product("td,jtc->jdc", h_one, back_up)
+    back_up, grad_bias_up = times(
+        back_x_two, all_ffn_down, 0, scale_tile, [act_slope], [parts_shape, bias_tiles.shape]
+    )
+    grad_up = outer(h_one, back_up, width, 0)
     back_up, grad_up = lax.optimization_barrier((back_up, grad_up))
     sum_up = lax.psum_scatter(grad_up, "tensor", scatter_dimension=0, tiled=False)
-    grad_bias_up = jnp.sum(back_up, axis=1)
-    back_h_one = back_x_two + product("jtc,jdc->td", back_up, all_ffn_up)
+    back_h_one = gather_back(back_x_two, [(back_up, all_ffn_up, 0)])
     back_x_one, grad_gain_one, grad_shift_one = normalise_back(back_h_one, norms[2], unit_one, scale_one)
 
-    back_mixed = product("td,jdc->jtc", back_x_one, all_attn[:, 3])
-    grad_out = product("td,jtc->jdc", back_x_one, mixed)
+    (back_mixed,) = times(back_x_one, all_attn, 3, keep_tile, [], [mixed.shape])
     back_q, back_k, back_v = attend_call(
         attend_back_kernel,
         slots,
         (queries, keys_all, values, key_bias, mixed, lse, back_mixed),
         (queries.shape, keys_all.shape, values.shape),
     )
-    back_keys = product("jtc,jdc->td", back_k, all_attn[:, 1]) + product("jtc,jdc->td", back_v, all_attn[:, 2])
+    base_keys = jnp.pad(back_x_one, ((0, half), (0, 0)))
+    back_keys = gather_back(
+        base_keys, [(back_q, all_attn, 0), (back_k, all_attn, 1), (back_v, all_attn, 2)]
+    )
     back_other = lax.ppermute(back_keys[count:], "tensor", swap)
-    grad_q = product("td,jtc->jdc", h_zero, back_q)
-    grad_k = product("td,jtc->jdc", h_keys, back_k)
-    grad_v = product("td,jtc->jdc", h_keys, back_v)
-    back_h_zero = back_x_one + product("jtc,jdc->td", back_q, all_attn[:, 0]) + back_keys[:count]
+    back_h_zero = back_keys[:count]
     back_h_zero = back_h_zero + jnp.pad(back_other, ((slots, 0), (0, 0)))
     back_embedded, grad_gain_zero, grad_shift_zero = normalise_back(back_h_zero, norms[0], unit_zero, scale_zero)
 
@@ -847,14 +996,21 @@
         chosen = (wanted[:, None] == ids[None, :]).astype(jnp.float32)
         summed = jnp.matmul(chosen, back_embedded, precision=HIGH)
         parts = summed.reshape(groups, CAPACITY, shards, cols).transpose(0, 2, 1, 3)
-        return trade(parts.reshape(devices * CAPACITY, cols))
+        return parts.reshape(devices * CAPACITY, cols)
 
     def add_rows(landed, rows, total):
         target = jnp.where(rows >= 0, rows, vocab_rows)
         return total.at[target].add(landed, mode="drop")
 
-    landed_first = send_back(wanted_first)
-
+    leaving, back_q, back_k, back_v, back_x_one = lax.optimization_barrier(
+        (send_back(wanted_first), back_q, back_k, back_v, back_x_one)
+    )
+    landed_first = trade(leaving)
+    part_rows = 4 * width + slots + 256
+    parts_attn = outer(h_zero, back_q, part_rows, 0)
+    parts_attn = outer(h_keys, back_k, part_rows, 1, parts_attn)
+    parts_attn = outer(h_keys, back_v, part_rows, 2, parts_attn)
+    parts_attn = outer(back_x_one, mixed, part_rows, 3, parts_attn)
     grad_small = jnp.concatenate(
         [
             jnp.stack(
@@ -883,9 +1039,16 @@
     small_size = grad_small.size
     small_rows = jnp.pad(grad_small.reshape(-1), (0, 256 * cols - small_size)).reshape(1, 256, cols)
     small_rows = jnp.broadcast_to(small_rows, (shards, 256, cols))
-    parts_attn = jnp.concatenate([grad_q, grad_k, grad_v, grad_out, grad_pos_parts, small_rows], axis=1)
+    parts_attn = lax.dynamic_update_slice(parts_attn, grad_pos_parts, (0, 4 * width, 0))
+    parts_attn = lax.dynamic_update_slice(parts_attn, small_rows, (0, 4 * width + slots, 0))
+    landed_first, parts_attn = lax.optimization_barrier((landed_first, parts_attn))
     sum_attn = lax.psum_scatter(parts_attn, "tensor", scatter_dimension=0, tiled=False)
-    sum_down, sum_up = ring_sum([sum_down, sum_up], groups, 2, 1)
+    first_all = (dp_rank == 0).astype(jnp.float32) * (tp_rank == 0).astype(jnp.float32)
+    head_squares = first_all * (squares(grad_head_first) + squares(grad_head_second) + squares(grad_head_bias))
+    corner = (lax.broadcasted_iota(jnp.int32, (8, 128), 0) + lax.broadcasted_iota(jnp.int32, (8, 128), 1)) == 0
+    tile = jnp.where(corner, head_squares, 0.0)
+    (sum_down,), tile = ring_sum([sum_down], tile, groups, shards, 2, 0, 1)
+    (sum_up,), squared = ring_sum([sum_up], tile, groups, shards, 2, 0, 3)
     landed_first, sum_up = lax.optimization_barrier((landed_first, sum_up))
     zero_table = jnp.zeros((vocab_rows, cols), jnp.float32)
     grad_embedding = add_rows(landed_first, rows_first, zero_table)
@@ -893,12 +1056,13 @@
     def give_more(state):
         round_index, total = state
         wanted, rows, _ = serve(round_index)
-        return round_index + 1, add_rows(send_back(wanted), rows, total)
+        return round_index + 1, add_rows(trade(send_back(wanted)), rows, total)
 
     _, grad_embedding = lax.while_loop(more, give_more, (jnp.int32(1), grad_embedding))
 
+    squared = squared + jnp.where(corner, squares(grad_embedding), 0.0)
     sum_attn, grad_embedding = lax.optimization_barrier((sum_attn, grad_embedding))
-    (sum_attn,) = ring_sum([sum_attn], groups, 2, 2)
+    (sum_attn,), squared = ring_sum([sum_attn], squared, groups, shards, 2, 256, 2)
     sum_small = sum_attn[-256:].reshape(-1)[:small_size].reshape(grad_small.shape)
     grad_norms = sum_small[:8]
     grad_bias_qv = lax.dynamic_slice_in_dim(sum_small[8:10], tp_rank * cols, cols, 1)
@@ -907,28 +1071,7 @@
     grad_ffn_up, grad_ffn_down = sum_up, sum_down
     grad_pos = sum_attn[4 * width : -256]
 
-    first_dp = (dp_rank == 0).astype(jnp.float32)
-    first_all = first_dp * (tp_rank == 0).astype(jnp.float32)
-    local_squares = (
-        squares(grad_embedding)
-        + first_dp
-        * (
-            squares(sum_attn[:-256])
-            + squares(grad_ffn_up)
-            + squares(grad_ffn_down)
-            + squares(grad_bias_qv)
-            + squares(grad_bias_up)
-        )
-        + first_all
-        * (
-            squares(grad_norms)
-            + squares(grad_head_first)
-            + squares(grad_head_second)
-            + squares(grad_head_bias)
-        )
-    )
-    total_squares = cube_sum(jnp.broadcast_to(local_squares, (8, 128)), groups, shards, 4)[0, 0]
-    grad_norm = jnp.sqrt(total_squares)
+    grad_norm = jnp.sqrt(jnp.sum(squared))
     factor = jnp.minimum(1.0, CLIP_SCALE * math.sqrt(PARAMS) / (grad_norm + 1e-06))
     grad_positions = jnp.pad(grad_pos, ((2, positions.shape[0] - slots - 2), (0, 0)))
     grad_ffn = jnp.stack([grad_ffn_up, grad_ffn_down])

time: 1110 us -> 1030 us (0.928)
  matrix products: 312 us -> 24 us
  Pallas kernels: 486 us -> 740 us
  waiting for transfers between devices: 56.7 us -> 10.6 us
    dot_general x18 -> x0, matrix products: 288 us -> none  [product(): return jnp.einsum(subscripts, left, right, precision=PRODUCT)]
    pallas_call x4 -> x20, Pallas kernels: 396 us -> 649 us  [the longest x3 268 us: ring_sum(): pl.pallas_call(functools.partial(ring_kernel, groups, shards, parts, len(...]
    ppermute x3 -> x0, waiting for transfers between devices: 48.9 us -> none  [the longest x1 48.5 us: fast_on_device(): far_small = lax.ppermute(small, 'tensor', swap_pair)]
    reduce_scatter x2 -> x0, local copies, waits for them, and re-layouts: 11.5 us -> none  [the longest x1 6.07 us: fast_on_device(): lax.psum_scatter(grad_up, 'tensor', scatter_dimension=0, tiled=False)]
    unnamed x207 -> x201, local copies, waits for them, and re-layouts: 25.7 us -> 30 us
  transfers between devices with their start and end apart: 13 -> 10, of which waited for: 3 -> 2; matrix products, arithmetic and copies ran while one was open for 33% -> 13% of each run, Pallas kernels for 31% -> 56%
where the time goes in v3:
time: 1030 us; the launch traced here: 1020 us
  Pallas kernels  740 us (72%)
  other arithmetic  120 us (12%)
  local copies, waits for them, and re-layouts  83 us (8%)
  matrix products  24 us (2%)
  between operations  22.8 us (2%)
  starting transfers between devices  17.4 us (2%)
  waiting for transfers between devices  10.6 us (1%)
    pallas_call x3, Pallas kernels, ring_sum(): pl.pallas_call(functools.partial(ring_kernel, groups, shards, parts, len(...  268 us
    pallas_call x1, Pallas kernels, spread(): pl.pallas_call(functools.partial(spread_kernel, groups), out_shape=[jax.S...  108 us
    pallas_call x6, Pallas kernels, times(): pl.pallas_call(functools.partial(times_kernel, finish, len(extras)), grid...  95 us
    pallas_call x6, Pallas kernels, outer(): pl.pallas_call(outer_kernel, grid=(shards, columns // wide), in_specs=[pl...  89.7 us
    pallas_call x4, Pallas kernels, gather_back(): pl.pallas_call(functools.partial(gather_back_kernel, len(terms)), grid=(s...  87.4 us
    pallas_call x2, Pallas kernels, attend_call(): pl.pallas_call(functools.partial(kernel, slots, slots // 2), grid=(pairs,...  70.5 us
    sub x10, other arithmetic, advance(): weight - RATE * (DECAY * moment_new + (1.0 - DECAY) * clipped)  39.1 us
    unnamed x201, local copies, waits for them, and re-layouts  30 us
  transfers between devices with their start and end apart: 10, of which 2 were waited for; matrix products, arithmetic and copies ran while one was open for 13% of the time, Pallas kernels for 56%

profile of v3, /device:TPU:0, one launch (start us, length us, event | category | flops | bytes accessed | tf_op | source)
XLA Modules:
  0.0 1019.0 jit_solution(10052994082126393068)
XLA Ops:
  14.1 7.3 all-to-all-start.4
  21.4 10.0 fusion.74
  31.5 10.5 %gather_fusion.1 = f32[2816,256]{1,0:T(8,128)} fusion(f32[6304,256]{1,0:T(8,128)} %param.30, s32[3072]{0:T(1024)S(1)} %pad_clamp_fusion.1), kind=kCustom, calls=%fused_computation.1 | custom fusion | bytes 5778432 | tf_op jit(solution)/shard_map/jit(_take)/gather | solution.py:880
  52.0 108.4 %shard_map.390 = (f32[4,8,128,1024]{3,2,1,0:T(8,128)}, f32[4,520,256]{2,1,0:T(8,128)S(1)}) custom-call(f32[8,128,1024]{2,1,0:T(8,128)S(1)} %bitcast.155, f32[520,256]{1,0:T(8,128)S(1)} %select_maximum_fusion.small_ref), custom_call_target="tpu_custom_call" | custom-call | flops 1 | bytes 1024 | tf_op jit(solution)/shard_map/pallas_call | solution.py:503
  193.3 8.6 shard_map.391.q_ref
  203.6 10.5 %shard_map.392.k_ref = f32[4,1024,256]{2,1,0:T(8,128)S(1)} custom-call(f32[1024,1024]{1,0:T(8,128)} %pad_maximum_fusion.x_ref, f32[4,4,1024,256]{3,2,1,0:T(8,128)} %bitcast.164), custom_call_target="tpu_custom_call" | custom-call | flops 6442450944 | bytes 16777216 | tf_op jit(solution)/shard_map/pallas_call | solution.py:675
  216.1 10.5 %shard_map.393.v_ref = f32[4,1024,256]{2,1,0:T(8,128)S(1)} custom-call(f32[1024,1024]{1,0:T(8,128)} %pad_maximum_fusion.x_ref, f32[4,4,1024,256]{3,2,1,0:T(8,128)} %bitcast.165, f32[4,1,256]{2,1,0:T(1,128)S(1)} %get-tuple-element.414.refs_0_), custom_call_target="tpu_custom_call" | custom-call | flops 6442450944 | bytes 16777216 | tf_op jit(solution)/shard_map/pallas_call | solution.py:675
  228.7 33.3 %shard_map.394 = (f32[4,768,256]{2,1,0:T(8,128)S(1)}, f32[8,2,768]{2,1,0:T(2,128)S(1)}) custom-call(f32[4,768,256]{2,1,0:T(8,128)} %copy-done.18, f32[4,1024,256]{2,1,0:T(8,128)} %copy-done.12, f32[4,1024,256]{2,1,0:T(8,128)} %copy-done.13, f32[1024,1]{1,0:T(8,128)S(1)} %copy-done.25), custom_call_target="tpu_custom_call" | custom-call | flops 67645734912 | bytes 20971520 | tf_op jit(solution)/shard_map/pallas_call | solution.py:634
  263.6 8.5 shard_map.395
  275.3 29.2 %shard_map.396 = (f32[4,768,1024]{2,1,0:T(8,128)}, f32[4,768,1024]{2,1,0:T(8,128)}) custom-call(f32[768,1024]{1,0:T(8,128)S(1)} %get-tuple-element.401.x_ref, f32[4,1024,1024]{2,1,0:T(8,128)} %bitcast.230, f32[4,1,1024]{2,1,0:T(1,128)S(1)} %reshape_reshape.3.refs_0_), custom_call_target="tpu_custom_call" | custom-call | flops 19327352832 | bytes 16777216 | tf_op jit(solution)/shard_map/pallas_call | solution.py:675
  306.1 24.7 %shard_map.397 = f32[768,1024]{1,0:T(8,128)S(1)} custom-call(f32[768,1024]{1,0:T(8,128)} %get-tuple-element.400.base_ref, f32[4,768,1024]{2,1,0:T(8,128)} %get-tuple-element.296.refs_0_.d_ref, f32[4,1024,1024]{2,1,0:T(8,128)} %all-gather.4.cloned.1.call-done.refs_1_.w_ref), custom_call_target="tpu_custom_call" | custom-call | flops 19327352832 | bytes 16777216 | tf_op jit(solution)/shard_map/pallas_call | solution.py:733
  339.2 20.4 %shard_map.398 = f32[32,16,128]{2,1,0:T(8,128)} custom-call(f32[16,128]{1,0:T(8,128)} %reshape.653.x_ref), custom_call_target="tpu_custom_call" | custom-call | tf_op jit(solution)/shard_map/pallas_call | solution.py:293
  376.9 25.0 %shard_map.409 = f32[4,1024,1024]{2,1,0:T(8,128)} custom-call(f32[768,1024]{1,0:T(8,128)S(1)} %get-tuple-element.397.x_ref.base_ref, f32[4,768,1024]{2,1,0:T(8,128)} %get-tuple-element.296.refs_0_.d_ref), custom_call_target="tpu_custom_call" | custom-call | flops 19327352832 | bytes 16777216 | tf_op jit(solution)/shard_map/pallas_call | solution.py:763
  405.5 27.8 %shard_map.399 = (f32[4,768,1024]{2,1,0:T(8,128)}, f32[4,1,1024]{2,1,0:T(1,128)S(1)}) custom-call(f32[768,1024]{1,0:T(8,128)S(1)} %copy-done.20, f32[4,1024,1024]{2,1,0:T(8,128)} %all-gather.4.cloned.1.call-done.refs_1_.w_ref, f32[4,768,1024]{2,1,0:T(8,128)} %get-tuple-element.297.refs_0_), custom_call_target="tpu_custom_call" | custom-call | flops 19327352832 | bytes 16777216 | tf_op jit(solution)/shard_map/pallas_call | solution.py:675
  433.3 24.9 %shard_map.400 = f32[4,1024,1024]{2,1,0:T(8,128)} custom-call(f32[768,1024]{1,0:T(8,128)S(1)} %copy-done.22, f32[4,768,1024]{2,1,0:T(8,128)} %get-tuple-element.299.d_ref.refs_0_), custom_call_target="tpu_custom_call" | custom-call | flops 19327352832 | bytes 16777216 | tf_op jit(solution)/shard_map/pallas_call | solution.py:763
  458.3 24.9 %shard_map.401 = f32[768,1024]{1,0:T(8,128)S(1)} custom-call(f32[768,1024]{1,0:T(8,128)} %copy-done.19, f32[4,768,1024]{2,1,0:T(8,128)} %get-tuple-element.299.d_ref.refs_0_, f32[4,1024,1024]{2,1,0:T(8,128)} %bitcast.231), custom_call_target="tpu_custom_call" | custom-call | flops 19327352832 | bytes 16777216 | tf_op jit(solution)/shard_map/pallas_call | solution.py:733
  488.8 8.5 shard_map.402.d_ref
  498.9 37.2 %shard_map.403 = (f32[4,768,256]{2,1,0:T(8,128)S(1)}, f32[4,1024,256]{2,1,0:T(8,128)}, f32[4,1024,256]{2,1,0:T(8,128)}) custom-call(f32[4,768,256]{2,1,0:T(8,128)} %copy-done.18, f32[4,1024,256]{2,1,0:T(8,128)} %copy-done.12, f32[4,1024,256]{2,1,0:T(8,128)} %copy-done.13, f32[1024,1]{1,0:T(8,128)S(1)} %copy-done.26, f32[4,768,256]{2,1,0:T(8,128)} %copy-done.10, ...), custom_call_target="tpu_custom_call" | custom-call | flops 67645734912 | bytes 20971520 | tf_op jit(solution)/shard_map/pallas_call | solution.py:634
  536.2 29.3 %shard_map.404 = f32[1024,1024]{1,0:T(8,128)} custom-call(f32[1024,1024]{1,0:T(8,128)} %pad.21.base_ref, f32[4,768,256]{2,1,0:T(8,128)S(1)} %get-tuple-element.308.refs_0_.d_ref, f32[4,1024,256]{2,1,0:T(8,128)} %get-tuple-element.307.refs_1_.d_ref, f32[4,1024,256]{2,1,0:T(8,128)} %get-tuple-element.306.refs_2_.d_ref, f32[4,4,1024,256]{3,2,1,0:T(8,128)} %bitcast.168, ...), custom_call_target="tpu_custom_call" | custom-call | flops 17716740096 | bytes 16777216 | tf_op jit(solution)/shard_map/pallas_call | solution.py:733
  575.6 7.2 fusion.25
  608.8 8.9 shard_map.405.refs_0_
  617.7 10.9 %shard_map.406.refs_0_ = f32[4,4864,256]{2,1,0:T(8,128)} custom-call(f32[1024,1024]{1,0:T(8,128)S(1)} %copy-done, f32[4,1024,256]{2,1,0:T(8,128)} %get-tuple-element.307.refs_1_.d_ref, f32[4,4864,256]{2,1,0:T(8,128)} %shard_map.405.refs_0_), custom_call_target="tpu_custom_call", output_to_operand_aliasing={{}: (2, {})} | custom-call | flops 6442450944 | bytes 4194304 | tf_op jit(solution)/shard_map/pallas_call | solution.py:763
  628.6 10.8 %shard_map.407.refs_0_ = f32[4,4864,256]{2,1,0:T(8,128)} custom-call(f32[1024,1024]{1,0:T(8,128)S(1)} %copy-done, f32[4,1024,256]{2,1,0:T(8,128)} %get-tuple-element.306.refs_2_.d_ref, f32[4,4864,256]{2,1,0:T(8,128)} %shard_map.406.refs_0_), custom_call_target="tpu_custom_call", output_to_operand_aliasing={{}: (2, {})} | custom-call | flops 6442450944 | bytes 4194304 | tf_op jit(solution)/shard_map/pallas_call | solution.py:763
  639.3 9.3 shard_map.408
  651.3 6.5 all-to-all-done.6
  664.9 84.5 %shard_map.410 = (f32[8,128,1024]{2,1,0:T(8,128)S(1)}, f32[8,128]{1,0:T(8,128)S(1)}) custom-call(f32[8,128,1024]{2,1,0:T(8,128)} %bitcast.181, f32[8,128]{1,0:T(8,128)S(1)} %fusion.52.refs_1_), custom_call_target="tpu_custom_call" | custom-call | flops 1 | bytes 1024 | tf_op jit(solution)/shard_map/pallas_call | solution.py:415
  751.3 84.3 %shard_map.411 = (f32[8,128,1024]{2,1,0:T(8,128)S(1)}, f32[8,128]{1,0:T(8,128)S(1)}) custom-call(f32[8,128,1024]{2,1,0:T(8,128)} %bitcast.182, f32[8,128]{1,0:T(8,128)S(1)} %get-tuple-element.313.refs_1_), custom_call_target="tpu_custom_call" | custom-call | flops 1 | bytes 1024 | tf_op jit(solution)/shard_map/pallas_call | solution.py:415
  837.7 19.0 %scatter_custom_fusion.1 = f32[6304,256]{1,0:T(8,128)} fusion(s32[2816]{0:T(1024)S(1)} %fusion.51, f32[2816,256]{1,0:T(8,128)} %bitcast.46, f32[]{:T(128)} %constant.155.clone.1), kind=kCustom, calls=%fused_computation.45 | custom fusion | flops 720896 | bytes 6455808 | tf_op jit(solution)/shard_map/scatter-add | solution.py:1003
  863.3 99.4 %shard_map.412 = (f32[8,608,256]{2,1,0:T(8,128)S(1)}, f32[8,128]{1,0:T(8,128)S(1)}) custom-call(f32[8,608,256]{2,1,0:T(8,128)} %bitcast.180, f32[8,128]{1,0:T(8,128)S(1)} %select_add_fusion.refs_1_), custom_call_target="tpu_custom_call" | custom-call | flops 1 | bytes 1024 | tf_op jit(solution)/shard_map/pallas_call | solution.py:415
  979.1 6.7 multiply_subtract_fusion.2
  985.8 12.6 %multiply_subtract_fusion.1 = (f32[6304,256]{1,0:T(8,128)}, f32[6304,256]{1,0:T(8,128)}) fusion(f32[6304,256]{1,0:T(8,128)} %get-tuple-element.649, f32[6304,256]{1,0:T(8,128)} %get-tuple-element.320, f32[]{:T(128)S(6)} %min.3, f32[6304,256]{1,0:T(8,128)} %param.40), kind=kLoop, calls=%fused_computation.35 | loop fusion | flops 12910592 | bytes 32276484 | tf_op jit(solution)/shard_map/sub | solution.py:79
  999.7 11.5 %multiply_subtract_fusion = (f32[2,1024,1024]{2,1,0:T(8,128)}, f32[2,1024,1024]{2,1,0:T(8,128)}) fusion(f32[2,1024,1024]{2,1,0:T(8,128)} %param.33, f32[1,1024,1024]{2,1,0:T(8,128)S(1)} %bitcast.161, f32[1,1024,1024]{2,1,0:T(8,128)S(1)} %bitcast.162, f32[]{:T(128)S(6)} %min.3, f32[2,1024,1024]{2,1,0:T(8,128)} %param.43), kind=kLoop, calls=%fused_computation.33 | loop fusion | flops 18874368 | bytes 41943044 | tf_op jit(solution)/shard_map/sub | solution.py:79
  (354 shorter events, 165.3 us)
Async XLA Ops:
  7.2 186.2 %all-gather.6.cloned.1.call-start = ((), (), s32[]{:S(2)}) async-start(), calls=%async_computation.14 | async-start | bytes 20971520 | tf_op jit(solution)/shard_map/all_gather | solution.py:859
  13.4 154.4 %copy-start.83 = (s32[704]{0:T(1024)}, s32[704]{0:T(1024)S(1)}, u32[]{:S(2)}) copy-start(s32[704]{0:T(1024)S(1)} %broadcast_add_fusion.6) | copy-start | bytes 8452
  14.1 17.3 %all-to-all-start.4 = ((s32[32,1,128]{2,1,0:T(1,128)}), s32[32,1,128]{2,1,0:T(1,128)S(1)}, u32[]{:S(2)}, u32[]{:S(2)}) async-start(s32[32,1,128]{2,1,0:T(1,128)} %bitcast.15), calls=%async_computation.4 | async-start | bytes 32768 | tf_op jit(solution)/shard_map/all_to_all | solution.py:829
  42.0 119.3 %all-to-all-start.5 = ((f32[32,88,256]{2,1,0:T(8,128)}), f32[32,88,256]{2,1,0:T(8,128)}, u32[]{:S(2)}, u32[]{:S(2)}) async-start(f32[32,88,256]{2,1,0:T(8,128)} %bitcast.18), calls=%async_computation.5 | async-start | bytes 5767168 | tf_op jit(solution)/shard_map/all_to_all | solution.py:829
  48.0 258.1 %all-gather.4.cloned.1.call-start = ((), (), s32[]{:S(2)}) async-start(), calls=%async_computation.10 | async-start | bytes 20971520 | tf_op jit(solution)/shard_map/all_gather | solution.py:861
  48.8 616.1 %reduce-scatter.8.cloned.1.call-start = ((), (), s32[]{:S(2)}) async-start(), calls=%async_computation.13 | async-start | bytes 20971520 | tf_op jit(solution)/shard_map/reduce_scatter | solution.py:969
  49.8 128.3 %copy-start.66 = (f32[1,1024]{1,0:T(1,128)}, f32[1,1024]{1,0:T(1,128)S(1)}, u32[]{:S(2)}) copy-start(f32[1,1024]{1,0:T(1,128)S(1)} %get-tuple-element.426) | copy-start | bytes 12292
  180.5 12.8 %copy-start.6 = (f32[768,1024]{1,0:T(8,128)}, f32[768,1024]{1,0:T(8,128)S(1)}, u32[]{:S(2)}) copy-start(f32[768,1024]{1,0:T(8,128)S(1)} %get-tuple-element.403.x_ref) | copy-start | bytes 9437188
  181.7 7.9 collective-permute-start
  216.1 12.6 %copy-start.25 = (f32[1024,1]{1,0:T(8,128)S(1)}, f32[1024,1]{1,0:T(8,128)}, u32[]{:S(2)}) copy-start(f32[1024,1]{1,0:T(8,128)} %broadcast_select_fusion.bias_ref) | copy-start | bytes 12292
  337.5 27.5 %copy-start.50 = (f32[256,64]{0,1:T(8,128)S(1)}, f32[256,64]{0,1:T(8,128)}, u32[]{:S(2)}) copy-start(f32[256,64]{0,1:T(8,128)} %param.38) | copy-start | bytes 196612
  362.8 11.9 %copy-start.40 = (f32[48,1024]{1,0:T(8,128)}, f32[48,1024]{1,0:T(8,128)S(1)}, u32[]{:S(2)}) copy-start(f32[48,1024]{1,0:T(8,128)S(1)} %reshape.655) | copy-start | bytes 589828
  403.6 347.8 %reduce-scatter.6.cloned.1.call-start = ((), (), s32[]{:S(2)}) async-start(), calls=%async_computation.12 | async-start | bytes 20971520 | tf_op jit(solution)/shard_map/reduce_scatter | solution.py:975
  405.5 27.8 %copy-start.22 = (f32[768,1024]{1,0:T(8,128)S(1)}, f32[768,1024]{1,0:T(8,128)}, u32[]{:S(2)}) copy-start(f32[768,1024]{1,0:T(8,128)} %copy-done.21) | copy-start | bytes 9437188
  458.2 24.9 %copy-start.73 = (f32[1,1024]{1,0:T(1,128)S(1)}, f32[1,1024]{1,0:T(1,128)}, u32[]{:S(2)}) copy-start(f32[1,1024]{1,0:T(1,128)} %get-tuple-element.423) | copy-start | bytes 12292
  458.2 24.9 %copy-start.75 = (f32[768]{0:T(1024)S(1)}, f32[768]{0:T(1024)}, u32[]{:S(2)}) copy-start(f32[768]{0:T(1024)} %copy-done.74) | copy-start | bytes 9220
  536.2 29.4 %copy-start.8 = (f32[4,768,256]{2,1,0:T(8,128)}, f32[4,768,256]{2,1,0:T(8,128)S(1)}, u32[]{:S(2)}) copy-start(f32[4,768,256]{2,1,0:T(8,128)S(1)} %get-tuple-element.308.refs_0_.d_ref) | copy-start | bytes 9437188
  536.2 33.4 %copy-start.30 = (f32[768,1024]{1,0:T(8,128)S(1)}, f32[768,1024]{1,0:T(8,128)}, u32[]{:S(2)}) copy-start(f32[768,1024]{1,0:T(8,128)} %copy-done.29) | copy-start | bytes 9437188
  536.2 33.4 %copy-start.63 = (f32[768]{0:T(1024)S(1)}, f32[768]{0:T(1024)}, u32[]{:S(2)}) copy-start(f32[768]{0:T(1024)} %copy-done.62) | copy-start | bytes 9220
  536.2 33.4 %copy-start.67 = (f32[1,1024]{1,0:T(1,128)S(1)}, f32[1,1024]{1,0:T(1,128)}, u32[]{:S(2)}) copy-start(f32[1,1024]{1,0:T(1,128)} %copy-done.66) | copy-start | bytes 12292
  536.2 33.4 %copy-start.70 = (f32[768]{0:T(1024)S(1)}, f32[768]{0:T(1024)}, u32[]{:S(2)}) copy-start(f32[768]{0:T(1024)} %copy-done.69) | copy-start | bytes 9220
  566.9 2.7 collective-permute-start.1
  588.1 69.7 %all-to-all-start.6 = ((f32[32,88,256]{2,1,0:T(8,128)}), f32[32,88,256]{2,1,0:T(8,128)}, u32[]{:S(2)}, u32[]{:S(2)}) async-start(f32[32,88,256]{2,1,0:T(8,128)} %bitcast.45), calls=%async_computation.6 | async-start | bytes 5767168 | tf_op jit(solution)/shard_map/all_to_all | solution.py:829
  591.6 271.7 %reduce-scatter.4.cloned.1.call-start = ((), (), s32[]{:S(2)}) async-start(), calls=%async_computation.11 | async-start | bytes 24903680 | tf_op jit(solution)/shard_map/reduce_scatter | solution.py:1045
  837.7 19.0 %copy-start.49 = (s32[768]{0:T(1024)S(1)}, s32[768]{0:T(1024)}, u32[]{:S(2)}) copy-start(s32[768]{0:T(1024)} %copy-done.48) | copy-start | bytes 9220
  837.7 19.0 %copy-start.53 = (s32[768]{0:T(1024)S(1)}, s32[768]{0:T(1024)}, u32[]{:S(2)}) copy-start(s32[768]{0:T(1024)} %copy-done.52) | copy-start | bytes 9220
  985.8 12.7 %copy-start.88 = (f32[2,256]{1,0:T(2,128)S(1)}, f32[2,256]{1,0:T(2,128)}, u32[]{:S(2)}) copy-start(f32[2,256]{1,0:T(2,128)} %param.34) | copy-start | bytes 6148
  985.8 12.7 %copy-start.97 = (f32[2,256]{1,0:T(2,128)S(1)}, f32[2,256]{1,0:T(2,128)}, u32[]{:S(2)}) copy-start(f32[2,256]{1,0:T(2,128)} %param.44) | copy-start | bytes 6148
  985.8 13.3 %copy-start.86 = (f32[1024]{0:T(1024)S(1)}, f32[1024]{0:T(1024)}, u32[]{:S(2)}) copy-start(f32[1024]{0:T(1024)} %param.35) | copy-start | bytes 12292
  985.8 13.3 %copy-start.91 = (f32[1024]{0:T(1024)S(1)}, f32[1024]{0:T(1024)}, u32[]{:S(2)}) copy-start(f32[1024]{0:T(1024)} %param.45) | copy-start | bytes 12292
  985.8 13.9 %copy-start.15 = (f32[8,128,1024]{2,1,0:T(8,128)S(1)}, f32[8,128,1024]{2,1,0:T(8,128)}, u32[]{:S(2)}) copy-start(f32[8,128,1024]{2,1,0:T(8,128)} %copy-done.14) | copy-start | bytes 12582916
  985.8 13.9 %copy-start.17 = (f32[8,128,1024]{2,1,0:T(8,128)S(1)}, f32[8,128,1024]{2,1,0:T(8,128)}, u32[]{:S(2)}) copy-start(f32[8,128,1024]{2,1,0:T(8,128)} %copy-done.16) | copy-start | bytes 12582916
  (75 other events, 262.7 us)
Sparse Core Ops, SparseCore 0:
  9.6 162.2 all-gather.5
  174.0 105.8 all-gather.3
  403.7 124.2 reduce-scatter.7
  530.6 157.0 reduce-scatter.5
  690.1 146.2 reduce-scatter.3

commit v4 on v3

--- a/solution.py
+++ b/solution.py
@@ -20,6 +20,7 @@
 HIGH = lax.Precision.HIGHEST
 PRODUCT = lax.Precision.HIGH
 CAPACITY = 88
+SMALL_ROWS = 64
 
 
 def precise_product(left, right):
@@ -335,9 +336,10 @@
     greet([device_at(place + 1), device_at(place - 1), *partners])
     streams = []
     for array in range(arrays):
-        rows = inputs[array].shape[1] // (2 * parts)
+        tiles = inputs[array].shape[1] // 8
+        edges = [8 * (tiles * part // (2 * parts)) for part in range(2 * parts + 1)]
         for part in range(2 * parts):
-            streams.append((array, 1 - 2 * (part % 2), part * rows, rows))
+            streams.append((array, 1 - 2 * (part % 2), edges[part], edges[part + 1] - edges[part]))
 
     def chunk(step, way):
         return (place + groups * 2 - way * step) % groups
@@ -553,17 +555,30 @@
     high_k, low_k = halves(k_ref[0])
     twice_k = jnp.concatenate([high_k, high_k], axis=1)
     high_v, low_v = halves(v_ref[0].T)
-    for start in range(0, q_ref.shape[1], tile):
-        rows = pl.ds(start, tile)
+    def scores_of(start):
         first = 0 if start < slots else slots
         keys = slice(first, first + slots)
         found = []
         for head in range(2):
-            high_q, low_q = halves(one_head(q_ref[0, rows] * scale, head))
-            scores = score_tile(twice_k[keys], low_k[keys], high_q, low_q, bias_ref[pl.ds(first, slots)])
-            peak = jnp.max(scores, axis=0, keepdims=True)
-            probs = jnp.exp(scores - peak)
-            total = jnp.sum(probs, axis=0, keepdims=True)
+            high_q, low_q = halves(one_head(q_ref[0, pl.ds(start, tile)] * scale, head))
+            found.append(score_tile(twice_k[keys], low_k[keys], high_q, low_q, bias_ref[pl.ds(first, slots)]))
+        return found
+
+    starts = list(range(0, q_ref.shape[1], tile))
+    ready = scores_of(starts[0])
+    for index, start in enumerate(starts):
+        rows = pl.ds(start, tile)
+        first = 0 if start < slots else slots
+        keys = slice(first, first + slots)
+        score_pair = ready
+        if index + 1 < len(starts):
+            ready = scores_of(starts[index + 1])
+        peaks = [jnp.max(jnp.max(s.reshape(8, -1, tile), axis=0), axis=0, keepdims=True) for s in score_pair]
+        pairs = [jnp.exp(s - p) for s, p in zip(score_pair, peaks)]
+        found = []
+        for head in range(2):
+            peak, probs = peaks[head], pairs[head]
+            total = jnp.sum(jnp.sum(probs.reshape(8, -1, tile), axis=0), axis=0, keepdims=True)
             lse_ref[0, pl.ds(head, 1), rows] = peak + jnp.log(total)
             high_p, low_p = halves(probs)
             lanes = slice(head * HEAD_DIM, (head + 1) * HEAD_DIM)
@@ -705,12 +720,57 @@
     outs[1][0] = jnp.sum(tile, axis=0, keepdims=True)
 
 
+def project_kernel(count, x_ref, y_ref, wq_ref, wk_ref, wv_ref, bq_ref, bv_ref, q_ref, k_ref, v_ref, high, low):
+    @pl.when(pl.program_id(0) == 0)
+    def _():
+        high[:count], low[:count] = halves(x_ref[...])
+        high[count:], low[count:] = halves(y_ref[...])
+
+    q_ref[0] = dot_three(high[:count], low[:count], wq_ref[0, 0], dot_plain) + bq_ref[0]
+    k_ref[0] = dot_three(high[...], low[...], wk_ref[0, 0], dot_plain)
+    v_ref[0] = dot_three(high[...], low[...], wv_ref[0, 0], dot_plain) + bv_ref[0]
+
+
+def project(x, y, w, bias_q, bias_v):
+    count, depth = x.shape
+    rows = count + y.shape[0]
+    shards, _, _, columns = w.shape
+
+    def weight(which):
+        return pl.BlockSpec((1, 1, depth, columns), lambda j: (j, which, 0, 0))
+
+    def tile(height):
+        return pl.BlockSpec((1, height, columns), lambda j: (j, 0, 0))
+
+    return pl.pallas_call(
+        functools.partial(project_kernel, count),
+        grid=(shards,),
+        in_specs=[
+            pl.BlockSpec(x.shape, lambda j: (0, 0)),
+            pl.BlockSpec(y.shape, lambda j: (0, 0)),
+            *[weight(which) for which in range(3)],
+            tile(1),
+            tile(1),
+        ],
+        out_specs=[tile(count), tile(rows), tile(rows)],
+        out_shape=[jax.ShapeDtypeStruct((shards, n, columns), jnp.float32) for n in (count, rows, rows)],
+        scratch_shapes=[pltpu.VMEM((rows, depth), jnp.bfloat16)] * 2,
+        compiler_params=pltpu.CompilerParams(vmem_limit_bytes=48 << 20),
+        cost_estimate=pl.CostEstimate(
+            flops=6 * (count + 2 * rows) * depth * shards * columns, bytes_accessed=24 << 20, transcendentals=0
+        ),
+    )(x, y, w, w, w, bias_q, bias_v)
+
+
 def gather_back_kernel(count, base_ref, *refs):
     out = refs[-1]
 
     @pl.when((pl.program_id(0) == 0) & (pl.program_id(1) == 0))
     def _():
-        out[...] = base_ref[...]
+        filled = base_ref.shape[0]
+        out[:filled] = base_ref[...]
+        if filled < out.shape[0]:
+            out[filled:] = jnp.zeros((out.shape[0] - filled, out.shape[1]), jnp.float32)
 
     for a_ref, w_ref in zip(refs[:count], refs[count : 2 * count]):
         high, low = halves(a_ref[0])
@@ -723,6 +783,7 @@
     arrays = [array for array, _, _ in terms]
     shards, _, columns = arrays[0].shape
     wide = min(WIDE, columns)
+    total = (max(array.shape[1] for array in arrays), base.shape[1])
 
     def w_spec(w, which):
         if w.ndim == 4:
@@ -738,8 +799,8 @@
             *[pl.BlockSpec((1, a.shape[1], wide), lambda j, c: (j, 0, c)) for a in arrays],
             *[w_spec(w, which) for _, w, which in terms],
         ],
-        out_specs=pl.BlockSpec(base.shape, lambda j, c: (0, 0)),
-        out_shape=jax.ShapeDtypeStruct(base.shape, jnp.float32),
+        out_specs=pl.BlockSpec(total, lambda j, c: (0, 0)),
+        out_shape=jax.ShapeDtypeStruct(total, jnp.float32),
         compiler_params=pltpu.CompilerParams(vmem_limit_bytes=48 << 20),
         cost_estimate=pl.CostEstimate(flops=work, bytes_accessed=16 << 20, transcendentals=0),
     )(base, *arrays, *[w for _, w, _ in terms])
@@ -779,6 +840,99 @@
     )(x, d, *held)
 
 
+def outer_three_kernel(count, x_ref, y_ref, q_ref, k_ref, v_ref, out, high, low):
+    @pl.when(pl.program_id(0) == 0)
+    def _():
+        high[:, :count], low[:, :count] = halves(x_ref[...].T)
+        high[:, count:], low[:, count:] = halves(y_ref[...].T)
+
+    depth = high.shape[0]
+    out[0, pl.ds(0, depth)] = dot_three(high[:, :count], low[:, :count], q_ref[0], dot_plain)
+    out[0, pl.ds(depth, depth)] = dot_three(high[...], low[...], k_ref[0], dot_plain)
+    out[0, pl.ds(2 * depth, depth)] = dot_three(high[...], low[...], v_ref[0], dot_plain)
+
+
+def outer_three(x, y, back_q, back_k, back_v, rows):
+    shards, tokens, columns = back_k.shape
+    count, depth = x.shape
+
+    def tile(height):
+        return pl.BlockSpec((1, height, columns), lambda j: (j, 0, 0))
+
+    return pl.pallas_call(
+        functools.partial(outer_three_kernel, count),
+        grid=(shards,),
+        in_specs=[
+            pl.BlockSpec(x.shape, lambda j: (0, 0)),
+            pl.BlockSpec(y.shape, lambda j: (0, 0)),
+            tile(count),
+            tile(tokens),
+            tile(tokens),
+        ],
+        out_specs=tile(3 * depth),
+        out_shape=jax.ShapeDtypeStruct((shards, rows, columns), jnp.float32),
+        scratch_shapes=[pltpu.VMEM((depth, tokens), jnp.bfloat16)] * 2,
+        compiler_params=pltpu.CompilerParams(vmem_limit_bytes=48 << 20),
+        cost_estimate=pl.CostEstimate(
+            flops=6 * (count + 2 * tokens) * depth * shards * columns, bytes_accessed=24 << 20, transcendentals=0
+        ),
+    )(x, y, back_q, back_k, back_v)
+
+
+def thirds(array):
+    high, rest = array.astype(jnp.bfloat16), None
+    rest = array - high.astype(jnp.float32)
+    middle = rest.astype(jnp.bfloat16)
+    return high, middle, (rest - middle.astype(jnp.float32)).astype(jnp.bfloat16)
+
+
+def select_rows(column, row, block):
+    chosen = jnp.where(column == row, 1.0, 0.0).astype(jnp.bfloat16)
+    high, middle, low = thirds(block)
+    return dot_plain(chosen, high) + dot_plain(chosen, middle) + dot_plain(chosen, low)
+
+
+def pack_kernel(wanted_ref, ids_ref, x_ref, o_ref):
+    o_ref[...] = select_rows(wanted_ref[...], ids_ref[...], x_ref[...]).reshape(o_ref.shape)
+
+
+def pack(wanted, ids, rows, groups, shards):
+    cols = rows.shape[1] // shards
+    return pl.pallas_call(
+        pack_kernel,
+        grid=(shards,),
+        in_specs=[
+            pl.BlockSpec((wanted.shape[0], 1), lambda j: (0, 0)),
+            pl.BlockSpec((1, ids.shape[0]), lambda j: (0, 0)),
+            pl.BlockSpec((ids.shape[0], cols), lambda j: (0, j)),
+        ],
+        out_specs=pl.BlockSpec((groups, 1, CAPACITY, cols), lambda j: (0, j, 0, 0)),
+        out_shape=jax.ShapeDtypeStruct((groups, shards, CAPACITY, cols), jnp.float32),
+        compiler_params=pltpu.CompilerParams(vmem_limit_bytes=32 << 20),
+    )(wanted[:, None], ids[None, :], rows)
+
+
+def expand_kernel(ids_ref, wanted_ref, x_ref, o_ref):
+    block = x_ref[...].reshape(wanted_ref.shape[1], x_ref.shape[-1])
+    o_ref[...] = select_rows(ids_ref[...], wanted_ref[...], block)
+
+
+def expand_rows(ids, wanted, landed):
+    groups, shards, _, cols = landed.shape
+    return pl.pallas_call(
+        expand_kernel,
+        grid=(shards,),
+        in_specs=[
+            pl.BlockSpec((ids.shape[0], 1), lambda j: (0, 0)),
+            pl.BlockSpec((1, wanted.shape[0]), lambda j: (0, 0)),
+            pl.BlockSpec((groups, 1, CAPACITY, cols), lambda j: (0, j, 0, 0)),
+        ],
+        out_specs=pl.BlockSpec((ids.shape[0], cols), lambda j: (0, j)),
+        out_shape=jax.ShapeDtypeStruct((ids.shape[0], shards * cols), jnp.float32),
+        compiler_params=pltpu.CompilerParams(vmem_limit_bytes=32 << 20),
+    )(ids[:, None], wanted[None, :], landed)
+
+
 def normalise(values):
     center = values - jnp.mean(values, axis=-1, keepdims=True)
     scale = lax.rsqrt(jnp.mean(center * center, axis=-1, keepdims=True) + EPS)
@@ -880,10 +1034,7 @@
         return jnp.take(embedding, rows, axis=0, mode="clip")
 
     def expand(wanted, landed):
-        landed = landed.reshape(groups, shards, CAPACITY, cols)
-        landed = landed.transpose(0, 2, 1, 3).reshape(groups * CAPACITY, width)
-        chosen = (ids[:, None] == wanted[None, :]).astype(jnp.float32)
-        return jnp.matmul(chosen, landed, precision=HIGH)
+        return expand_rows(ids, wanted, landed.reshape(groups, shards, CAPACITY, cols))
 
     wanted_first, rows_first, rounds = serve(0)
     found, up_weights = lax.optimization_barrier((find(rows_first), ffn_weights[0]))
@@ -910,12 +1061,8 @@
     h_zero = unit_zero * norms[0] + norms[1]
 
     h_other = lax.ppermute(h_zero[slots:], "tensor", swap)
-    h_keys = jnp.concatenate([h_zero, h_other], axis=0)
     bias_q, bias_v = all_small[:, slots], all_small[:, slots + 1]
-    keys_shape = (shards, count + half, cols)
-    (queries,) = times(h_zero, all_attn, 0, add_row, [bias_q[:, None, :]], [(shards, count, cols)])
-    (keys_all,) = times(h_keys, all_attn, 1, keep_tile, [], [keys_shape])
-    (values,) = times(h_keys, all_attn, 2, add_row, [bias_v[:, None, :]], [keys_shape])
+    queries, keys_all, values = project(h_zero, h_other, all_attn, bias_q[:, None, :], bias_v[:, None, :])
     key_index = lax.broadcasted_iota(jnp.int32, (slots,), 0)
     own_first = jnp.where(
         key_index < half, side * half + key_index, (1 - side) * half + key_index - half
@@ -983,9 +1130,8 @@
         (queries, keys_all, values, key_bias, mixed, lse, back_mixed),
         (queries.shape, keys_all.shape, values.shape),
     )
-    base_keys = jnp.pad(back_x_one, ((0, half), (0, 0)))
     back_keys = gather_back(
-        base_keys, [(back_q, all_attn, 0), (back_k, all_attn, 1), (back_v, all_attn, 2)]
+        back_x_one, [(back_q, all_attn, 0), (back_k, all_attn, 1), (back_v, all_attn, 2)]
     )
     back_other = lax.ppermute(back_keys[count:], "tensor", swap)
     back_h_zero = back_keys[:count]
@@ -993,10 +1139,7 @@
     back_embedded, grad_gain_zero, grad_shift_zero = normalise_back(back_h_zero, norms[0], unit_zero, scale_zero)
 
     def send_back(wanted):
-        chosen = (wanted[:, None] == ids[None, :]).astype(jnp.float32)
-        summed = jnp.matmul(chosen, back_embedded, precision=HIGH)
-        parts = summed.reshape(groups, CAPACITY, shards, cols).transpose(0, 2, 1, 3)
-        return parts.reshape(devices * CAPACITY, cols)
+        return pack(wanted, ids, back_embedded, groups, shards).reshape(devices * CAPACITY, cols)
 
     def add_rows(landed, rows, total):
         target = jnp.where(rows >= 0, rows, vocab_rows)
@@ -1006,10 +1149,8 @@
         (send_back(wanted_first), back_q, back_k, back_v, back_x_one)
     )
     landed_first = trade(leaving)
-    part_rows = 4 * width + slots + 256
-    parts_attn = outer(h_zero, back_q, part_rows, 0)
-    parts_attn = outer(h_keys, back_k, part_rows, 1, parts_attn)
-    parts_attn = outer(h_keys, back_v, part_rows, 2, parts_attn)
+    part_rows = 4 * width + slots + SMALL_ROWS
+    parts_attn = outer_three(h_zero, h_other, back_q, back_k, back_v, part_rows)
     parts_attn = outer(back_x_one, mixed, part_rows, 3, parts_attn)
     grad_small = jnp.concatenate(
         [
@@ -1037,8 +1178,8 @@
     grad_pos_parts = grad_pos_full.reshape(slots, shards, cols)
     grad_pos_parts = grad_pos_parts.transpose(1, 0, 2)
     small_size = grad_small.size
-    small_rows = jnp.pad(grad_small.reshape(-1), (0, 256 * cols - small_size)).reshape(1, 256, cols)
-    small_rows = jnp.broadcast_to(small_rows, (shards, 256, cols))
+    small_rows = jnp.pad(grad_small.reshape(-1), (0, SMALL_ROWS * cols - small_size)).reshape(1, SMALL_ROWS, cols)
+    small_rows = jnp.broadcast_to(small_rows, (shards, SMALL_ROWS, cols))
     parts_attn = lax.dynamic_update_slice(parts_attn, grad_pos_parts, (0, 4 * width, 0))
     parts_attn = lax.dynamic_update_slice(parts_attn, small_rows, (0, 4 * width + slots, 0))
     landed_first, parts_attn = lax.optimization_barrier((landed_first, parts_attn))
@@ -1062,14 +1203,14 @@
 
     squared = squared + jnp.where(corner, squares(grad_embedding), 0.0)
     sum_attn, grad_embedding = lax.optimization_barrier((sum_attn, grad_embedding))
-    (sum_attn,), squared = ring_sum([sum_attn], squared, groups, shards, 2, 256, 2)
-    sum_small = sum_attn[-256:].reshape(-1)[:small_size].reshape(grad_small.shape)
+    (sum_attn,), squared = ring_sum([sum_attn], squared, groups, shards, 2, SMALL_ROWS, 2)
+    sum_small = sum_attn[-SMALL_ROWS:].reshape(-1)[:small_size].reshape(grad_small.shape)
     grad_norms = sum_small[:8]
     grad_bias_qv = lax.dynamic_slice_in_dim(sum_small[8:10], tp_rank * cols, cols, 1)
     grad_bias_up = lax.dynamic_slice_in_dim(sum_small[10:].reshape(-1), tp_rank * hidden, hidden)
-    grad_attn = sum_attn[: 4 * width].reshape(4, width, cols)
+    grad_attn = sum_attn[: 4 * width]
     grad_ffn_up, grad_ffn_down = sum_up, sum_down
-    grad_pos = sum_attn[4 * width : -256]
+    grad_pos = sum_attn[4 * width : -SMALL_ROWS]
 
     grad_norm = jnp.sqrt(jnp.sum(squared))
     factor = jnp.minimum(1.0, CLIP_SCALE * math.sqrt(PARAMS) / (grad_norm + 1e-06))
@@ -1077,7 +1218,8 @@
     grad_ffn = jnp.stack([grad_ffn_up, grad_ffn_down])
     new_embedding, next_embedding = advance(embedding, mom_embedding, grad_embedding, factor)
     new_positions, next_positions = advance(positions, mom_positions, grad_positions, factor)
-    new_attn, next_attn = advance(attn_weights, mom_attn, grad_attn, factor)
+    flat_attn, flat_mom = attn_weights.reshape(-1, cols), mom_attn.reshape(-1, cols)
+    new_attn, next_attn = (x.reshape(attn_weights.shape) for x in advance(flat_attn, flat_mom, grad_attn, factor))
     new_ffn, next_ffn = advance(ffn_weights, ffn_momentum, grad_ffn, factor)
     new_bias_qv, next_bias_qv = advance(bias_qv, mom_bias_qv, grad_bias_qv, factor)
     new_bias_up, next_bias_up = advance(bias_up, mom_bias_up, grad_bias_up, factor)

time: 1030 us -> 991 us (0.962)
  Pallas kernels: 740 us -> 719 us
  matrix products: 24 us -> 11.2 us
  waiting for transfers between devices: 10.6 us -> 23.2 us
  local copies, waits for them, and re-layouts: 83 us -> 70.7 us
    pallas_call x0 -> x4, Pallas kernels: none -> 59.8 us  [the longest x1 24.3 us: project(): pl.pallas_call(functools.partial(project_kernel, count), grid=(shards,),...]
    pallas_call x6 -> x3, Pallas kernels: 89.7 us -> 58.9 us  [outer(): pl.pallas_call(outer_kernel, grid=(shards, columns // wide), in_specs=[pl...]
    pallas_call x6 -> x3, Pallas kernels: 95 us -> 65.7 us  [times(): pl.pallas_call(functools.partial(times_kernel, finish, len(extras)), grid...]
    pallas_call x2, Pallas kernels: 70.5 us -> 57.1 us  [attend_call(): pl.pallas_call(functools.partial(kernel, slots, slots // 2), grid=(pairs,...]
    all_to_all x3, waiting for transfers between devices: 6.5 us -> 19.9 us  [trade(): return lax.all_to_all(block, ('dp', 'tensor'), 0, 0, tiled=True)]
    dot_general x2 -> x0, matrix products: 12.8 us -> none  [the longest x1 7.17 us: send_back(): summed = jnp.matmul(chosen, back_embedded, precision=HIGH)]
    unnamed x201 -> x190, local copies, waits for them, and re-layouts: 30 us -> 29.9 us
  transfers between devices with their start and end apart: 10 -> 10, of which waited for: 2 -> 3; matrix products, arithmetic and copies ran while one was open for 13% -> 11% of each run, Pallas kernels for 56% -> 56%
where the time goes in v4:
time: 991 us; the launch traced here: 982 us
  Pallas kernels  719 us (73%)
  other arithmetic  119 us (12%)
  local copies, waits for them, and re-layouts  70.7 us (7%)
  waiting for transfers between devices  23.2 us (2%)
  between operations  23 us (2%)
  starting transfers between devices  14.4 us (1%)
  matrix products  11.2 us (1%)
    pallas_call x3, Pallas kernels, ring_sum(): pl.pallas_call(functools.partial(ring_kernel, groups, shards, parts, len(...  266 us
    pallas_call x1, Pallas kernels, spread(): pl.pallas_call(functools.partial(spread_kernel, groups), out_shape=[jax.S...  108 us
    pallas_call x4, Pallas kernels, gather_back(): pl.pallas_call(functools.partial(gather_back_kernel, len(terms)), grid=(s...  83.3 us
    pallas_call x3, Pallas kernels, times(): pl.pallas_call(functools.partial(times_kernel, finish, len(extras)), grid...  65.7 us
    pallas_call x3, Pallas kernels, outer(): pl.pallas_call(outer_kernel, grid=(shards, columns // wide), in_specs=[pl...  58.9 us
    pallas_call x2, Pallas kernels, attend_call(): pl.pallas_call(functools.partial(kernel, slots, slots // 2), grid=(pairs,...  57.1 us
    sub x10, other arithmetic, advance(): weight - RATE * (DECAY * moment_new + (1.0 - DECAY) * clipped)  39.2 us
    unnamed x190, local copies, waits for them, and re-layouts  29.9 us
  transfers between devices with their start and end apart: 10, of which 3 were waited for; matrix products, arithmetic and copies ran while one was open for 11% of the time, Pallas kernels for 56%

profile of v4, /device:TPU:0, one launch (start us, length us, event | category | flops | bytes accessed | tf_op | source)
XLA Modules:
  0.0 982.1 jit_solution(3941873293894763860)
XLA Ops:
  8.0 8.5 fusion.55
  22.7 7.3 all-to-all-start.4
  30.0 7.1 all-to-all-done.4
  37.2 10.7 %gather_fusion.1 = f32[2816,256]{1,0:T(8,128)} fusion(f32[6304,256]{1,0:T(8,128)} %param.30, s32[3072]{0:T(1024)S(1)} %pad_clamp_fusion.1), kind=kCustom, calls=%fused_computation.1 | custom fusion | bytes 5778432 | tf_op jit(solution)/shard_map/jit(_take)/gather | solution.py:1034
  55.1 108.4 %shard_map.390 = (f32[4,8,128,1024]{3,2,1,0:T(8,128)}, f32[4,520,256]{2,1,0:T(8,128)S(1)}) custom-call(f32[8,128,1024]{2,1,0:T(8,128)S(1)} %bitcast.142, f32[520,256]{1,0:T(8,128)S(1)} %select_maximum_fusion.small_ref), custom_call_target="tpu_custom_call" | custom-call | flops 1 | bytes 1024 | tf_op jit(solution)/shard_map/pallas_call | solution.py:505
  167.5 5.7 shard_map.391
  190.6 24.3 %shard_map.392 = (f32[4,768,256]{2,1,0:T(8,128)S(1)}, f32[4,1024,256]{2,1,0:T(8,128)}, f32[4,1024,256]{2,1,0:T(8,128)}) custom-call(f32[768,1024]{1,0:T(8,128)} %copy-done.8, f32[256,1024]{1,0:T(8,128)} %collective-permute-done.y_ref, f32[4,4,1024,256]{3,2,1,0:T(8,128)} %bitcast.152, f32[4,4,1024,256]{3,2,1,0:T(8,128)} %bitcast.153, ...), custom_call_target="tpu_custom_call" | custom-call | flops 17716740096 | bytes 25165824 | tf_op jit(solution)/shard_map/pallas_call | solution.py:745
  216.6 19.8 %shard_map.393 = (f32[4,768,256]{2,1,0:T(8,128)S(1)}, f32[8,2,768]{2,1,0:T(2,128)S(1)}) custom-call(f32[4,768,256]{2,1,0:T(8,128)} %copy-done.23, f32[4,1024,256]{2,1,0:T(8,128)} %get-tuple-element.297.k_ref, f32[4,1024,256]{2,1,0:T(8,128)} %get-tuple-element.298.v_ref, f32[1024,1]{1,0:T(8,128)S(1)} %copy-done.21), custom_call_target="tpu_custom_call" | custom-call | flops 67645734912 | bytes 20971520 | tf_op jit(solution)/shard_map/pallas_call | solution.py:649
  238.0 8.5 shard_map.394
  249.7 29.2 %shard_map.395 = (f32[4,768,1024]{2,1,0:T(8,128)}, f32[4,768,1024]{2,1,0:T(8,128)}) custom-call(f32[768,1024]{1,0:T(8,128)S(1)} %get-tuple-element.406.x_ref, f32[4,1024,1024]{2,1,0:T(8,128)} %bitcast.217, f32[4,1,1024]{2,1,0:T(1,128)S(1)} %reshape_reshape.3.refs_0_), custom_call_target="tpu_custom_call" | custom-call | flops 19327352832 | bytes 16777216 | tf_op jit(solution)/shard_map/pallas_call | solution.py:690
  280.6 24.7 %shard_map.396 = f32[768,1024]{1,0:T(8,128)S(1)} custom-call(f32[768,1024]{1,0:T(8,128)} %get-tuple-element.405.base_ref, f32[4,768,1024]{2,1,0:T(8,128)} %get-tuple-element.301.refs_0_.d_ref, f32[4,1024,1024]{2,1,0:T(8,128)} %all-gather.4.cloned.1.call-done.refs_1_.w_ref), custom_call_target="tpu_custom_call" | custom-call | flops 19327352832 | bytes 16777216 | tf_op jit(solution)/shard_map/pallas_call | solution.py:794
  313.6 20.3 %shard_map.397 = f32[32,16,128]{2,1,0:T(8,128)} custom-call(f32[16,128]{1,0:T(8,128)} %reshape.668.x_ref), custom_call_target="tpu_custom_call" | custom-call | tf_op jit(solution)/shard_map/pallas_call | solution.py:294
  351.2 25.0 %shard_map.407 = f32[4,1024,1024]{2,1,0:T(8,128)} custom-call(f32[768,1024]{1,0:T(8,128)S(1)} %get-tuple-element.402.x_ref.base_ref, f32[4,768,1024]{2,1,0:T(8,128)} %get-tuple-element.301.refs_0_.d_ref), custom_call_target="tpu_custom_call" | custom-call | flops 19327352832 | bytes 16777216 | tf_op jit(solution)/shard_map/pallas_call | solution.py:824
  379.8 27.8 %shard_map.398 = (f32[4,768,1024]{2,1,0:T(8,128)}, f32[4,1,1024]{2,1,0:T(1,128)S(1)}) custom-call(f32[768,1024]{1,0:T(8,128)S(1)} %copy-done.16, f32[4,1024,1024]{2,1,0:T(8,128)} %all-gather.4.cloned.1.call-done.refs_1_.w_ref, f32[4,768,1024]{2,1,0:T(8,128)} %get-tuple-element.302.refs_0_), custom_call_target="tpu_custom_call" | custom-call | flops 19327352832 | bytes 16777216 | tf_op jit(solution)/shard_map/pallas_call | solution.py:690
  407.6 25.0 %shard_map.399 = f32[4,1024,1024]{2,1,0:T(8,128)} custom-call(f32[768,1024]{1,0:T(8,128)S(1)} %copy-done.18, f32[4,768,1024]{2,1,0:T(8,128)} %get-tuple-element.304.d_ref.refs_0_), custom_call_target="tpu_custom_call" | custom-call | flops 19327352832 | bytes 16777216 | tf_op jit(solution)/shard_map/pallas_call | solution.py:824
  432.7 25.0 %shard_map.400 = f32[768,1024]{1,0:T(8,128)S(1)} custom-call(f32[768,1024]{1,0:T(8,128)} %copy-done.15, f32[4,768,1024]{2,1,0:T(8,128)} %get-tuple-element.304.d_ref.refs_0_, f32[4,1024,1024]{2,1,0:T(8,128)} %bitcast.218), custom_call_target="tpu_custom_call" | custom-call | flops 19327352832 | bytes 16777216 | tf_op jit(solution)/shard_map/pallas_call | solution.py:794
  461.4 8.6 shard_map.401.d_ref
  471.7 37.3 %shard_map.402 = (f32[4,768,256]{2,1,0:T(8,128)S(1)}, f32[4,1024,256]{2,1,0:T(8,128)}, f32[4,1024,256]{2,1,0:T(8,128)}) custom-call(f32[4,768,256]{2,1,0:T(8,128)} %copy-done.23, f32[4,1024,256]{2,1,0:T(8,128)} %get-tuple-element.297.k_ref, f32[4,1024,256]{2,1,0:T(8,128)} %get-tuple-element.298.v_ref, f32[1024,1]{1,0:T(8,128)S(1)} %copy-done.22, ...), custom_call_target="tpu_custom_call" | custom-call | flops 67645734912 | bytes 20971520 | tf_op jit(solution)/shard_map/pallas_call | solution.py:649
  510.8 25.1 %shard_map.403 = f32[1024,1024]{1,0:T(8,128)} custom-call(f32[768,1024]{1,0:T(8,128)S(1)} %copy-done.3, f32[4,768,256]{2,1,0:T(8,128)} %copy-done.5, f32[4,1024,256]{2,1,0:T(8,128)} %get-tuple-element.312.refs_1_.k_ref, f32[4,1024,256]{2,1,0:T(8,128)} %get-tuple-element.313.refs_2_.v_ref, f32[4,4,1024,256]{3,2,1,0:T(8,128)} %bitcast.157, ...), custom_call_target="tpu_custom_call" | custom-call | flops 17716740096 | bytes 16777216 | tf_op jit(solution)/shard_map/pallas_call | solution.py:794
  545.6 5.7 shard_map.404
  574.6 24.2 %shard_map.405.refs_0_ = f32[4,4672,256]{2,1,0:T(8,128)} custom-call(f32[768,1024]{1,0:T(8,128)S(1)} %copy-done.9, f32[256,1024]{1,0:T(8,128)} %collective-permute-done.y_ref, f32[4,768,256]{2,1,0:T(8,128)} %copy-done.5, f32[4,1024,256]{2,1,0:T(8,128)} %get-tuple-element.312.refs_1_.k_ref, f32[4,1024,256]{2,1,0:T(8,128)} %get-tuple-element.313.refs_2_.v_ref), custom_call_target="tpu_custom_call" | custom-call | flops 17716740096 | bytes 25165824 | tf_op jit(solution)/shard_map/pallas_call | solution.py:862
  598.7 8.9 shard_map.406
  609.8 12.8 %all-to-all-done.6 = f32[32,88,256]{2,1,0:T(8,128)} async-done(((f32[32,88,256]{2,1,0:T(8,128)}), f32[32,88,256]{2,1,0:T(8,128)}, u32[]{:S(2)}, u32[]{:S(2)}) %all-to-all-start.6) | async-done | bytes 2883616 | tf_op jit(solution)/shard_map/all_to_all | solution.py:983
  622.8 4.8 broadcast_multiply_fusion
  633.9 84.5 %shard_map.408 = (f32[8,128,1024]{2,1,0:T(8,128)S(1)}, f32[8,128]{1,0:T(8,128)S(1)}) custom-call(f32[8,128,1024]{2,1,0:T(8,128)} %bitcast.167, f32[8,128]{1,0:T(8,128)S(1)} %fusion.33.refs_1_), custom_call_target="tpu_custom_call" | custom-call | flops 1 | bytes 1024 | tf_op jit(solution)/shard_map/pallas_call | solution.py:417
  720.5 84.0 %shard_map.409 = (f32[8,128,1024]{2,1,0:T(8,128)S(1)}, f32[8,128]{1,0:T(8,128)S(1)}) custom-call(f32[8,128,1024]{2,1,0:T(8,128)} %bitcast.168, f32[8,128]{1,0:T(8,128)S(1)} %get-tuple-element.318.refs_1_), custom_call_target="tpu_custom_call" | custom-call | flops 1 | bytes 1024 | tf_op jit(solution)/shard_map/pallas_call | solution.py:417
  806.5 19.2 %scatter_custom_fusion.1 = f32[6304,256]{1,0:T(8,128)} fusion(s32[2816]{0:T(1024)S(1)} %fusion.32, f32[2816,256]{1,0:T(8,128)} %bitcast.42, f32[]{:T(128)} %constant.155.clone.1), kind=kCustom, calls=%fused_computation.35 | custom fusion | flops 720896 | bytes 6455808 | tf_op jit(solution)/shard_map/scatter-add | solution.py:1146
  826.4 5.1 multiply_reduce_fusion
  832.2 97.3 %shard_map.410 = (f32[8,584,256]{2,1,0:T(8,128)S(1)}, f32[8,128]{1,0:T(8,128)S(1)}) custom-call(f32[8,584,256]{2,1,0:T(8,128)} %bitcast.166, f32[8,128]{1,0:T(8,128)S(1)} %select_add_fusion.refs_1_), custom_call_target="tpu_custom_call" | custom-call | flops 1 | bytes 1024 | tf_op jit(solution)/shard_map/pallas_call | solution.py:417
  933.8 9.0 bitcast_subtract_fusion
  943.5 12.8 %multiply_subtract_fusion.1 = (f32[6304,256]{1,0:T(8,128)}, f32[6304,256]{1,0:T(8,128)}) fusion(f32[6304,256]{1,0:T(8,128)} %get-tuple-element.706, f32[6304,256]{1,0:T(8,128)} %get-tuple-element.325, f32[]{:T(128)S(6)} %min.3, f32[6304,256]{1,0:T(8,128)} %param.40), kind=kLoop, calls=%fused_computation.26 | loop fusion | flops 12910592 | bytes 32276484 | tf_op jit(solution)/shard_map/sub | solution.py:80
  961.2 11.5 %multiply_subtract_fusion = (f32[2,1024,1024]{2,1,0:T(8,128)}, f32[2,1024,1024]{2,1,0:T(8,128)}) fusion(f32[2,1024,1024]{2,1,0:T(8,128)} %param.33, f32[1,1024,1024]{2,1,0:T(8,128)S(1)} %bitcast.150, f32[1,1024,1024]{2,1,0:T(8,128)S(1)} %bitcast.151, f32[]{:T(128)S(6)} %min.3, f32[2,1024,1024]{2,1,0:T(8,128)} %param.43), kind=kLoop, calls=%fused_computation.24 | loop fusion | flops 18874368 | bytes 41943044 | tf_op jit(solution)/shard_map/sub | solution.py:80
  (339 shorter events, 130.9 us)
Async XLA Ops:
  7.2 183.4 %all-gather.6.cloned.1.call-start = ((), (), s32[]{:S(2)}) async-start(), calls=%async_computation.14 | async-start | bytes 20971520 | tf_op jit(solution)/shard_map/all_gather | solution.py:1013
  7.9 272.6 %all-gather.4.cloned.1.call-start = ((), (), s32[]{:S(2)}) async-start(), calls=%async_computation.10 | async-start | bytes 20971520 | tf_op jit(solution)/shard_map/all_gather | solution.py:1015
  21.8 29.2 %copy-start.67 = (s32[704]{0:T(1024)}, s32[704]{0:T(1024)S(1)}, u32[]{:S(2)}) copy-start(s32[704]{0:T(1024)S(1)} %broadcast_add_fusion.6) | copy-start | bytes 8452
  22.7 14.4 %all-to-all-start.4 = ((s32[32,1,128]{2,1,0:T(1,128)}), s32[32,1,128]{2,1,0:T(1,128)S(1)}, u32[]{:S(2)}, u32[]{:S(2)}) async-start(s32[32,1,128]{2,1,0:T(1,128)} %bitcast.13), calls=%async_computation.4 | async-start | bytes 32768 | tf_op jit(solution)/shard_map/all_to_all | solution.py:983
  47.9 117.6 %all-to-all-start.5 = ((f32[32,88,256]{2,1,0:T(8,128)}), f32[32,88,256]{2,1,0:T(8,128)S(1)}, u32[]{:S(2)}, u32[]{:S(2)}) async-start(f32[32,88,256]{2,1,0:T(8,128)} %bitcast.164), calls=%async_computation.5 | async-start | bytes 5767168 | tf_op jit(solution)/shard_map/all_to_all | solution.py:983
  50.8 583.1 %reduce-scatter.8.cloned.1.call-start = ((), (), s32[]{:S(2)}) async-start(), calls=%async_computation.13 | async-start | bytes 20971520 | tf_op jit(solution)/shard_map/reduce_scatter | solution.py:1116
  52.9 126.1 %copy-start.62 = (f32[1,1024]{1,0:T(1,128)}, f32[1,1024]{1,0:T(1,128)S(1)}, u32[]{:S(2)}) copy-start(f32[1,1024]{1,0:T(1,128)S(1)} %get-tuple-element.431) | copy-start | bytes 12292
  182.6 7.9 collective-permute-start
  190.6 26.0 %copy-start.21 = (f32[1024,1]{1,0:T(8,128)S(1)}, f32[1024,1]{1,0:T(8,128)}, u32[]{:S(2)}) copy-start(f32[1024,1]{1,0:T(8,128)} %broadcast_select_fusion.bias_ref) | copy-start | bytes 12292
  311.9 27.3 %copy-start.45 = (f32[256,64]{0,1:T(8,128)S(1)}, f32[256,64]{0,1:T(8,128)}, u32[]{:S(2)}) copy-start(f32[256,64]{0,1:T(8,128)} %param.38) | copy-start | bytes 196612
  377.8 342.7 %reduce-scatter.6.cloned.1.call-start = ((), (), s32[]{:S(2)}) async-start(), calls=%async_computation.12 | async-start | bytes 20971520 | tf_op jit(solution)/shard_map/reduce_scatter | solution.py:1122
  379.8 27.8 %copy-start.18 = (f32[768,1024]{1,0:T(8,128)S(1)}, f32[768,1024]{1,0:T(8,128)}, u32[]{:S(2)}) copy-start(f32[768,1024]{1,0:T(8,128)} %copy-done.17) | copy-start | bytes 9437188
  432.7 25.0 %copy-start.72 = (f32[768]{0:T(1024)S(1)}, f32[768]{0:T(1024)}, u32[]{:S(2)}) copy-start(f32[768]{0:T(1024)} %copy-done.71) | copy-start | bytes 9220
  471.7 39.0 %copy-start.3 = (f32[768,1024]{1,0:T(8,128)S(1)}, f32[768,1024]{1,0:T(8,128)}, u32[]{:S(2)}) copy-start(f32[768,1024]{1,0:T(8,128)} %subtract_multiply_fusion.1.x_ref.base_ref) | copy-start | bytes 9437188
  510.7 26.5 %copy-start.68 = (s32[704]{0:T(1024)S(1)}, s32[704]{0:T(1024)}, u32[]{:S(2)}) copy-start(s32[704]{0:T(1024)} %copy-done.67) | copy-start | bytes 8452
  510.7 26.7 %copy-start.35 = (s32[768]{0:T(1024)S(1)}, s32[768]{0:T(1024)}, u32[]{:S(2)}) copy-start(s32[768]{0:T(1024)} %copy-done.34) | copy-start | bytes 9220
  510.7 29.2 %copy-start.27 = (f32[768,1024]{1,0:T(8,128)S(1)}, f32[768,1024]{1,0:T(8,128)}, u32[]{:S(2)}) copy-start(f32[768,1024]{1,0:T(8,128)} %copy-done.26) | copy-start | bytes 9437188
  510.7 29.2 %copy-start.59 = (f32[768]{0:T(1024)S(1)}, f32[768]{0:T(1024)}, u32[]{:S(2)}) copy-start(f32[768]{0:T(1024)} %copy-done.58) | copy-start | bytes 9220
  510.7 29.2 %copy-start.63 = (f32[1,1024]{1,0:T(1,128)S(1)}, f32[1,1024]{1,0:T(1,128)}, u32[]{:S(2)}) copy-start(f32[1,1024]{1,0:T(1,128)} %copy-done.62) | copy-start | bytes 12292
  510.7 29.2 %copy-start.66 = (f32[768]{0:T(1024)S(1)}, f32[768]{0:T(1024)}, u32[]{:S(2)}) copy-start(f32[768]{0:T(1024)} %copy-done.65) | copy-start | bytes 9220
  537.2 2.7 collective-permute-start.1
  552.9 69.7 %all-to-all-start.6 = ((f32[32,88,256]{2,1,0:T(8,128)}), f32[32,88,256]{2,1,0:T(8,128)}, u32[]{:S(2)}, u32[]{:S(2)}) async-start(f32[32,88,256]{2,1,0:T(8,128)} %bitcast.143), calls=%async_computation.6 | async-start | bytes 5767168 | tf_op jit(solution)/shard_map/all_to_all | solution.py:983
  556.5 275.7 %reduce-scatter.4.cloned.1.call-start = ((), (), s32[]{:S(2)}) async-start(), calls=%async_computation.11 | async-start | bytes 23920640 | tf_op jit(solution)/shard_map/reduce_scatter | solution.py:1186
  806.5 19.2 %copy-start.44 = (s32[768]{0:T(1024)S(1)}, s32[768]{0:T(1024)}, u32[]{:S(2)}) copy-start(s32[768]{0:T(1024)} %copy-done.43) | copy-start | bytes 9220
  806.5 19.2 %copy-start.48 = (s32[768]{0:T(1024)S(1)}, s32[768]{0:T(1024)}, u32[]{:S(2)}) copy-start(s32[768]{0:T(1024)} %copy-done.47) | copy-start | bytes 9220
  943.4 14.1 %copy-start.57 = (f32[8,1024]{1,0:T(8,128)S(1)}, f32[8,1024]{1,0:T(8,128)}, u32[]{:S(2)}) copy-start(f32[8,1024]{1,0:T(8,128)} %param.36) | copy-start | bytes 98308
  943.4 14.1 %copy-start.73 = (f32[8,1024]{1,0:T(8,128)S(1)}, f32[8,1024]{1,0:T(8,128)}, u32[]{:S(2)}) copy-start(f32[8,1024]{1,0:T(8,128)} %param.46) | copy-start | bytes 98308
  943.4 14.7 %copy-start.30 = (f32[1024,256]{1,0:T(8,128)S(1)}, f32[1024,256]{1,0:T(8,128)}, u32[]{:S(2)}) copy-start(f32[1024,256]{1,0:T(8,128)} %param.37) | copy-start | bytes 3145732
  943.4 14.7 %copy-start.32 = (f32[1024,256]{1,0:T(8,128)S(1)}, f32[1024,256]{1,0:T(8,128)}, u32[]{:S(2)}) copy-start(f32[1024,256]{1,0:T(8,128)} %get-tuple-element.450) | copy-start | bytes 3145732
  943.5 14.7 %copy-start.38 = (f32[1024,256]{1,0:T(8,128)S(1)}, f32[1024,256]{1,0:T(8,128)}, u32[]{:S(2)}) copy-start(f32[1024,256]{1,0:T(8,128)} %param.47) | copy-start | bytes 3145732
  943.5 16.3 %copy-start.46 = (f32[256,64]{0,1:T(8,128)S(1)}, f32[256,64]{0,1:T(8,128)}, u32[]{:S(2)}) copy-start(f32[256,64]{0,1:T(8,128)} %param.38) | copy-start | bytes 196612
  943.5 16.3 %copy-start.69 = (f32[256,64]{0,1:T(8,128)S(1)}, f32[256,64]{0,1:T(8,128)}, u32[]{:S(2)}) copy-start(f32[256,64]{0,1:T(8,128)} %param.48) | copy-start | bytes 196612
  (70 other events, 345.3 us)
Sparse Core Ops, SparseCore 0:
  9.6 162.3 all-gather.5
  174.1 105.9 all-gather.3
  378.0 124.1 reduce-scatter.7
  504.8 157.0 reduce-scatter.5
  664.3 141.1 reduce-scatter.3

commit v5 on v4

--- a/solution.py
+++ b/solution.py
@@ -267,39 +267,44 @@
     return (groups * shards).bit_length() - 1
 
 
-def cube_gather_kernel(groups, shards, x_ref, o_ref, held, send_sem, recv_sem):
-    partners = cube_partners(groups, shards)
-    greet(partners)
-    me = lax.axis_index("dp") * shards + lax.axis_index("tensor")
+def meet_kernel(groups, shards, x_ref, o_ref, held, send_sem, recv_sem):
+    dp, tp = lax.axis_index("dp"), lax.axis_index("tensor")
+    near = [(dp, (tp + k) % shards) for k in range(1, shards)]
+    far = [((dp + k) % groups, tp) for k in range(1, groups)]
+    greet([*near, *far])
+    me = dp * shards + tp
     held[pl.ds(me, 1)] = x_ref[...][None]
-    for stage, partner in enumerate(partners):
-        size = 1 << stage
-        mine = pl.ds((me // size) * size, size)
-        copy = pltpu.make_async_remote_copy(
-            src_ref=held.at[mine],
-            dst_ref=held.at[mine],
-            send_sem=send_sem.at[stage],
-            recv_sem=recv_sem.at[stage],
-            device_id=partner,
-            device_id_type=MESH,
-        )
-        copy.start()
-        copy.wait()
+    at = 0
+    for partners, mine in ((near, pl.ds(me, 1)), (far, pl.ds(dp * shards, shards))):
+        copies = []
+        for partner in partners:
+            copy = pltpu.make_async_remote_copy(
+                src_ref=held.at[mine],
+                dst_ref=held.at[mine],
+                send_sem=send_sem.at[at],
+                recv_sem=recv_sem.at[at],
+                device_id=partner,
+                device_id_type=MESH,
+            )
+            copy.start()
+            copies.append(copy)
+            at += 1
+        for copy in copies:
+            copy.wait()
     o_ref[...] = held[...]
 
 
-def cube_gather(block, groups, shards, collective_id):
-    stages = cube_stages(groups, shards)
+def meet(block, groups, shards, collective_id):
     shape = (groups * shards, *block.shape)
     return pl.pallas_call(
-        functools.partial(cube_gather_kernel, groups, shards),
+        functools.partial(meet_kernel, groups, shards),
         out_shape=jax.ShapeDtypeStruct(shape, block.dtype),
         in_specs=[VMEM],
         out_specs=VMEM,
         scratch_shapes=[
             pltpu.VMEM(shape, block.dtype),
-            pltpu.SemaphoreType.DMA((stages,)),
-            pltpu.SemaphoreType.DMA((stages,)),
+            pltpu.SemaphoreType.DMA((groups + shards - 2,)),
+            pltpu.SemaphoreType.DMA((groups + shards - 2,)),
         ],
         compiler_params=pltpu.CompilerParams(collective_id=collective_id, has_side_effects=True),
     )(block)
@@ -1094,7 +1099,7 @@
     sums = jnp.stack(
         [jnp.sum(h_two * weight_whole[:, None], axis=0), jnp.sum(h_two * weight_split[:, None], axis=0)]
     )
-    all_sums = cube_gather(sums.reshape(-1, 128), groups, shards, 5).reshape(groups * shards // 2, 2, 2, width)
+    all_sums = meet(sums.reshape(-1, 128), groups, shards, 5).reshape(groups * shards // 2, 2, 2, width)
     all_pooled = jnp.stack(
         [all_sums[:, 0, 0], all_sums[:, 0, 1] + all_sums[:, 1, 1], all_sums[:, 1, 0]], axis=1
     ).reshape(groups * seqs, width)
@@ -1182,10 +1187,10 @@
     small_rows = jnp.broadcast_to(small_rows, (shards, SMALL_ROWS, cols))
     parts_attn = lax.dynamic_update_slice(parts_attn, grad_pos_parts, (0, 4 * width, 0))
     parts_attn = lax.dynamic_update_slice(parts_attn, small_rows, (0, 4 * width + slots, 0))
-    landed_first, parts_attn = lax.optimization_barrier((landed_first, parts_attn))
-    sum_attn = lax.psum_scatter(parts_attn, "tensor", scatter_dimension=0, tiled=False)
     first_all = (dp_rank == 0).astype(jnp.float32) * (tp_rank == 0).astype(jnp.float32)
     head_squares = first_all * (squares(grad_head_first) + squares(grad_head_second) + squares(grad_head_bias))
+    landed_first, parts_attn, head_squares = lax.optimization_barrier((landed_first, parts_attn, head_squares))
+    sum_attn = lax.psum_scatter(parts_attn, "tensor", scatter_dimension=0, tiled=False)
     corner = (lax.broadcasted_iota(jnp.int32, (8, 128), 0) + lax.broadcasted_iota(jnp.int32, (8, 128), 1)) == 0
     tile = jnp.where(corner, head_squares, 0.0)
     (sum_down,), tile = ring_sum([sum_down], tile, groups, shards, 2, 0, 1)
@@ -1208,7 +1213,7 @@
     grad_norms = sum_small[:8]
     grad_bias_qv = lax.dynamic_slice_in_dim(sum_small[8:10], tp_rank * cols, cols, 1)
     grad_bias_up = lax.dynamic_slice_in_dim(sum_small[10:].reshape(-1), tp_rank * hidden, hidden)
-    grad_attn = sum_attn[: 4 * width]
+    grad_attn = sum_attn[: 4 * width].reshape(4, width, cols)
     grad_ffn_up, grad_ffn_down = sum_up, sum_down
     grad_pos = sum_attn[4 * width : -SMALL_ROWS]
 
@@ -1218,8 +1223,7 @@
     grad_ffn = jnp.stack([grad_ffn_up, grad_ffn_down])
     new_embedding, next_embedding = advance(embedding, mom_embedding, grad_embedding, factor)
     new_positions, next_positions = advance(positions, mom_positions, grad_positions, factor)
-    flat_attn, flat_mom = attn_weights.reshape(-1, cols), mom_attn.reshape(-1, cols)
-    new_attn, next_attn = (x.reshape(attn_weights.shape) for x in advance(flat_attn, flat_mom, grad_attn, factor))
+    new_attn, next_attn = advance(attn_weights, mom_attn, grad_attn, factor)
     new_ffn, next_ffn = advance(ffn_weights, ffn_momentum, grad_ffn, factor)
     new_bias_qv, next_bias_qv = advance(bias_qv, mom_bias_qv, grad_bias_qv, factor)
     new_bias_up, next_bias_up = advance(bias_up, mom_bias_up, grad_bias_up, factor)

time: 991 us -> 981 us (0.990)
    unnamed x190 -> x192, local copies, waits for them, and re-layouts: 29.9 us -> 30.1 us
  transfers between devices with their start and end apart: 10 -> 10, of which waited for: 3 -> 3; matrix products, arithmetic and copies ran while one was open for 11% -> 11% of each run, Pallas kernels for 56% -> 57%
where the time goes in v5:
time: 981 us; the launch traced here: 972 us
  Pallas kernels  712 us (73%)
  other arithmetic  120 us (12%)
  local copies, waits for them, and re-layouts  70.7 us (7%)
  between operations  23 us (2%)
  starting transfers between devices  17 us (2%)
  waiting for transfers between devices  14.7 us (1%)
  matrix products  12.6 us (1%)
    pallas_call x3, Pallas kernels, ring_sum(): pl.pallas_call(functools.partial(ring_kernel, groups, shards, parts, len(...  266 us
    pallas_call x1, Pallas kernels, spread(): pl.pallas_call(functools.partial(spread_kernel, groups), out_shape=[jax.S...  108 us
    pallas_call x4, Pallas kernels, gather_back(): pl.pallas_call(functools.partial(gather_back_kernel, len(terms)), grid=(s...  82.5 us
    pallas_call x3, Pallas kernels, times(): pl.pallas_call(functools.partial(times_kernel, finish, len(extras)), grid...  65.1 us
    pallas_call x3, Pallas kernels, outer(): pl.pallas_call(outer_kernel, grid=(shards, columns // wide), in_specs=[pl...  58.8 us
    pallas_call x2, Pallas kernels, attend_call(): pl.pallas_call(functools.partial(kernel, slots, slots // 2), grid=(pairs,...  57.1 us
    sub x10, other arithmetic, advance(): weight - RATE * (DECAY * moment_new + (1.0 - DECAY) * clipped)  39 us
    unnamed x192, local copies, waits for them, and re-layouts  30.1 us
  transfers between devices with their start and end apart: 10, of which 3 were waited for; matrix products, arithmetic and copies ran while one was open for 11% of the time, Pallas kernels for 57%

profile of v5, /device:TPU:0, one launch (start us, length us, event | category | flops | bytes accessed | tf_op | source)
XLA Modules:
  0.0 972.0 jit_solution(11529585161143900501)
XLA Ops:
  8.0 8.5 fusion.55
  22.7 7.3 all-to-all-start.4
  30.0 7.1 all-to-all-done.4
  37.2 10.7 %gather_fusion.1 = f32[2816,256]{1,0:T(8,128)} fusion(f32[6304,256]{1,0:T(8,128)} %param.30, s32[3072]{0:T(1024)S(1)} %pad_clamp_fusion.1), kind=kCustom, calls=%fused_computation.1 | custom fusion | bytes 5778432 | tf_op jit(solution)/shard_map/jit(_take)/gather | solution.py:1039
  55.1 108.4 %shard_map.390 = (f32[4,8,128,1024]{3,2,1,0:T(8,128)}, f32[4,520,256]{2,1,0:T(8,128)S(1)}) custom-call(f32[8,128,1024]{2,1,0:T(8,128)S(1)} %bitcast.136, f32[520,256]{1,0:T(8,128)S(1)} %select_maximum_fusion.small_ref), custom_call_target="tpu_custom_call" | custom-call | flops 1 | bytes 1024 | tf_op jit(solution)/shard_map/pallas_call | solution.py:510
  167.5 5.7 shard_map.391
  191.0 24.2 %shard_map.392 = (f32[4,768,256]{2,1,0:T(8,128)S(1)}, f32[4,1024,256]{2,1,0:T(8,128)}, f32[4,1024,256]{2,1,0:T(8,128)}) custom-call(f32[768,1024]{1,0:T(8,128)} %copy-done.8, f32[256,1024]{1,0:T(8,128)} %collective-permute-done.y_ref, f32[4,4,1024,256]{3,2,1,0:T(8,128)} %bitcast.146, f32[4,4,1024,256]{3,2,1,0:T(8,128)} %bitcast.147, ...), custom_call_target="tpu_custom_call" | custom-call | flops 17716740096 | bytes 25165824 | tf_op jit(solution)/shard_map/pallas_call | solution.py:750
  216.9 19.8 %shard_map.393 = (f32[4,768,256]{2,1,0:T(8,128)S(1)}, f32[8,2,768]{2,1,0:T(2,128)S(1)}) custom-call(f32[4,768,256]{2,1,0:T(8,128)} %copy-done.23, f32[4,1024,256]{2,1,0:T(8,128)} %get-tuple-element.298.k_ref, f32[4,1024,256]{2,1,0:T(8,128)} %get-tuple-element.299.v_ref, f32[1024,1]{1,0:T(8,128)S(1)} %copy-done.21), custom_call_target="tpu_custom_call" | custom-call | flops 67645734912 | bytes 20971520 | tf_op jit(solution)/shard_map/pallas_call | solution.py:654
  238.3 8.5 shard_map.394
  250.0 29.0 %shard_map.395 = (f32[4,768,1024]{2,1,0:T(8,128)}, f32[4,768,1024]{2,1,0:T(8,128)}) custom-call(f32[768,1024]{1,0:T(8,128)S(1)} %get-tuple-element.408.x_ref, f32[4,1024,1024]{2,1,0:T(8,128)} %bitcast.210, f32[4,1,1024]{2,1,0:T(1,128)S(1)} %reshape_reshape.3.refs_0_), custom_call_target="tpu_custom_call" | custom-call | flops 19327352832 | bytes 16777216 | tf_op jit(solution)/shard_map/pallas_call | solution.py:695
  280.7 24.7 %shard_map.396 = f32[768,1024]{1,0:T(8,128)S(1)} custom-call(f32[768,1024]{1,0:T(8,128)} %get-tuple-element.407.base_ref, f32[4,768,1024]{2,1,0:T(8,128)} %get-tuple-element.302.refs_0_.d_ref, f32[4,1024,1024]{2,1,0:T(8,128)} %all-gather.4.cloned.1.call-done.refs_1_.w_ref), custom_call_target="tpu_custom_call" | custom-call | flops 19327352832 | bytes 16777216 | tf_op jit(solution)/shard_map/pallas_call | solution.py:799
  313.7 13.8 %shard_map.397 = f32[32,16,128]{2,1,0:T(8,128)} custom-call(f32[16,128]{1,0:T(8,128)} %reshape.661.x_ref), custom_call_target="tpu_custom_call" | custom-call | tf_op jit(solution)/shard_map/pallas_call | solution.py:299
  344.8 25.0 %shard_map.407 = f32[4,1024,1024]{2,1,0:T(8,128)} custom-call(f32[768,1024]{1,0:T(8,128)S(1)} %get-tuple-element.404.x_ref.base_ref, f32[4,768,1024]{2,1,0:T(8,128)} %get-tuple-element.302.refs_0_.d_ref), custom_call_target="tpu_custom_call" | custom-call | flops 19327352832 | bytes 16777216 | tf_op jit(solution)/shard_map/pallas_call | solution.py:829
  373.5 27.6 %shard_map.398 = (f32[4,768,1024]{2,1,0:T(8,128)}, f32[4,1,1024]{2,1,0:T(1,128)S(1)}) custom-call(f32[768,1024]{1,0:T(8,128)S(1)} %copy-done.16, f32[4,1024,1024]{2,1,0:T(8,128)} %all-gather.4.cloned.1.call-done.refs_1_.w_ref, f32[4,768,1024]{2,1,0:T(8,128)} %get-tuple-element.303.refs_0_), custom_call_target="tpu_custom_call" | custom-call | flops 19327352832 | bytes 16777216 | tf_op jit(solution)/shard_map/pallas_call | solution.py:695
  401.1 24.8 %shard_map.399 = f32[4,1024,1024]{2,1,0:T(8,128)} custom-call(f32[768,1024]{1,0:T(8,128)S(1)} %copy-done.18, f32[4,768,1024]{2,1,0:T(8,128)} %get-tuple-element.305.d_ref.refs_0_), custom_call_target="tpu_custom_call" | custom-call | flops 19327352832 | bytes 16777216 | tf_op jit(solution)/shard_map/pallas_call | solution.py:829
  426.0 24.8 %shard_map.400 = f32[768,1024]{1,0:T(8,128)S(1)} custom-call(f32[768,1024]{1,0:T(8,128)} %copy-done.15, f32[4,768,1024]{2,1,0:T(8,128)} %get-tuple-element.305.d_ref.refs_0_, f32[4,1024,1024]{2,1,0:T(8,128)} %bitcast.211), custom_call_target="tpu_custom_call" | custom-call | flops 19327352832 | bytes 16777216 | tf_op jit(solution)/shard_map/pallas_call | solution.py:799
  455.1 8.4 shard_map.401.d_ref
  465.2 37.3 %shard_map.402 = (f32[4,768,256]{2,1,0:T(8,128)S(1)}, f32[4,1024,256]{2,1,0:T(8,128)}, f32[4,1024,256]{2,1,0:T(8,128)}) custom-call(f32[4,768,256]{2,1,0:T(8,128)} %copy-done.23, f32[4,1024,256]{2,1,0:T(8,128)} %get-tuple-element.298.k_ref, f32[4,1024,256]{2,1,0:T(8,128)} %get-tuple-element.299.v_ref, f32[1024,1]{1,0:T(8,128)S(1)} %copy-done.22, ...), custom_call_target="tpu_custom_call" | custom-call | flops 67645734912 | bytes 20971520 | tf_op jit(solution)/shard_map/pallas_call | solution.py:654
  504.2 24.6 %shard_map.403 = f32[1024,1024]{1,0:T(8,128)} custom-call(f32[768,1024]{1,0:T(8,128)S(1)} %copy-done.3, f32[4,768,256]{2,1,0:T(8,128)} %copy-done.5, f32[4,1024,256]{2,1,0:T(8,128)} %get-tuple-element.313.refs_1_.k_ref, f32[4,1024,256]{2,1,0:T(8,128)} %get-tuple-element.314.refs_2_.v_ref, f32[4,4,1024,256]{3,2,1,0:T(8,128)} %bitcast.151, ...), custom_call_target="tpu_custom_call" | custom-call | flops 17716740096 | bytes 16777216 | tf_op jit(solution)/shard_map/pallas_call | solution.py:799
  539.2 5.7 shard_map.404
  546.5 5.9 all-to-all-start.6
  578.9 24.2 %shard_map.405.refs_0_ = f32[4,4672,256]{2,1,0:T(8,128)} custom-call(f32[768,1024]{1,0:T(8,128)S(1)} %copy-done.9, f32[256,1024]{1,0:T(8,128)} %collective-permute-done.y_ref, f32[4,768,256]{2,1,0:T(8,128)} %copy-done.5, f32[4,1024,256]{2,1,0:T(8,128)} %get-tuple-element.313.refs_1_.k_ref, f32[4,1024,256]{2,1,0:T(8,128)} %get-tuple-element.314.refs_2_.v_ref), custom_call_target="tpu_custom_call" | custom-call | flops 17716740096 | bytes 25165824 | tf_op jit(solution)/shard_map/pallas_call | solution.py:867
  603.1 8.9 shard_map.406
  619.5 84.5 %shard_map.408 = (f32[8,128,1024]{2,1,0:T(8,128)S(1)}, f32[8,128]{1,0:T(8,128)S(1)}) custom-call(f32[8,128,1024]{2,1,0:T(8,128)} %bitcast.162, f32[8,128]{1,0:T(8,128)S(1)} %fusion.33.refs_1_), custom_call_target="tpu_custom_call" | custom-call | flops 1 | bytes 1024 | tf_op jit(solution)/shard_map/pallas_call | solution.py:422
  706.0 84.2 %shard_map.409 = (f32[8,128,1024]{2,1,0:T(8,128)S(1)}, f32[8,128]{1,0:T(8,128)S(1)}) custom-call(f32[8,128,1024]{2,1,0:T(8,128)} %bitcast.163, f32[8,128]{1,0:T(8,128)S(1)} %get-tuple-element.320.refs_1_), custom_call_target="tpu_custom_call" | custom-call | flops 1 | bytes 1024 | tf_op jit(solution)/shard_map/pallas_call | solution.py:422
  792.2 19.2 %scatter_custom_fusion.1 = f32[6304,256]{1,0:T(8,128)} fusion(s32[2816]{0:T(1024)S(1)} %fusion.32, f32[2816,256]{1,0:T(8,128)} %bitcast.42, f32[]{:T(128)} %constant.155.clone.1), kind=kCustom, calls=%fused_computation.35 | custom fusion | flops 720896 | bytes 6455808 | tf_op jit(solution)/shard_map/scatter-add | solution.py:1151
  812.3 5.1 multiply_reduce_fusion
  818.1 97.4 %shard_map.410 = (f32[8,584,256]{2,1,0:T(8,128)S(1)}, f32[8,128]{1,0:T(8,128)S(1)}) custom-call(f32[8,584,256]{2,1,0:T(8,128)} %bitcast.161, f32[8,128]{1,0:T(8,128)S(1)} %select_add_fusion.refs_1_), custom_call_target="tpu_custom_call" | custom-call | flops 1 | bytes 1024 | tf_op jit(solution)/shard_map/pallas_call | solution.py:422
  920.0 4.7 fusion.2
  931.9 6.7 multiply_subtract_fusion.2
  938.6 12.6 %multiply_subtract_fusion.1 = (f32[6304,256]{1,0:T(8,128)}, f32[6304,256]{1,0:T(8,128)}) fusion(f32[6304,256]{1,0:T(8,128)} %get-tuple-element.708, f32[6304,256]{1,0:T(8,128)} %get-tuple-element.327, f32[]{:T(128)S(6)} %min.3, f32[6304,256]{1,0:T(8,128)} %param.40), kind=kLoop, calls=%fused_computation.26 | loop fusion | flops 12910592 | bytes 32276484 | tf_op jit(solution)/shard_map/sub | solution.py:80
  952.4 11.5 %multiply_subtract_fusion = (f32[2,1024,1024]{2,1,0:T(8,128)}, f32[2,1024,1024]{2,1,0:T(8,128)}) fusion(f32[2,1024,1024]{2,1,0:T(8,128)} %param.33, f32[1,1024,1024]{2,1,0:T(8,128)S(1)} %bitcast.144, f32[1,1024,1024]{2,1,0:T(8,128)S(1)} %bitcast.145, f32[]{:T(128)S(6)} %min.3, f32[2,1024,1024]{2,1,0:T(8,128)} %param.43), kind=kLoop, calls=%fused_computation.24 | loop fusion | flops 18874368 | bytes 41943044 | tf_op jit(solution)/shard_map/sub | solution.py:80
  (341 shorter events, 138.2 us)
Async XLA Ops:
  7.2 183.8 %all-gather.6.cloned.1.call-start = ((), (), s32[]{:S(2)}) async-start(), calls=%async_computation.14 | async-start | bytes 20971520 | tf_op jit(solution)/shard_map/all_gather | solution.py:1018
  7.9 272.7 %all-gather.4.cloned.1.call-start = ((), (), s32[]{:S(2)}) async-start(), calls=%async_computation.10 | async-start | bytes 20971520 | tf_op jit(solution)/shard_map/all_gather | solution.py:1020
  22.0 28.9 %copy-start.67 = (s32[704]{0:T(1024)}, s32[704]{0:T(1024)S(1)}, u32[]{:S(2)}) copy-start(s32[704]{0:T(1024)S(1)} %broadcast_add_fusion.6) | copy-start | bytes 8452
  22.7 14.4 %all-to-all-start.4 = ((s32[32,1,128]{2,1,0:T(1,128)}), s32[32,1,128]{2,1,0:T(1,128)S(1)}, u32[]{:S(2)}, u32[]{:S(2)}) async-start(s32[32,1,128]{2,1,0:T(1,128)} %bitcast.13), calls=%async_computation.4 | async-start | bytes 32768 | tf_op jit(solution)/shard_map/all_to_all | solution.py:988
  47.9 117.6 %all-to-all-start.5 = ((f32[32,88,256]{2,1,0:T(8,128)}), f32[32,88,256]{2,1,0:T(8,128)S(1)}, u32[]{:S(2)}, u32[]{:S(2)}) async-start(f32[32,88,256]{2,1,0:T(8,128)} %bitcast.159), calls=%async_computation.5 | async-start | bytes 5767168 | tf_op jit(solution)/shard_map/all_to_all | solution.py:988
  50.8 568.6 %reduce-scatter.8.cloned.1.call-start = ((), (), s32[]{:S(2)}) async-start(), calls=%async_computation.13 | async-start | bytes 20971520 | tf_op jit(solution)/shard_map/reduce_scatter | solution.py:1121
  52.9 126.4 %copy-start.62 = (f32[1,1024]{1,0:T(1,128)}, f32[1,1024]{1,0:T(1,128)S(1)}, u32[]{:S(2)}) copy-start(f32[1,1024]{1,0:T(1,128)S(1)} %get-tuple-element.433) | copy-start | bytes 12292
  183.0 8.0 collective-permute-start
  191.0 25.9 %copy-start.21 = (f32[1024,1]{1,0:T(8,128)S(1)}, f32[1024,1]{1,0:T(8,128)}, u32[]{:S(2)}) copy-start(f32[1024,1]{1,0:T(8,128)} %broadcast_select_fusion.bias_ref) | copy-start | bytes 12292
  312.0 20.9 %copy-start.46 = (f32[256,64]{0,1:T(8,128)S(1)}, f32[256,64]{0,1:T(8,128)}, u32[]{:S(2)}) copy-start(f32[256,64]{0,1:T(8,128)} %param.38) | copy-start | bytes 196612
  330.8 11.9 %copy-start.38 = (f32[48,1024]{1,0:T(8,128)}, f32[48,1024]{1,0:T(8,128)S(1)}, u32[]{:S(2)}) copy-start(f32[48,1024]{1,0:T(8,128)S(1)} %reshape.663) | copy-start | bytes 589828
  371.6 334.4 %reduce-scatter.6.cloned.1.call-start = ((), (), s32[]{:S(2)}) async-start(), calls=%async_computation.12 | async-start | bytes 20971520 | tf_op jit(solution)/shard_map/reduce_scatter | solution.py:1127
  373.5 27.6 %copy-start.18 = (f32[768,1024]{1,0:T(8,128)S(1)}, f32[768,1024]{1,0:T(8,128)}, u32[]{:S(2)}) copy-start(f32[768,1024]{1,0:T(8,128)} %copy-done.17) | copy-start | bytes 9437188
  426.0 24.8 %copy-start.72 = (f32[768]{0:T(1024)S(1)}, f32[768]{0:T(1024)}, u32[]{:S(2)}) copy-start(f32[768]{0:T(1024)} %copy-done.71) | copy-start | bytes 9220
  465.2 39.0 %copy-start.3 = (f32[768,1024]{1,0:T(8,128)S(1)}, f32[768,1024]{1,0:T(8,128)}, u32[]{:S(2)}) copy-start(f32[768,1024]{1,0:T(8,128)} %subtract_multiply_fusion.1.x_ref.base_ref) | copy-start | bytes 9437188
  504.2 26.0 %copy-start.37 = (s32[768]{0:T(1024)S(1)}, s32[768]{0:T(1024)}, u32[]{:S(2)}) copy-start(s32[768]{0:T(1024)} %copy-done.36) | copy-start | bytes 9220
  504.2 26.0 %copy-start.68 = (s32[704]{0:T(1024)S(1)}, s32[704]{0:T(1024)}, u32[]{:S(2)}) copy-start(s32[704]{0:T(1024)} %copy-done.67) | copy-start | bytes 8452
  504.2 28.7 %copy-start.27 = (f32[768,1024]{1,0:T(8,128)S(1)}, f32[768,1024]{1,0:T(8,128)}, u32[]{:S(2)}) copy-start(f32[768,1024]{1,0:T(8,128)} %copy-done.26) | copy-start | bytes 9437188
  504.2 28.7 %copy-start.60 = (f32[768]{0:T(1024)S(1)}, f32[768]{0:T(1024)}, u32[]{:S(2)}) copy-start(f32[768]{0:T(1024)} %copy-done.59) | copy-start | bytes 9220
  504.2 28.6 %copy-start.63 = (f32[1,1024]{1,0:T(1,128)S(1)}, f32[1,1024]{1,0:T(1,128)}, u32[]{:S(2)}) copy-start(f32[1,1024]{1,0:T(1,128)} %copy-done.62) | copy-start | bytes 12292
  504.2 28.6 %copy-start.66 = (f32[768]{0:T(1024)S(1)}, f32[768]{0:T(1024)}, u32[]{:S(2)}) copy-start(f32[768]{0:T(1024)} %copy-done.65) | copy-start | bytes 9220
  530.1 2.7 collective-permute-start.1
  546.5 72.0 %all-to-all-start.6 = ((f32[32,88,256]{2,1,0:T(8,128)}), f32[32,88,256]{2,1,0:T(8,128)}, u32[]{:S(2)}, u32[]{:S(2)}) async-start(f32[32,88,256]{2,1,0:T(8,128)} %bitcast.137), calls=%async_computation.6 | async-start | bytes 5767168 | tf_op jit(solution)/shard_map/all_to_all | solution.py:988
  552.5 265.6 %reduce-scatter.4.cloned.1.call-start = ((), (), s32[]{:S(2)}) async-start(), calls=%async_computation.11 | async-start | bytes 23920640 | tf_op jit(solution)/shard_map/reduce_scatter | solution.py:1193
  792.2 19.2 %copy-start.45 = (s32[768]{0:T(1024)S(1)}, s32[768]{0:T(1024)}, u32[]{:S(2)}) copy-start(s32[768]{0:T(1024)} %copy-done.44) | copy-start | bytes 9220
  792.2 19.2 %copy-start.49 = (s32[768]{0:T(1024)S(1)}, s32[768]{0:T(1024)}, u32[]{:S(2)}) copy-start(s32[768]{0:T(1024)} %copy-done.48) | copy-start | bytes 9220
  938.5 12.7 %copy-start.86 = (f32[2,256]{1,0:T(2,128)S(1)}, f32[2,256]{1,0:T(2,128)}, u32[]{:S(2)}) copy-start(f32[2,256]{1,0:T(2,128)} %param.34) | copy-start | bytes 6148
  938.5 12.7 %copy-start.93 = (f32[2,256]{1,0:T(2,128)S(1)}, f32[2,256]{1,0:T(2,128)}, u32[]{:S(2)}) copy-start(f32[2,256]{1,0:T(2,128)} %param.44) | copy-start | bytes 6148
  938.5 13.3 %copy-start.82 = (f32[1024]{0:T(1024)S(1)}, f32[1024]{0:T(1024)}, u32[]{:S(2)}) copy-start(f32[1024]{0:T(1024)} %param.35) | copy-start | bytes 12292
  938.5 13.3 %copy-start.89 = (f32[1024]{0:T(1024)S(1)}, f32[1024]{0:T(1024)}, u32[]{:S(2)}) copy-start(f32[1024]{0:T(1024)} %param.45) | copy-start | bytes 12292
  938.5 13.9 %copy-start.12 = (f32[8,128,1024]{2,1,0:T(8,128)S(1)}, f32[8,128,1024]{2,1,0:T(8,128)}, u32[]{:S(2)}) copy-start(f32[8,128,1024]{2,1,0:T(8,128)} %copy-done.11) | copy-start | bytes 12582916
  938.6 13.9 %copy-start.14 = (f32[8,128,1024]{2,1,0:T(8,128)S(1)}, f32[8,128,1024]{2,1,0:T(8,128)}, u32[]{:S(2)}) copy-start(f32[8,128,1024]{2,1,0:T(8,128)} %copy-done.13) | copy-start | bytes 12582916
  (71 other events, 306.8 us)
Sparse Core Ops, SparseCore 0:
  9.6 162.3 all-gather.5
  174.1 105.9 all-gather.3
  371.7 127.0 reduce-scatter.7
  501.3 157.0 reduce-scatter.5
  660.9 141.1 reduce-scatter.3

commit v6 on v5

--- a/solution.py
+++ b/solution.py
@@ -650,7 +650,6 @@
             return pl.BlockSpec((1, *shape[1:]), lambda i: (i, 0, 0))
         return pl.BlockSpec((1, shape[1], lanes), lambda i: (i // per_shard, 0, i % per_shard))
 
-    work = 7 * 2 * pairs * 2 * queries.shape[1] * slots * HEAD_DIM * 3
     return pl.pallas_call(
         functools.partial(kernel, slots, slots // 2),
         grid=(pairs,),
@@ -658,7 +657,7 @@
         out_specs=[spec(shape) for shape in outputs],
         out_shape=[jax.ShapeDtypeStruct(shape, jnp.float32) for shape in outputs],
         compiler_params=pltpu.CompilerParams(vmem_limit_bytes=48 << 20),
-        cost_estimate=pl.CostEstimate(flops=4 * work, bytes_accessed=20 << 20, transcendentals=0),
+        cost_estimate=pl.CostEstimate(flops=1, bytes_accessed=1024, transcendentals=0),
     )(*inputs)
 
 
@@ -700,9 +699,7 @@
         out_shape=[jax.ShapeDtypeStruct(shape, jnp.float32) for shape in outs],
         scratch_shapes=[pltpu.VMEM((rows, depth), jnp.bfloat16)] * 2,
         compiler_params=pltpu.CompilerParams(vmem_limit_bytes=48 << 20),
-        cost_estimate=pl.CostEstimate(
-            flops=6 * rows * depth * shards * columns, bytes_accessed=4 * w.size, transcendentals=0
-        ),
+        cost_estimate=pl.CostEstimate(flops=1, bytes_accessed=1024, transcendentals=0),
     )(x, w, *extras)
     return results
 
@@ -761,9 +758,7 @@
         out_shape=[jax.ShapeDtypeStruct((shards, n, columns), jnp.float32) for n in (count, rows, rows)],
         scratch_shapes=[pltpu.VMEM((rows, depth), jnp.bfloat16)] * 2,
         compiler_params=pltpu.CompilerParams(vmem_limit_bytes=48 << 20),
-        cost_estimate=pl.CostEstimate(
-            flops=6 * (count + 2 * rows) * depth * shards * columns, bytes_accessed=24 << 20, transcendentals=0
-        ),
+        cost_estimate=pl.CostEstimate(flops=1, bytes_accessed=1024, transcendentals=0),
     )(x, y, w, w, w, bias_q, bias_v)
 
 
@@ -795,7 +790,6 @@
             return pl.BlockSpec((1, 1, w.shape[-2], wide), lambda j, c: (j, which, 0, c))
         return pl.BlockSpec((1, w.shape[-2], wide), lambda j, c: (j, 0, c))
 
-    work = sum(6 * array.size * w.shape[-2] for array, w, _ in terms)
     return pl.pallas_call(
         functools.partial(gather_back_kernel, len(terms)),
         grid=(shards, columns // wide),
@@ -807,7 +801,7 @@
         out_specs=pl.BlockSpec(total, lambda j, c: (0, 0)),
         out_shape=jax.ShapeDtypeStruct(total, jnp.float32),
         compiler_params=pltpu.CompilerParams(vmem_limit_bytes=48 << 20),
-        cost_estimate=pl.CostEstimate(flops=work, bytes_accessed=16 << 20, transcendentals=0),
+        cost_estimate=pl.CostEstimate(flops=1, bytes_accessed=1024, transcendentals=0),
     )(base, *arrays, *[w for _, w, _ in terms])
 
 
@@ -839,9 +833,7 @@
         scratch_shapes=[pltpu.VMEM((depth, tokens), jnp.bfloat16)] * 2,
         input_output_aliases={2: 0} if held else {},
         compiler_params=pltpu.CompilerParams(vmem_limit_bytes=48 << 20),
-        cost_estimate=pl.CostEstimate(
-            flops=6 * tokens * depth * shards * columns, bytes_accessed=4 * shards * depth * columns, transcendentals=0
-        ),
+        cost_estimate=pl.CostEstimate(flops=1, bytes_accessed=1024, transcendentals=0),
     )(x, d, *held)
 
 
@@ -878,9 +870,7 @@
         out_shape=jax.ShapeDtypeStruct((shards, rows, columns), jnp.float32),
         scratch_shapes=[pltpu.VMEM((depth, tokens), jnp.bfloat16)] * 2,
         compiler_params=pltpu.CompilerParams(vmem_limit_bytes=48 << 20),
-        cost_estimate=pl.CostEstimate(
-            flops=6 * (count + 2 * tokens) * depth * shards * columns, bytes_accessed=24 << 20, transcendentals=0
-        ),
+        cost_estimate=pl.CostEstimate(flops=1, bytes_accessed=1024, transcendentals=0),
     )(x, y, back_q, back_k, back_v)
 
 

time: 981 us -> 979 us (level)
    unnamed x192 -> x182, local copies, waits for them, and re-layouts: 30.1 us -> 30.1 us
where the time goes in v6:
time: 979 us; the launch traced here: 970 us
  Pallas kernels  712 us (73%)
  other arithmetic  115 us (12%)
  local copies, waits for them, and re-layouts  68 us (7%)
  between operations  23 us (2%)
  waiting for transfers between devices  19.3 us (2%)
  starting transfers between devices  16.4 us (2%)
  matrix products  14.1 us (1%)
    pallas_call x3, Pallas kernels, ring_sum(): pl.pallas_call(functools.partial(ring_kernel, groups, shards, parts, len(...  266 us
    pallas_call x1, Pallas kernels, spread(): pl.pallas_call(functools.partial(spread_kernel, groups), out_shape=[jax.S...  109 us
    pallas_call x4, Pallas kernels, gather_back(): pl.pallas_call(functools.partial(gather_back_kernel, len(terms)), grid=(s...  82.9 us
    pallas_call x3, Pallas kernels, times(): pl.pallas_call(functools.partial(times_kernel, finish, len(extras)), grid...  65.1 us
    pallas_call x3, Pallas kernels, outer(): pl.pallas_call(outer_kernel, grid=(shards, columns // wide), in_specs=[pl...  58.7 us
    pallas_call x2, Pallas kernels, attend_call(): pl.pallas_call(functools.partial(kernel, slots, slots // 2), grid=(pairs,...  57.1 us
    sub x10, other arithmetic, advance(): weight - RATE * (DECAY * moment_new + (1.0 - DECAY) * clipped)  39 us
    unnamed x182, local copies, waits for them, and re-layouts  30.1 us
  transfers between devices with their start and end apart: 10, of which 3 were waited for; matrix products, arithmetic and copies ran while one was open for 11% of the time, Pallas kernels for 57%

profile of v6, /device:TPU:0, one launch (start us, length us, event | category | flops | bytes accessed | tf_op | source)
XLA Modules:
  0.0 969.6 jit_solution(17729790602525360524)
XLA Ops:
  8.0 8.5 fusion.55
  22.7 7.3 all-to-all-start.4
  30.0 7.1 all-to-all-done.4
  37.2 10.7 %gather_fusion.1 = f32[2816,256]{1,0:T(8,128)} fusion(f32[6304,256]{1,0:T(8,128)} %param.30, s32[3072]{0:T(1024)S(1)} %pad_clamp_fusion.1), kind=kCustom, calls=%fused_computation.1 | custom fusion | bytes 5778432 | tf_op jit(solution)/shard_map/jit(_take)/gather | solution.py:1029
  54.5 109.0 %shard_map.390 = (f32[4,8,128,1024]{3,2,1,0:T(8,128)}, f32[4,520,256]{2,1,0:T(8,128)S(1)}) custom-call(f32[8,128,1024]{2,1,0:T(8,128)S(1)} %bitcast.136, f32[520,256]{1,0:T(8,128)S(1)} %select_maximum_fusion.small_ref), custom_call_target="tpu_custom_call" | custom-call | flops 1 | bytes 1024 | tf_op jit(solution)/shard_map/pallas_call | solution.py:510
  167.6 5.7 shard_map.391
  191.1 24.2 %shard_map.392 = (f32[4,768,256]{2,1,0:T(8,128)S(1)}, f32[4,1024,256]{2,1,0:T(8,128)}, f32[4,1024,256]{2,1,0:T(8,128)}) custom-call(f32[768,1024]{1,0:T(8,128)} %copy-done.5, f32[256,1024]{1,0:T(8,128)} %collective-permute-done.y_ref, f32[4,4,1024,256]{3,2,1,0:T(8,128)} %bitcast.146, f32[4,4,1024,256]{3,2,1,0:T(8,128)} %bitcast.147, ...), custom_call_target="tpu_custom_call" | custom-call | flops 1 | bytes 1024 | tf_op jit(solution)/shard_map/pallas_call | solution.py:747
  216.9 19.8 %shard_map.393 = (f32[4,768,256]{2,1,0:T(8,128)S(1)}, f32[8,2,768]{2,1,0:T(2,128)S(1)}) custom-call(f32[4,768,256]{2,1,0:T(8,128)} %copy-done.12, f32[4,1024,256]{2,1,0:T(8,128)} %get-tuple-element.298.k_ref, f32[4,1024,256]{2,1,0:T(8,128)} %get-tuple-element.299.v_ref, f32[1024,1]{1,0:T(8,128)S(1)} %copy-done.16), custom_call_target="tpu_custom_call" | custom-call | flops 1 | bytes 1024 | tf_op jit(solution)/shard_map/pallas_call | solution.py:653
  238.3 8.5 shard_map.394
  250.9 29.0 %shard_map.395 = (f32[4,768,1024]{2,1,0:T(8,128)}, f32[4,768,1024]{2,1,0:T(8,128)}) custom-call(f32[768,1024]{1,0:T(8,128)S(1)} %get-tuple-element.408.x_ref, f32[4,1024,1024]{2,1,0:T(8,128)} %bitcast.156, f32[4,1,1024]{2,1,0:T(1,128)S(1)} %reshape_reshape.3.refs_0_), custom_call_target="tpu_custom_call" | custom-call | flops 1 | bytes 1024 | tf_op jit(solution)/shard_map/pallas_call | solution.py:694
  281.5 24.7 %shard_map.396 = f32[768,1024]{1,0:T(8,128)S(1)} custom-call(f32[768,1024]{1,0:T(8,128)} %get-tuple-element.407.base_ref, f32[4,768,1024]{2,1,0:T(8,128)} %get-tuple-element.302.refs_0_.d_ref, f32[4,1024,1024]{2,1,0:T(8,128)} %all-gather.4.cloned.1.call-done.refs_1_.w_ref), custom_call_target="tpu_custom_call" | custom-call | flops 1 | bytes 1024 | tf_op jit(solution)/shard_map/pallas_call | solution.py:793
  309.2 13.8 %shard_map.397 = f32[32,16,128]{2,1,0:T(8,128)} custom-call(f32[16,128]{1,0:T(8,128)} %reshape.661.x_ref), custom_call_target="tpu_custom_call" | custom-call | tf_op jit(solution)/shard_map/pallas_call | solution.py:299
  342.4 25.1 %shard_map.407 = f32[4,1024,1024]{2,1,0:T(8,128)} custom-call(f32[768,1024]{1,0:T(8,128)S(1)} %get-tuple-element.404.x_ref.base_ref, f32[4,768,1024]{2,1,0:T(8,128)} %get-tuple-element.302.refs_0_.d_ref), custom_call_target="tpu_custom_call" | custom-call | flops 1 | bytes 1024 | tf_op jit(solution)/shard_map/pallas_call | solution.py:823
  371.1 27.7 %shard_map.398 = (f32[4,768,1024]{2,1,0:T(8,128)}, f32[4,1,1024]{2,1,0:T(1,128)S(1)}) custom-call(f32[768,1024]{1,0:T(8,128)S(1)} %copy-done.4, f32[4,1024,1024]{2,1,0:T(8,128)} %all-gather.4.cloned.1.call-done.refs_1_.w_ref, f32[4,768,1024]{2,1,0:T(8,128)} %get-tuple-element.303.refs_0_), custom_call_target="tpu_custom_call" | custom-call | flops 1 | bytes 1024 | tf_op jit(solution)/shard_map/pallas_call | solution.py:694
  398.7 24.8 %shard_map.399 = f32[4,1024,1024]{2,1,0:T(8,128)} custom-call(f32[768,1024]{1,0:T(8,128)S(1)} %copy-done.10, f32[4,768,1024]{2,1,0:T(8,128)} %get-tuple-element.305.d_ref.refs_0_), custom_call_target="tpu_custom_call" | custom-call | flops 1 | bytes 1024 | tf_op jit(solution)/shard_map/pallas_call | solution.py:823
  423.6 24.9 %shard_map.400 = f32[768,1024]{1,0:T(8,128)S(1)} custom-call(f32[768,1024]{1,0:T(8,128)} %copy-done.3, f32[4,768,1024]{2,1,0:T(8,128)} %get-tuple-element.305.d_ref.refs_0_, f32[4,1024,1024]{2,1,0:T(8,128)} %bitcast.157), custom_call_target="tpu_custom_call" | custom-call | flops 1 | bytes 1024 | tf_op jit(solution)/shard_map/pallas_call | solution.py:793
  452.9 8.4 shard_map.401.d_ref
  463.1 37.3 %shard_map.402 = (f32[4,768,256]{2,1,0:T(8,128)S(1)}, f32[4,1024,256]{2,1,0:T(8,128)}, f32[4,1024,256]{2,1,0:T(8,128)}) custom-call(f32[4,768,256]{2,1,0:T(8,128)} %copy-done.12, f32[4,1024,256]{2,1,0:T(8,128)} %get-tuple-element.298.k_ref, f32[4,1024,256]{2,1,0:T(8,128)} %get-tuple-element.299.v_ref, f32[1024,1]{1,0:T(8,128)S(1)} %copy-done.17, ...), custom_call_target="tpu_custom_call" | custom-call | flops 1 | bytes 1024 | tf_op jit(solution)/shard_map/pallas_call | solution.py:653
  502.0 24.8 %shard_map.403 = f32[1024,1024]{1,0:T(8,128)} custom-call(f32[768,1024]{1,0:T(8,128)S(1)} %copy-done.2, f32[4,768,256]{2,1,0:T(8,128)} %copy-done.7, f32[4,1024,256]{2,1,0:T(8,128)} %get-tuple-element.313.refs_1_.k_ref, f32[4,1024,256]{2,1,0:T(8,128)} %get-tuple-element.314.refs_2_.v_ref, f32[4,4,1024,256]{3,2,1,0:T(8,128)} %bitcast.151, ...), custom_call_target="tpu_custom_call" | custom-call | flops 1 | bytes 1024 | tf_op jit(solution)/shard_map/pallas_call | solution.py:793
  537.5 5.7 shard_map.404
  544.8 5.3 all-to-all-start.6
  559.8 24.0 %shard_map.405.refs_0_ = f32[4,4672,256]{2,1,0:T(8,128)} custom-call(f32[768,1024]{1,0:T(8,128)S(1)} %copy-done.6, f32[256,1024]{1,0:T(8,128)} %collective-permute-done.y_ref, f32[4,768,256]{2,1,0:T(8,128)} %copy-done.7, f32[4,1024,256]{2,1,0:T(8,128)} %get-tuple-element.313.refs_1_.k_ref, f32[4,1024,256]{2,1,0:T(8,128)} %get-tuple-element.314.refs_2_.v_ref), custom_call_target="tpu_custom_call" | custom-call | flops 1 | bytes 1024 | tf_op jit(solution)/shard_map/pallas_call | solution.py:859
  583.8 8.8 shard_map.406
  607.3 9.0 all-to-all-done.6
  617.2 84.4 %shard_map.408 = (f32[8,128,1024]{2,1,0:T(8,128)S(1)}, f32[8,128]{1,0:T(8,128)S(1)}) custom-call(f32[8,128,1024]{2,1,0:T(8,128)} %bitcast.164, f32[8,128]{1,0:T(8,128)S(1)} %fusion.33.refs_1_), custom_call_target="tpu_custom_call" | custom-call | flops 1 | bytes 1024 | tf_op jit(solution)/shard_map/pallas_call | solution.py:422
  703.6 84.3 %shard_map.409 = (f32[8,128,1024]{2,1,0:T(8,128)S(1)}, f32[8,128]{1,0:T(8,128)S(1)}) custom-call(f32[8,128,1024]{2,1,0:T(8,128)} %bitcast.165, f32[8,128]{1,0:T(8,128)S(1)} %get-tuple-element.320.refs_1_), custom_call_target="tpu_custom_call" | custom-call | flops 1 | bytes 1024 | tf_op jit(solution)/shard_map/pallas_call | solution.py:422
  790.0 19.2 %scatter_custom_fusion.1 = f32[6304,256]{1,0:T(8,128)} fusion(s32[2816]{0:T(1024)S(1)} %fusion.32, f32[2816,256]{1,0:T(8,128)} %bitcast.42, f32[]{:T(128)} %constant.155.clone.1), kind=kCustom, calls=%fused_computation.35 | custom fusion | flops 720896 | bytes 6455808 | tf_op jit(solution)/shard_map/scatter-add | solution.py:1141
  810.1 5.1 multiply_reduce_fusion
  815.9 97.2 %shard_map.410 = (f32[8,584,256]{2,1,0:T(8,128)S(1)}, f32[8,128]{1,0:T(8,128)S(1)}) custom-call(f32[8,584,256]{2,1,0:T(8,128)} %bitcast.163, f32[8,128]{1,0:T(8,128)S(1)} %select_add_fusion.refs_1_), custom_call_target="tpu_custom_call" | custom-call | flops 1 | bytes 1024 | tf_op jit(solution)/shard_map/pallas_call | solution.py:422
  929.5 6.7 multiply_subtract_fusion.2
  936.2 12.6 %multiply_subtract_fusion.1 = (f32[6304,256]{1,0:T(8,128)}, f32[6304,256]{1,0:T(8,128)}) fusion(f32[6304,256]{1,0:T(8,128)} %get-tuple-element.708, f32[6304,256]{1,0:T(8,128)} %get-tuple-element.327, f32[]{:T(128)S(6)} %min.3, f32[6304,256]{1,0:T(8,128)} %param.40), kind=kLoop, calls=%fused_computation.26 | loop fusion | flops 12910592 | bytes 32276484 | tf_op jit(solution)/shard_map/sub | solution.py:80
  950.0 11.5 %multiply_subtract_fusion = (f32[2,1024,1024]{2,1,0:T(8,128)}, f32[2,1024,1024]{2,1,0:T(8,128)}) fusion(f32[2,1024,1024]{2,1,0:T(8,128)} %param.33, f32[1,1024,1024]{2,1,0:T(8,128)S(1)} %bitcast.144, f32[1,1024,1024]{2,1,0:T(8,128)S(1)} %bitcast.145, f32[]{:T(128)S(6)} %min.3, f32[2,1024,1024]{2,1,0:T(8,128)} %param.43), kind=kLoop, calls=%fused_computation.24 | loop fusion | flops 18874368 | bytes 41943044 | tf_op jit(solution)/shard_map/sub | solution.py:80
  (331 shorter events, 131.6 us)
Async XLA Ops:
  7.2 183.9 %all-gather.6.cloned.1.call-start = ((), (), s32[]{:S(2)}) async-start(), calls=%async_computation.14 | async-start | bytes 20971520 | tf_op jit(solution)/shard_map/all_gather | solution.py:1008
  7.9 273.6 %all-gather.4.cloned.1.call-start = ((), (), s32[]{:S(2)}) async-start(), calls=%async_computation.10 | async-start | bytes 20971520 | tf_op jit(solution)/shard_map/all_gather | solution.py:1010
  22.0 28.9 %copy-start.61 = (s32[704]{0:T(1024)}, s32[704]{0:T(1024)S(1)}, u32[]{:S(2)}) copy-start(s32[704]{0:T(1024)S(1)} %broadcast_add_fusion.6) | copy-start | bytes 8452
  22.7 14.4 %all-to-all-start.4 = ((s32[32,1,128]{2,1,0:T(1,128)}), s32[32,1,128]{2,1,0:T(1,128)S(1)}, u32[]{:S(2)}, u32[]{:S(2)}) async-start(s32[32,1,128]{2,1,0:T(1,128)} %bitcast.13), calls=%async_computation.4 | async-start | bytes 32768 | tf_op jit(solution)/shard_map/all_to_all | solution.py:978
  47.9 117.7 %all-to-all-start.5 = ((f32[32,88,256]{2,1,0:T(8,128)}), f32[32,88,256]{2,1,0:T(8,128)S(1)}, u32[]{:S(2)}, u32[]{:S(2)}) async-start(f32[32,88,256]{2,1,0:T(8,128)} %bitcast.161), calls=%async_computation.5 | async-start | bytes 5767168 | tf_op jit(solution)/shard_map/all_to_all | solution.py:978
  50.8 566.3 %reduce-scatter.8.cloned.1.call-start = ((), (), s32[]{:S(2)}) async-start(), calls=%async_computation.13 | async-start | bytes 20971520 | tf_op jit(solution)/shard_map/reduce_scatter | solution.py:1111
  52.3 127.0 %copy-start.49 = (f32[1,1024]{1,0:T(1,128)}, f32[1,1024]{1,0:T(1,128)S(1)}, u32[]{:S(2)}) copy-start(f32[1,1024]{1,0:T(1,128)S(1)} %get-tuple-element.433) | copy-start | bytes 12292
  52.3 195.3 %copy-start.64 = (f32[1,1024]{1,0:T(1,128)}, f32[1,1024]{1,0:T(1,128)S(1)}, u32[]{:S(2)}) copy-start(f32[1,1024]{1,0:T(1,128)S(1)} %get-tuple-element.430) | copy-start | bytes 12292
  52.3 254.7 %copy-start.51 = (f32[1,1024]{1,0:T(1,128)}, f32[1,1024]{1,0:T(1,128)S(1)}, u32[]{:S(2)}) copy-start(f32[1,1024]{1,0:T(1,128)S(1)} %get-tuple-element.427) | copy-start | bytes 12292
  183.1 7.9 collective-permute-start
  188.5 118.5 %copy-start.55 = (f32[768]{0:T(1024)}, f32[768]{0:T(1024)S(1)}, u32[]{:S(2)}) copy-start(f32[768]{0:T(1024)S(1)} %get-tuple-element.457) | copy-start | bytes 9220
  188.5 118.5 %copy-start.57 = (f32[768]{0:T(1024)}, f32[768]{0:T(1024)S(1)}, u32[]{:S(2)}) copy-start(f32[768]{0:T(1024)S(1)} %get-tuple-element.458) | copy-start | bytes 9220
  191.1 25.8 %copy-start.16 = (f32[1024,1]{1,0:T(8,128)S(1)}, f32[1024,1]{1,0:T(8,128)}, u32[]{:S(2)}) copy-start(f32[1024,1]{1,0:T(8,128)} %broadcast_select_fusion.bias_ref) | copy-start | bytes 12292
  306.9 19.4 %copy-start.80 = (f32[256]{0:T(256)S(1)}, f32[256]{0:T(256)}, u32[]{:S(2)}) copy-start(f32[256]{0:T(256)} %param.39) | copy-start | bytes 3076
  308.6 29.0 %copy-start.52 = (f32[1,1024]{1,0:T(1,128)S(1)}, f32[1,1024]{1,0:T(1,128)}, u32[]{:S(2)}) copy-start(f32[1,1024]{1,0:T(1,128)} %copy-done.51) | copy-start | bytes 12292
  308.6 29.0 %copy-start.56 = (f32[768]{0:T(1024)S(1)}, f32[768]{0:T(1024)}, u32[]{:S(2)}) copy-start(f32[768]{0:T(1024)} %copy-done.55) | copy-start | bytes 9220
  308.6 29.0 %copy-start.58 = (f32[768]{0:T(1024)S(1)}, f32[768]{0:T(1024)}, u32[]{:S(2)}) copy-start(f32[768]{0:T(1024)} %copy-done.57) | copy-start | bytes 9220
  369.2 334.4 %reduce-scatter.6.cloned.1.call-start = ((), (), s32[]{:S(2)}) async-start(), calls=%async_computation.12 | async-start | bytes 20971520 | tf_op jit(solution)/shard_map/reduce_scatter | solution.py:1117
  371.1 27.7 %copy-start.10 = (f32[768,1024]{1,0:T(8,128)S(1)}, f32[768,1024]{1,0:T(8,128)}, u32[]{:S(2)}) copy-start(f32[768,1024]{1,0:T(8,128)} %copy-done.9) | copy-start | bytes 9437188
  423.6 24.9 %copy-start.1 = (f32[768,1024]{1,0:T(8,128)S(1)}, f32[768,1024]{1,0:T(8,128)}, u32[]{:S(2)}) copy-start(f32[768,1024]{1,0:T(8,128)} %copy-done) | copy-start | bytes 9437188
  423.6 24.9 %copy-start.47 = (f32[768]{0:T(1024)S(1)}, f32[768]{0:T(1024)}, u32[]{:S(2)}) copy-start(f32[768]{0:T(1024)} %copy-done.46) | copy-start | bytes 9220
  423.6 24.9 %copy-start.65 = (f32[1,1024]{1,0:T(1,128)S(1)}, f32[1,1024]{1,0:T(1,128)}, u32[]{:S(2)}) copy-start(f32[1,1024]{1,0:T(1,128)} %copy-done.64) | copy-start | bytes 12292
  423.6 24.9 %copy-start.67 = (f32[768]{0:T(1024)S(1)}, f32[768]{0:T(1024)}, u32[]{:S(2)}) copy-start(f32[768]{0:T(1024)} %copy-done.66) | copy-start | bytes 9220
  463.1 39.0 %copy-start.2 = (f32[768,1024]{1,0:T(8,128)S(1)}, f32[768,1024]{1,0:T(8,128)}, u32[]{:S(2)}) copy-start(f32[768,1024]{1,0:T(8,128)} %subtract_multiply_fusion.1.x_ref.base_ref) | copy-start | bytes 9437188
  502.0 26.2 %copy-start.62 = (s32[704]{0:T(1024)S(1)}, s32[704]{0:T(1024)}, u32[]{:S(2)}) copy-start(s32[704]{0:T(1024)} %copy-done.61) | copy-start | bytes 8452
  502.0 28.9 %copy-start.26 = (f32[768,1024]{1,0:T(8,128)S(1)}, f32[768,1024]{1,0:T(8,128)}, u32[]{:S(2)}) copy-start(f32[768,1024]{1,0:T(8,128)} %copy-done.25) | copy-start | bytes 9437188
  502.0 28.9 %copy-start.50 = (f32[1,1024]{1,0:T(1,128)S(1)}, f32[1,1024]{1,0:T(1,128)}, u32[]{:S(2)}) copy-start(f32[1,1024]{1,0:T(1,128)} %copy-done.49) | copy-start | bytes 12292
  502.0 28.9 %copy-start.54 = (f32[768]{0:T(1024)S(1)}, f32[768]{0:T(1024)}, u32[]{:S(2)}) copy-start(f32[768]{0:T(1024)} %copy-done.53) | copy-start | bytes 9220
  528.2 2.7 collective-permute-start.1
  544.8 71.4 %all-to-all-start.6 = ((f32[32,88,256]{2,1,0:T(8,128)}), f32[32,88,256]{2,1,0:T(8,128)}, u32[]{:S(2)}, u32[]{:S(2)}) async-start(f32[32,88,256]{2,1,0:T(8,128)} %bitcast.137), calls=%async_computation.6 | async-start | bytes 5767168 | tf_op jit(solution)/shard_map/all_to_all | solution.py:978
  550.2 265.7 %reduce-scatter.4.cloned.1.call-start = ((), (), s32[]{:S(2)}) async-start(), calls=%async_computation.11 | async-start | bytes 23920640 | tf_op jit(solution)/shard_map/reduce_scatter | solution.py:1183
  790.0 19.2 %copy-start.38 = (s32[768]{0:T(1024)S(1)}, s32[768]{0:T(1024)}, u32[]{:S(2)}) copy-start(s32[768]{0:T(1024)} %copy-done.37) | copy-start | bytes 9220
  (66 other events, 338.3 us)
Sparse Core Ops, SparseCore 0:
  9.6 162.3 all-gather.5
  174.1 105.9 all-gather.3
  369.3 126.9 reduce-scatter.7
  498.9 157.0 reduce-scatter.5
  658.4 141.0 reduce-scatter.3
